TPU v7x, 256 devices: a whole 4x4x8 slice. The times are simulated.
256 devices in a mesh: item: 16 (over y, x_lo, core), feat: 16 (over x_hi, z).
Axes of the slice: x: 4 (x_hi: 2, x_lo: 2; x = x_hi * 2 + x_lo), y: 4, z: 8, core: 2. Of those that a mesh axis runs over, the one named last changes fastest.
Arguments:
- teacher: bfloat16 [32768, 4096], P('item', 'feat'), may hold values from -16 to 16
- codebooks: bfloat16 [4, 256, 512], replicated, may hold values from -3 to 3
- codes: int32 [32768, 4], P(('item', 'feat')), may hold values from 0 to 255, as said below
Outputs:
- loss: float32 [], replicated
- codebook_grad: float32 [4, 256, 512], replicated
Inputs may be any that keep to these rules, and one draw needn't show every extreme that they name: codes index the rows of their level's codebook. Let q be an item's index divided by 128, w = 1 and h = 128. An item's level-0 code is q * w + r modulo 256, and its level-1 code is (q modulo h) * 2 * w + r' modulo 256, with r and r' from 0 to 2 * w - 1; the other levels' codes are unrestricted.
All inputs are finite; a program needn't handle non-finite values.
Results may differ from a plain program's by a relative error of at most 0.0065.
Values may be sent and summed in bfloat16 or wider, within the bound.
No kernel may reach another device: no remote copies, remote signals or barrier semaphores. Data moves between devices by JAX's collectives and lax.ppermute only.
A program may use at most 64 MiB of HBM per device.

v0:
```python
import jax
import jax.numpy as jnp
from jax import lax
from jax.sharding import Mesh
from jax.sharding import PartitionSpec as P

DT = 4096
ITEM = ("item_0", "item_1", "item_2")
ITEM_FEAT = ("item_0", "item_1", "item_2", "feat")


epsilon = 1e-06


def from_everyone(array, axis):
    peers = lax.axis_size(axis)
    return lax.all_to_all(
        jnp.broadcast_to(array[None], (peers, *array.shape)), axis, 0, 0, tiled=True
    )


def taken_together(array, axis):
    everything = from_everyone(array, axis)
    return jnp.sum(everything, axis=0)


def joined_along(pieces, dim):
    pieces = jnp.moveaxis(pieces, 0, dim)
    dims = pieces.shape
    return pieces.reshape(*dims[:dim], dims[dim] * dims[dim + 1], *dims[dim + 2 :])


def gathered_copies(array, axis, dim):
    pieces = from_everyone(array, axis)
    return joined_along(pieces, dim)


def in_blocks(array, dim, peers):
    before, after = (array.shape[:dim], array.shape[dim + 1 :])
    return jnp.moveaxis(array.reshape(*before, peers, -1, *after), dim, 0)


def sum_at_owner(array, axis, dim):
    pieces = in_blocks(array, dim, lax.axis_size(axis))
    arrived = lax.all_to_all(pieces, axis, split_axis=0, concat_axis=0, tiled=True)
    return arrived.sum(axis=0)


def sum_in_two_steps(array, axes, dim):
    far, near = axes
    pieces = in_blocks(array, dim, lax.axis_size(far))
    nearer = sum_at_owner(pieces, near, dim + 1)
    arrived = lax.all_to_all(nearer, far, split_axis=0, concat_axis=0, tiled=True)
    return arrived.sum(axis=0)


def filled_up(lines, peers):
    spare = -lines.shape[0] % peers
    if not spare:
        return lines
    return jnp.concatenate([lines, jnp.zeros((spare, *lines.shape[1:]), lines.dtype)])


def gather_axes(array, axes, dim):
    far, near = axes
    first = from_everyone(array, far)
    pieces = jnp.swapaxes(from_everyone(first, near), 0, 1)
    return joined_along(pieces.reshape(-1, *array.shape), dim)


def total_of(array, axes):
    own = sum_in_two_steps(
        filled_up(array, lax.axis_size(axes[0]) * lax.axis_size(axes[1])), axes, 0
    )
    whole = gather_axes(own, axes, 0)
    return whole[: len(array)].reshape(array.shape)


def in_one(arrays, axis):
    ends = [0]
    for a in arrays:
        ends.append(ends[-1] + a.size)
    subtotal = total_of(jnp.concatenate([a.ravel() for a in arrays]), axis)
    return tuple((subtotal[b:e].reshape(a.shape) for a, b, e in zip(arrays, ends, ends[1:])))


def rebuild(codes, codebooks):
    recon = jnp.zeros((codes.shape[0], codebooks.shape[2]), jnp.float32)
    for level in range(codebooks.shape[0]):
        recon = recon + jnp.take(codebooks[level], codes[:, level], axis=0).astype(jnp.float32)
    inv = lax.rsqrt(jnp.mean(recon * recon, axis=-1, keepdims=True) + epsilon)
    return (recon * inv, inv)


def contract_rows(left, right):
    return lax.dot_general(
        left, right, (((0,), (0,)), ((), ())), preferred_element_type=jnp.float32
    )


def row_map(values, s_full, inv):
    return inv * (values - s_full * jnp.mean(values * s_full, axis=-1, keepdims=True))


def code_sums_exact(code_table, values, code_ids):
    terms = []
    for level in range(code_table.shape[1]):
        onehot = (code_table[:, level][:, None] == code_ids[None, :]).astype(jnp.float32)
        terms.append(jnp.einsum("nk,nd->kd", onehot, values, precision=lax.Precision.HIGHEST))
    return jnp.stack(terms)


def code_sums_split(code_table, values, code_ids):
    upper = values.astype(jnp.bfloat16)
    lower = (values - upper.astype(jnp.float32)).astype(jnp.bfloat16)
    terms = []
    for level in range(code_table.shape[1]):
        onehot = (code_table[:, level][:, None] == code_ids[None, :]).astype(jnp.bfloat16)
        first = jnp.einsum("nk,nd->kd", onehot, upper, preferred_element_type=jnp.float32)
        second = jnp.einsum("nk,nd->kd", onehot, lower, preferred_element_type=jnp.float32)
        terms.append(first + second)
    return jnp.stack(terms)


def on_device(teacher, codebooks, codes):
    feat_count = lax.axis_size("feat")
    item_count = lax.axis_size(ITEM)
    own_rows = codes.shape[0]
    width = codebooks.shape[2]
    code_count = codebooks.shape[1]
    total_items = float(own_rows * feat_count * item_count)
    tfull = teacher.astype(jnp.float32)
    squares = taken_together(jnp.sum(tfull * tfull, axis=-1), "feat")
    tnorm = (tfull * lax.rsqrt(squares[:, None] / DT + epsilon)).astype(jnp.bfloat16)
    position = lax.axis_index("feat") * own_rows
    all_codes = gathered_copies(codes, "feat", 0)
    group_full, group_inv = rebuild(all_codes, codebooks)
    group_student = group_full.astype(jnp.bfloat16)
    s_full = lax.dynamic_slice_in_dim(group_full, position, own_rows, 0)
    inv = lax.dynamic_slice_in_dim(group_inv, position, own_rows, 0)
    student = s_full.astype(jnp.bfloat16)
    cross_part = contract_rows(tnorm, group_student)
    gram_part = contract_rows(group_student, group_student)
    cross, gram = in_one((cross_part, gram_part), (("item_0", "item_1"), "item_2"))
    cross_total = taken_together(jnp.sum(cross * cross), "feat")
    scale = total_items * total_items * float(width)
    loss = (jnp.sum(gram * gram) - 2.0 * cross_total) / scale
    cross_b = cross.astype(jnp.bfloat16)
    gram_b = gram.astype(jnp.bfloat16)
    code_ids = jnp.arange(code_count, dtype=jnp.int32)
    push = jnp.dot(student, gram_b, preferred_element_type=jnp.float32)
    block_pull = jnp.dot(tnorm, cross_b, preferred_element_type=jnp.float32)
    block_pull = lax.optimization_barrier(block_pull.astype(jnp.bfloat16)).astype(jnp.float32)
    pull_term = row_map(block_pull, group_full, group_inv) / total_items
    push_term = row_map(push, s_full, inv) / total_items
    local = code_sums_exact(codes, push_term, code_ids) - code_sums_split(
        all_codes, pull_term, code_ids
    )
    grads = lax.psum(local, ITEM_FEAT)
    return (loss, grads)


def solution(mesh):
    split = Mesh(
        mesh.devices.reshape(4, 2, 2, mesh.shape["feat"]), ("item_0", "item_1", "item_2", "feat")
    )
    return jax.shard_map(
        on_device,
        mesh=split,
        in_specs=(P(ITEM, "feat"), P(), P(ITEM_FEAT, None)),
        out_specs=(P(), P()),
        check_vma=False,
    )
```

profile of v0, /device:TPU:1, one launch (start us, length us, event | category | flops | bytes accessed | tf_op | source)
XLA Modules:
  0.0 435.3 jit_solution(3975521551385590303)
XLA Ops:
  8.6 11.6 %all-to-all-start.1 = ((s32[16,128,4]{1,2,0:T(4,128)}), s32[16,128,4]{1,2,0:T(4,128)S(1)}, u32[]{:S(2)}, u32[]{:S(2)}) async-start(s32[16,128,4]{1,2,0:T(4,128)} %broadcast_in_dim.22), calls=%async_computation.1 | async-start | bytes 65536 | tf_op jit(solution)/shard_map/all_to_all | solution.py:17
  21.8 7.2 %all-to-all-done.1 = s32[16,128,4]{1,2,0:T(4,128)S(1)} async-done(((s32[16,128,4]{1,2,0:T(4,128)}), s32[16,128,4]{1,2,0:T(4,128)S(1)}, u32[]{:S(2)}, u32[]{:S(2)}) %all-to-all-start.1) | async-done | bytes 32800 | tf_op jit(solution)/shard_map/all_to_all | solution.py:17
  29.7 3.5 all-to-all-start
  35.1 9.2 %gather_fusion.3 = bf16[2048,512]{1,0:T(8,128)(2,1)} fusion(bf16[256,512]{1,0:T(8,128)(2,1)S(1)} %get-tuple-element.9, s32[2048]{0:T(1024)S(1)} %fusion.42), kind=kCustom, calls=%fused_computation.3.clone | custom fusion | bytes 4202496 | tf_op jit(solution)/shard_map/jit(_take)/gather | solution.py:90
  44.3 9.2 %gather_fusion.2 = bf16[2048,512]{1,0:T(8,128)(2,1)} fusion(bf16[256,512]{1,0:T(8,128)(2,1)S(1)} %get-tuple-element.10, s32[2048]{0:T(1024)S(1)} %fusion.41), kind=kCustom, calls=%fused_computation.2.clone | custom fusion | bytes 4202496 | tf_op jit(solution)/shard_map/jit(_take)/gather | solution.py:90
  53.5 9.2 %gather_fusion.1 = bf16[2048,512]{1,0:T(8,128)(2,1)} fusion(bf16[256,512]{1,0:T(8,128)(2,1)S(1)} %get-tuple-element.8, s32[2048]{0:T(1024)S(1)} %fusion.40), kind=kCustom, calls=%fused_computation.1.clone | custom fusion | bytes 4202496 | tf_op jit(solution)/shard_map/jit(_take)/gather | solution.py:90
  62.7 9.2 %gather_fusion = bf16[2048,512]{1,0:T(8,128)(2,1)} fusion(bf16[256,512]{1,0:T(8,128)(2,1)S(1)} %get-tuple-element.7, s32[2048]{0:T(1024)S(1)} %copy-done.12), kind=kCustom, calls=%fused_computation.clone | custom fusion | bytes 4202496 | tf_op jit(solution)/shard_map/jit(_take)/gather | solution.py:90
  71.9 5.1 %multiply_reduce_fusion = (f32[2048]{0:T(1024)S(1)}, f32[2048,512]{1,0:T(8,128)S(1)}) fusion(bf16[2048,512]{1,0:T(8,128)(2,1)S(1)} %copy-done.4, pred[2048]{0:T(1024)(128)(4,1)} %get-tuple-element.21, bf16[2048,512]{1,0:T(8,128)(2,1)} %gather_fusion.2, pred[2048]{0:T(1024)(128)(4,1)} %get-tuple-element.22, bf16[2048,512]{1,0:T(8,128)(2,1)} %gather_fusion.1, ...), kind=kLoop, calls=%fused_computation.10 | loop fusion | flops 13629440 | bytes 12599296 | tf_op jit(solution)/shard_map/reduce_sum | solution.py:91
  77.4 1.6 copy-done
  82.3 3.7 convolution_bitcast_fusion.5
  86.3 2.1 reshape_reshape.4
  88.4 2.3 copy.12
  90.8 6.7 %all_to_all.42 = f32[2,8,24576]{2,1,0:T(8,128)S(1)} all-to-all(f32[2,8,24576]{2,1,0:T(8,128)S(1)} %copy.12), channel_id=1, replica_groups=mesh['item_0'=4,'item_1'=2,'item_2'=2,'feat'=16] {'item_2'}, dimensions={0} | all-to-all | bytes 3145728 | tf_op jit(solution)/shard_map/all_to_all | solution.py:45
  98.2 16.1 %all_to_all.43 = f32[8,1,24576]{2,1,0:T(1,128)S(1)} all-to-all(f32[8,1,24576]{2,1,0:T(1,128)S(1)} %all_to_all.30), channel_id=1, replica_groups=mesh['item_0'=4,'item_1'=2,'item_2'=2,'feat'=16] {'item_0','item_1'}, dimensions={0} | all-to-all | bytes 1572864 | tf_op jit(solution)/shard_map/all_to_all | solution.py:53
  116.2 3.5 all-to-all-start.4
  119.9 11.0 %all-to-all-done.4 = f32[8,1,24576]{2,1,0:T(1,128)S(1)} async-done(((f32[8,1,24576]{2,1,0:T(1,128)}), f32[8,1,24576]{2,1,0:T(1,128)S(1)}, u32[]{:S(2)}, u32[]{:S(2)}) %all-to-all-start.4) | async-done | bytes 786464 | tf_op jit(solution)/shard_map/all_to_all | solution.py:17
  131.5 7.3 %all_to_all.44 = f32[2,8,24576]{2,1,0:T(8,128)S(1)} all-to-all(f32[2,8,24576]{2,1,0:T(8,128)S(1)} %broadcast_in_dim.25), channel_id=1, replica_groups=mesh['item_0'=4,'item_1'=2,'item_2'=2,'feat'=16] {'item_2'}, dimensions={0} | all-to-all | bytes 3145728 | tf_op jit(solution)/shard_map/all_to_all | solution.py:17
  138.8 2.4 copy.13
  141.1 2.6 slice.58
  160.4 1.8 maximum_subtract_fusion
  164.2 9.9 %all-to-all-start.6 = ((f32[16,1,1]{2,1,0:T(1,128)}), f32[16,1,1]{2,1,0:T(1,128)S(1)}, u32[]{:S(2)}, u32[]{:S(2)}) async-start(f32[16,1,1]{2,1,0:T(1,128)} %broadcast_in_dim.26), calls=%async_computation.6 | async-start | bytes 16384 | tf_op jit(solution)/shard_map/all_to_all | solution.py:17
  175.0 8.0 %all-to-all-done.6 = f32[16,1,1]{2,1,0:T(1,128)S(1)} async-done(((f32[16,1,1]{2,1,0:T(1,128)}), f32[16,1,1]{2,1,0:T(1,128)S(1)}, u32[]{:S(2)}, u32[]{:S(2)}) %all-to-all-start.6) | async-done | bytes 96 | tf_op jit(solution)/shard_map/all_to_all | solution.py:17
  184.8 239.4 %all-reduce.2.cloned.1.call-done = f32[4,256,512]{2,1,0:T(8,128)} async-done(((f32[4,256,512]{2,1,0:T(8,128)}), f32[4,256,512]{2,1,0:T(8,128)}) %all-reduce.2.cloned.1.call-update) | async-done | bytes 2097168 | tf_op jit(solution)/shard_map/psum | solution.py:159
  424.2 3.1 copy.23
  (80 shorter events, 32.7 us)
Async XLA Ops:
  7.2 14.2 %copy-start.3 = (bf16[2048,256]{1,0:T(8,128)(2,1)S(1)}, bf16[2048,256]{1,0:T(8,128)(2,1)}, u32[]{:S(2)}) copy-start(bf16[2048,256]{1,0:T(8,128)(2,1)} %param.5) | copy-start | bytes 3145732
  8.6 20.4 %all-to-all-start.1 = ((s32[16,128,4]{1,2,0:T(4,128)}), s32[16,128,4]{1,2,0:T(4,128)S(1)}, u32[]{:S(2)}, u32[]{:S(2)}) async-start(s32[16,128,4]{1,2,0:T(4,128)} %broadcast_in_dim.22), calls=%async_computation.1 | async-start | bytes 65536 | tf_op jit(solution)/shard_map/all_to_all | solution.py:17
  29.7 52.5 %all-to-all-start = ((f32[16,1,2048]{2,1,0:T(1,128)}), f32[16,1,2048]{2,1,0:T(1,128)S(1)}, u32[]{:S(2)}, u32[]{:S(2)}) async-start(f32[16,1,2048]{2,1,0:T(1,128)} %broadcast_in_dim.21), calls=%async_computation | async-start | bytes 262144 | tf_op jit(solution)/shard_map/all_to_all | solution.py:17
  33.3 11.1 %copy-start.6 = (s32[2048,1]{0,1:T(1,128)}, s32[2048,1]{0,1:T(1,128)S(1)}, u32[]{:S(2)}) copy-start(s32[2048,1]{0,1:T(1,128)S(1)} %get-tuple-element.14) | copy-start | bytes 24580
  33.3 11.1 %copy-start.8 = (s32[2048,1]{0,1:T(1,128)}, s32[2048,1]{0,1:T(1,128)S(1)}, u32[]{:S(2)}) copy-start(s32[2048,1]{0,1:T(1,128)S(1)} %get-tuple-element.13) | copy-start | bytes 24580
  33.3 11.0 %copy-start.10 = (s32[2048,1]{0,1:T(1,128)}, s32[2048,1]{0,1:T(1,128)S(1)}, u32[]{:S(2)}) copy-start(s32[2048,1]{0,1:T(1,128)S(1)} %get-tuple-element.12) | copy-start | bytes 24580
  53.5 9.2 %copy-start.12 = (s32[2048]{0:T(1024)S(1)}, s32[2048]{0:T(1024)}, u32[]{:S(2)}) copy-start(s32[2048]{0:T(1024)} %fusion.39) | copy-start | bytes 24580
  62.7 9.2 %copy-start.4 = (bf16[2048,512]{1,0:T(8,128)(2,1)S(1)}, bf16[2048,512]{1,0:T(8,128)(2,1)}, u32[]{:S(2)}) copy-start(bf16[2048,512]{1,0:T(8,128)(2,1)} %gather_fusion.3) | copy-start | bytes 6291460
  77.1 2.0 copy-start
  79.0 1.9 copy-start.2
  82.3 3.9 copy-start.5
  98.2 21.5 %copy-start.13 = (s32[128,4]{0,1:T(4,128)S(1)}, s32[128,4]{0,1:T(4,128)}, u32[]{:S(2)}) copy-start(s32[128,4]{0,1:T(4,128)} %param.7) | copy-start | bytes 6148
  116.2 14.8 %all-to-all-start.4 = ((f32[8,1,24576]{2,1,0:T(1,128)}), f32[8,1,24576]{2,1,0:T(1,128)S(1)}, u32[]{:S(2)}, u32[]{:S(2)}) async-start(f32[8,1,24576]{2,1,0:T(1,128)} %broadcast_in_dim.23), calls=%async_computation.4 | async-start | bytes 1572864 | tf_op jit(solution)/shard_map/all_to_all | solution.py:17
  119.7 304.5 %all-reduce.2.cloned.1.call-start = ((), (), s32[]{:S(2)}) async-start(), calls=%async_computation.7 | async-start | bytes 4194304 | tf_op jit(solution)/shard_map/psum | solution.py:159
  143.8 2.3 copy-start.1
  147.0 1.3 copy-start.11
  148.3 1.1 copy-start.9
  149.5 1.1 copy-start.7
  164.2 18.7 %all-to-all-start.6 = ((f32[16,1,1]{2,1,0:T(1,128)}), f32[16,1,1]{2,1,0:T(1,128)S(1)}, u32[]{:S(2)}, u32[]{:S(2)}) async-start(f32[16,1,1]{2,1,0:T(1,128)} %broadcast_in_dim.26), calls=%async_computation.6 | async-start | bytes 16384 | tf_op jit(solution)/shard_map/all_to_all | solution.py:17
Sparse Core Ops, SparseCore 0:
  162.3 261.8 all-reduce.1
where the time goes:
time: 437 us; the launch traced here: 435 us
  waiting for transfers between devices  266 us (61%)
  local copies, waits for them, and re-layouts  60.2 us (14%)
  blocking collectives  30.1 us (7%)
  starting transfers between devices  28.6 us (7%)
  matrix products  18.1 us (4%)
  between operations  16.9 us (4%)
  other arithmetic  15.9 us (4%)
    psum x1, waiting for transfers between devices, on_device(): grads = lax.psum(local, ITEM_FEAT)  239 us
    gather x4, local copies, waits for them, and re-layouts, rebuild(): jnp.take(codebooks[level], codes[:, level], axis=0).astype(jnp.float32)  36.8 us
    all_to_all x4, starting transfers between devices, from_everyone(): lax.all_to_all(jnp.broadcast_to(array[None], (peers, *array.shape)), axis...  28.5 us
    all_to_all x4, waiting for transfers between devices, from_everyone(): lax.all_to_all(jnp.broadcast_to(array[None], (peers, *array.shape)), axis...  26.2 us
    all_to_all x1, blocking collectives, sum_in_two_steps(): lax.all_to_all(nearer, far, split_axis=0, concat_axis=0, tiled=True)  16.1 us
  transfers between devices with their start and end apart: 5, of which 4 were waited for; matrix products, arithmetic and copies ran while one was open for 12% of the time, Pallas kernels for 0%

commit v1 on v0

v1 whole, which is shorter than its diff:
```python
import jax
import jax.numpy as jnp
from jax import lax
from jax.experimental import pallas as pl
from jax.experimental.pallas import tpu as pltpu
from jax.sharding import Mesh
from jax.sharding import PartitionSpec as P

DT = 4096
DS = 512
EPS = 1e-06
F32 = jnp.float32
BF16 = jnp.bfloat16
FEAT = ("xh", "za", "zb")
ITEM = ("y", "xl", "c")
ROWS = 576
CHUNK = 512

NT = (((1,), (1,)), ((), ()))


def lanes_of(packed_ref, row, start, count):
    return jnp.concatenate([packed_ref[start + j, row : row + 1, :] for j in range(count)], axis=1)


def codes_of(packed_ref, level, start, count):
    return lanes_of(packed_ref, 16 + level, start, count).astype(jnp.int32)


def cross_kernel(where_ref, packed_ref, teacher_ref, book_ref, keep_ref, send_ref, student_ref, tnorm_ref, inv_ref, table, parts):
    item, feat, me = where_ref[0], where_ref[1], where_ref[2]
    low = item & 7
    picked = jnp.concatenate(
        [
            book_ref[0, item],
            book_ref[0, (item + 1) & 15],
            book_ref[1, 2 * low],
            book_ref[1, 2 * low + 1],
            book_ref[2].reshape(256, DS),
            book_ref[3].reshape(256, DS),
        ],
        axis=0,
    )
    table[...] = picked.astype(F32).T.astype(BF16)
    per = CHUNK // 128
    small = lax.broadcasted_iota(jnp.int32, (32, CHUNK), 0)
    large = lax.broadcasted_iota(jnp.int32, (256, CHUNK), 0)
    for n in range(2048 // CHUNK):
        first = (codes_of(packed_ref, 0, n * per, per) - 16 * item) & 255
        second = codes_of(packed_ref, 1, n * per, per) - 32 * low
        onehot = jnp.concatenate(
            [
                (small == first).astype(F32),
                (small == second).astype(F32),
                (large == codes_of(packed_ref, 2, n * per, per)).astype(F32),
                (large == codes_of(packed_ref, 3, n * per, per)).astype(F32),
            ],
            axis=0,
        ).astype(BF16)
        recon = jnp.dot(table[...], onehot, preferred_element_type=F32)
        inv = lax.rsqrt(jnp.sum(recon * recon, axis=0, keepdims=True) / DS + EPS)
        student_ref[:, n * CHUNK : (n + 1) * CHUNK] = (recon * inv).astype(BF16)
        inv_ref[:, n * CHUNK : (n + 1) * CHUNK] = inv
    squares = packed_ref[0, 0:16, :]
    for j in range(1, 16):
        squares = squares + packed_ref[j, 0:16, :]
    factor = lax.rsqrt(squares / DT + EPS)
    for j in range(16):
        column = jnp.broadcast_to(factor[j : j + 1, :], (128, 128)).T
        rows = teacher_ref[j * 128 : (j + 1) * 128, :].astype(F32)
        tnorm_ref[j * 128 : (j + 1) * 128, :] = (rows * jnp.concatenate([column, column], axis=1)).astype(BF16)
    student = student_ref[...]
    cross = jnp.dot(student, tnorm_ref[...], preferred_element_type=F32)
    mine = student_ref[pl.ds(pl.multiple_of(feat * 32, 32), 32), :]
    gram = lax.dot_general(mine, student, NT, preferred_element_type=F32)
    for b in range(4):
        to = b ^ me
        parts[to, 0:128, :] = cross[b * 128 : (b + 1) * 128, 0:128]
        parts[to, 128:256, :] = cross[b * 128 : (b + 1) * 128, 128:256]
        parts[to, 256:288, :] = gram[:, b * 128 : (b + 1) * 128]
    keep_ref[...] = parts[0:2]
    send_ref[...] = parts[2:4].astype(BF16)


def grad_kernel(where_ref, packed_ref, whole_ref, student_ref, tnorm_ref, inv_ref, keep_ref, send_ref, near_ref, other_ref, next_ref, loss_ref, cross, gram):
    item, feat, me = where_ref[0], where_ref[1], where_ref[2]
    place, zb, half = where_ref[3], where_ref[4], where_ref[5]
    for b in range(4):
        block = whole_ref[b ^ me]
        cross[b * 128 : (b + 1) * 128, 0:128] = block[0:128]
        cross[b * 128 : (b + 1) * 128, 128:256] = block[128:256]
        gram[:, b * 128 : (b + 1) * 128] = block[256:288]
    cross_f = cross[...].astype(F32)
    gram_f = gram[...].astype(F32)
    loss = jnp.sum(gram_f * gram_f, keepdims=True) - 2.0 * jnp.sum(cross_f * cross_f, keepdims=True)
    loss_ref[...] = jnp.broadcast_to(loss, (8, 128))
    gram_t = gram_f.T.astype(BF16)
    per = CHUNK // 128
    total = jnp.zeros((ROWS, DS), F32)
    large = lax.broadcasted_iota(jnp.int32, (512, CHUNK), 0)
    small = lax.broadcasted_iota(jnp.int32, (64, CHUNK), 0) + 512
    for n in range(2048 // CHUNK):
        span = slice(n * CHUNK, (n + 1) * CHUNK)
        mine = student_ref[pl.ds(pl.multiple_of(feat * 32, 32), 32), span]
        push = jnp.dot(gram_t, mine, preferred_element_type=F32)
        pull = lax.dot_general(cross[...], tnorm_ref[span, :], NT, preferred_element_type=F32)
        value = push - pull
        student = student_ref[:, span].astype(F32)
        mean = jnp.sum(value * student, axis=0, keepdims=True) / DS
        grad = ((value - student * mean) * (inv_ref[:, span] / 32768.0)).astype(BF16)

        def spot(code, level):
            low = code & 15
            return (((code >> 4) ^ place) << 5) + (((low >> 3) ^ zb) << 4) + 8 * level + (low & 7)

        first = (codes_of(packed_ref, 0, n * per, per) - 16 * item) & 255
        own = 512 + (((first >> 3) ^ zb) << 4) + (first & 7)
        first = jnp.where(first < 16, own, 560 + (zb << 3))
        second = codes_of(packed_ref, 1, n * per, per) - 32 * (item & 7)
        low = second & 15
        side = (low >> 3) ^ zb
        second = jnp.where(
            ((second >> 4) ^ half) == 0, 520 + (side << 4) + (low & 7), 544 + (side << 3) + (low & 7)
        )
        third = spot(codes_of(packed_ref, 2, n * per, per), 0)
        fourth = spot(codes_of(packed_ref, 3, n * per, per), 1)
        onehot = jnp.concatenate(
            [
                ((large == third) | (large == fourth)).astype(F32),
                ((small == first) | (small == second)).astype(F32),
            ],
            axis=0,
        ).astype(BF16)
        total = total + lax.dot_general(onehot, grad, NT, preferred_element_type=F32)
    keep_ref[...] = total[0:256].reshape(keep_ref.shape)
    send_ref[...] = total[256:512].reshape(send_ref.shape).astype(BF16)
    near_ref[...] = total[512:544].reshape(near_ref.shape)
    other_ref[...] = total[544:560].reshape(other_ref.shape).astype(BF16)
    next_ref[...] = total[560:576].reshape(next_ref.shape).astype(BF16)


def spread_kernel(where_ref, *refs):
    *pieces, out_ref = refs
    place, zb = where_ref[3], where_ref[4]
    for rank, piece in enumerate(pieces):
        for y in range(4):
            at = (rank * 4 + y) ^ place
            ay, axl, ac = at & 3, (at >> 2) & 1, at >> 3
            row0 = (ay * 4 + axl * 2 + ac) * 16
            row1 = ((ay & 1) * 4 + axl * 2 + ac) * 32 + (ay >> 1) * 16
            row2 = at * 16
            for z in range(2):
                shift = (z ^ zb) * 8
                out_ref[2, pl.ds(pl.multiple_of(row2 + shift, 8), 8), :] = piece[y, z, 0].astype(F32)
                out_ref[3, pl.ds(pl.multiple_of(row2 + shift, 8), 8), :] = piece[y, z, 1].astype(F32)
                out_ref[0, pl.ds(pl.multiple_of(row0 + shift, 8), 8), :] = piece[y, z, 2].astype(F32)
                out_ref[1, pl.ds(pl.multiple_of(row1 + shift, 8), 8), :] = piece[y, z, 3].astype(F32)


def call(kernel, outs, scratch=()):
    smem = pl.BlockSpec(memory_space=pltpu.SMEM)
    vmem = pl.BlockSpec(memory_space=pltpu.VMEM)

    def run(where, *args):
        return pl.pallas_call(
            kernel,
            out_shape=[jax.ShapeDtypeStruct(s, d) for s, d in outs],
            in_specs=[smem] + [vmem] * len(args),
            out_specs=[vmem] * len(outs),
            scratch_shapes=list(scratch),
            compiler_params=pltpu.CompilerParams(vmem_limit_bytes=48 << 20),
        )(where, *args)

    return run


def swap(array, axis, size, bit):
    return lax.ppermute(array, axis, [(j, j ^ bit) for j in range(size)])


def pieces_of(value):
    high = value.astype(BF16)
    rest = value - high.astype(F32)
    middle = rest.astype(BF16)
    low = (rest - middle.astype(F32)).astype(BF16)
    return jnp.stack([high, middle, low])


def on_device(teacher, codebooks, codes):
    y, xl, c = lax.axis_index("y"), lax.axis_index("xl"), lax.axis_index("c")
    zb = lax.axis_index("zb")
    item = y * 4 + xl * 2 + c
    feat = lax.axis_index(FEAT)
    where = jnp.stack([item, feat, c * 2 + xl, c * 8 + xl * 4 + y, zb, y >> 1]).astype(jnp.int32)

    tfull = teacher.astype(F32)
    squares = jnp.sum(tfull * tfull, axis=-1).reshape(16, 128)
    packed = jnp.concatenate([squares, codes.T.astype(F32)], axis=0)
    packed = lax.all_to_all(jnp.broadcast_to(packed[None], (16, 20, 128)), FEAT, 0, 0, tiled=True)

    keep, send, student, tnorm, inv = call(
        cross_kernel,
        [((2, 288, 128), F32), ((2, 288, 128), BF16), ((DS, 2048), BF16), ((2048, 256), BF16), ((1, 2048), F32)],
        [pltpu.VMEM((DS, ROWS), BF16), pltpu.VMEM((4, 288, 128), F32)],
    )(where, packed, teacher, codebooks.reshape(4, 16, 16, DS))

    part = keep + swap(send, "c", 2, 1).astype(F32)
    part = part[0] + swap(part[1].astype(BF16), "xl", 2, 1).astype(F32)
    own = part.astype(BF16)
    a, b, d = (swap(own, "y", 4, k) for k in (1, 2, 3))
    whole = ((own.astype(F32) + a.astype(F32)) + (b.astype(F32) + d.astype(F32))).astype(BF16)
    whole = jnp.stack([whole, swap(whole, "xl", 2, 1)])
    whole = jnp.concatenate([whole, swap(whole, "c", 2, 1)])

    keep, send, near, other, after, loss = call(
        grad_kernel,
        [
            ((2, 4, 2, 2, 8, DS), F32),
            ((2, 4, 2, 2, 8, DS), BF16),
            ((2, 2, 8, DS), F32),
            ((2, 8, DS), BF16),
            ((2, 8, DS), BF16),
            ((8, 128), F32),
        ],
        [pltpu.VMEM((DS, 256), BF16), pltpu.VMEM((32, DS), BF16)],
    )(where, packed, whole, student, tnorm, inv)

    after = lax.ppermute(after, ITEM, [(j, (j + 1) % 16) for j in range(16)])
    other = swap(other, "y", 4, 2)
    sums = keep + swap(send, "c", 2, 1).astype(F32)
    sums = sums[0] + swap(sums[1].astype(BF16), "xl", 2, 1).astype(F32)
    sent = sums[1:].astype(BF16)
    sums = sums[0]
    for k in (1, 2, 3):
        sums = sums + swap(sent[k - 1], "y", 4, k).astype(F32)
    near = near + jnp.stack([after, other], axis=1).astype(F32)
    rows = jnp.concatenate([sums, near], axis=1)

    scalar = jnp.zeros((1, 8, DS), BF16)
    loss = loss[0, 0]
    scalar = scalar.at[0, 0, 0:3].set(pieces_of(loss))
    sent = jnp.concatenate([rows[1].astype(BF16), scalar])
    got = swap(sent, "zb", 2, 1).astype(F32)
    loss = loss + jnp.sum(got[4, 0, 0:3])
    rows = rows[0] + got[0:4]
    scalar = jnp.zeros((1, 8, DS), BF16).at[0, 0, 0:3].set(pieces_of(loss))
    sent = jnp.concatenate([rows.astype(BF16), scalar])
    got = lax.all_to_all(jnp.broadcast_to(sent[None], (8, 5, 8, DS)), ("xh", "za"), 0, 0, tiled=True)
    got = jnp.sum(got.astype(F32), axis=0)
    loss = jnp.sum(got[4, 0, 0:3]) / (32768.0 * 32768.0 * DS)

    rows = got[0:4].astype(BF16)
    rows = jnp.stack([rows, swap(rows, "zb", 2, 1)])
    rows = jnp.stack([rows] + [swap(rows, "y", 4, k) for k in (1, 2, 3)])
    beside = swap(rows, "xl", 2, 1)
    far = swap(rows, "c", 2, 1)
    far_beside = swap(beside, "c", 2, 1)
    (grads,) = call(spread_kernel, [((4, 256, DS), F32)])(where, rows, beside, far, far_beside)
    return (loss, grads)


def solution(mesh):
    split = Mesh(mesh.devices.reshape(4, 2, 2, 2, 4, 2), ITEM + FEAT)
    return jax.shard_map(
        on_device,
        mesh=split,
        in_specs=(P(ITEM, FEAT), P(), P(ITEM + FEAT, None)),
        out_specs=(P(), P()),
        check_vma=False,
    )
```

time: 437 us -> 120 us (0.27)
  waiting for transfers between devices: 266 us -> 31.2 us
  local copies, waits for them, and re-layouts: 60.2 us -> 2.61 us
  starting transfers between devices: 28.6 us -> 50 us
  matrix products: 18.1 us -> 0 us
  blocking collectives: 30.1 us -> 15.4 us
  other arithmetic: 15.9 us -> 4.13 us
  between operations: 16.9 us -> 5.28 us
  Pallas kernels: 0 us -> 10.6 us
    psum x1 -> x0, waiting for transfers between devices: 239 us -> none  [on_device(): grads = lax.psum(local, ITEM_FEAT)]
    ppermute x0 -> x22, starting transfers between devices: none -> 38.4 us  [the longest x21 36.7 us: swap(): return lax.ppermute(array, axis, [(j, j ^ bit) for j in range(size)])]
    gather x4 -> x0, local copies, waits for them, and re-layouts: 36.8 us -> none  [rebuild(): jnp.take(codebooks[level], codes[:, level], axis=0).astype(jnp.float32)]
    ppermute x0 -> x22, waiting for transfers between devices: none -> 22.3 us  [the longest x21 22.3 us: swap(): return lax.ppermute(array, axis, [(j, j ^ bit) for j in range(size)])]
    dot_general x16 -> x0, matrix products: 18.1 us -> none  [the longest x2 4.97 us: contract_rows(): lax.dot_general(left, right, (((0,), (0,)), ((), ())), preferred_element_...]
    all_to_all x4 -> x1, waiting for transfers between devices: 26.2 us -> 8.93 us  [on_device(): lax.all_to_all(jnp.broadcast_to(packed[None], (16, 20, 128)), FEAT, 0, 0,...]
    all_to_all x4 -> x1, starting transfers between devices: 28.5 us -> 11.6 us  [on_device(): lax.all_to_all(jnp.broadcast_to(packed[None], (16, 20, 128)), FEAT, 0, 0,...]
    all_to_all x3 -> x1, blocking collectives: 30.1 us -> 15.4 us  [on_device(): lax.all_to_all(jnp.broadcast_to(sent[None], (8, 5, 8, DS)), ('xh', 'za'),...]
  transfers between devices with their start and end apart: 5 -> 23, of which waited for: 4 -> 15; matrix products, arithmetic and copies ran while one was open for 12% -> 1% of each run, Pallas kernels for 0% -> 0%
where the time goes in v1:
time: 120 us; the launch traced here: 119 us
  starting transfers between devices  50 us (42%)
  waiting for transfers between devices  31.2 us (26%)
  blocking collectives  15.4 us (13%)
  Pallas kernels  10.6 us (9%)
  between operations  5.28 us (4%)
  other arithmetic  4.13 us (3%)
  local copies, waits for them, and re-layouts  2.61 us (2%)
    ppermute x21, starting transfers between devices, swap(): return lax.ppermute(array, axis, [(j, j ^ bit) for j in range(size)])  36.7 us
    ppermute x21, waiting for transfers between devices, swap(): return lax.ppermute(array, axis, [(j, j ^ bit) for j in range(size)])  22.3 us
    all_to_all x1, blocking collectives, on_device(): lax.all_to_all(jnp.broadcast_to(sent[None], (8, 5, 8, DS)), ('xh', 'za'),...  15.4 us
    all_to_all x1, starting transfers between devices, on_device(): lax.all_to_all(jnp.broadcast_to(packed[None], (16, 20, 128)), FEAT, 0, 0,...  11.6 us
    pallas_call x3, Pallas kernels, run(): pl.pallas_call(kernel, out_shape=[jax.ShapeDtypeStruct(s, d) for s, d in...  10.6 us
    all_to_all x1, waiting for transfers between devices, on_device(): lax.all_to_all(jnp.broadcast_to(packed[None], (16, 20, 128)), FEAT, 0, 0,...  8.93 us
  transfers between devices with their start and end apart: 23, of which 15 were waited for; matrix products, arithmetic and copies ran while one was open for 1% of the time, Pallas kernels for 0%

profile of v1, /device:TPU:1, one launch (start us, length us, event | category | flops | bytes accessed | tf_op | source)
XLA Modules:
  0.0 119.2 jit_solution(8088812183287775275)
XLA Ops:
  1.4 1.6 %multiply_reduce_fusion = f32[2048]{0:T(1024)S(1)} fusion(bf16[2048,256]{1,0:T(8,128)(2,1)} %teacher_ref.1), kind=kLoop, calls=%fused_computation | loop fusion | flops 1570816 | bytes 1056768 | tf_op jit(solution)/shard_map/reduce_sum | solution.py:197
  3.7 11.6 %all-to-all-start = ((f32[16,20,128]{2,1,0:T(8,128)}), f32[16,20,128]{2,1,0:T(8,128)S(1)}, u32[]{:S(2)}, u32[]{:S(2)}) async-start(f32[16,20,128]{2,1,0:T(8,128)} %broadcast_in_dim.4), calls=%async_computation | async-start | bytes 393216 | tf_op jit(solution)/shard_map/all_to_all | solution.py:199
  15.4 8.9 %all-to-all-done.packed_ref = f32[16,20,128]{2,1,0:T(8,128)S(1)} async-done(((f32[16,20,128]{2,1,0:T(8,128)}), f32[16,20,128]{2,1,0:T(8,128)S(1)}, u32[]{:S(2)}, u32[]{:S(2)}) %all-to-all-start) | async-done | bytes 163872 | tf_op jit(solution)/shard_map/all_to_all | solution.py:199
  25.5 4.1 %shard_map.50 = (f32[2,288,128]{2,1,0:T(8,128)S(1)}, bf16[2,288,128]{2,1,0:T(8,128)(2,1)S(1)}, bf16[512,2048]{1,0:T(8,128)(2,1)S(1)}, bf16[2048,256]{1,0:T(8,128)(2,1)S(1)}, f32[1,2048]{1,0:T(1,128)S(1)}) custom-call(s32[6]{0:T(128)S(1)} %stack.93.where_ref, f32[16,20,128]{2,1,0:T(8,128)S(1)} %all-to-all-done.packed_ref, bf16[2048,256]{1,0:T(8,128)(2,1)S(1)} %copy-done, ...), custom_call_target="tpu_custom_call" | custom-call | tf_op jit(solution)/shard_map/pallas_call | solution.py:165
  29.7 2.5 %collective-permute-start = (bf16[2,288,128]{2,1,0:T(8,128)(2,1)S(1)}, bf16[2,288,128]{2,1,0:T(8,128)(2,1)S(1)}, u32[]{:S(2)}, u32[]{:S(2)}) collective-permute-start(bf16[2,288,128]{2,1,0:T(8,128)(2,1)S(1)} %get-tuple-element.38), channel_id=1, source_target_pairs={{0,16},{16,0},{1,17},{17,1},{2,18},{18,2},{3,19},{19,3},{4,20},{20... | collective-permute-start | bytes 442376 | tf_op jit(solution)/shard_map/ppermute | solution.py:178
  33.7 2.9 %collective-permute-done.1 = bf16[288,128]{1,0:T(8,128)(2,1)S(1)} collective-permute-done((bf16[288,128]{1,0:T(8,128)(2,1)S(1)}, bf16[288,128]{1,0:T(8,128)(2,1)S(1)}, u32[]{:S(2)}, u32[]{:S(2)}) %collective-permute-start.1) | collective-permute-done | bytes 73760 | tf_op jit(solution)/shard_map/ppermute | solution.py:178
  36.6 2.8 %collective-permute-start.4 = (bf16[288,128]{1,0:T(8,128)(2,1)S(1)}, bf16[288,128]{1,0:T(8,128)(2,1)S(1)}, u32[]{:S(2)}, u32[]{:S(2)}) collective-permute-start(bf16[288,128]{1,0:T(8,128)(2,1)S(1)} %fusion.2), channel_id=1, source_target_pairs={{0,192},{64,128},{128,64},{192,0},{1,193},{65,129},{129,65},{193,1... | collective-permute-start | bytes 221192 | tf_op jit(solution)/shard_map/ppermute | solution.py:178
  41.5 2.6 %collective-permute-done.3 = bf16[288,128]{1,0:T(8,128)(2,1)S(1)} collective-permute-done((bf16[288,128]{1,0:T(8,128)(2,1)S(1)}, bf16[288,128]{1,0:T(8,128)(2,1)S(1)}, u32[]{:S(2)}, u32[]{:S(2)}) %collective-permute-start.3) | collective-permute-done | bytes 73760 | tf_op jit(solution)/shard_map/ppermute | solution.py:178
  44.6 2.9 %collective-permute-done.5 = bf16[288,128]{1,0:T(8,128)(2,1)S(1)} collective-permute-done((bf16[288,128]{1,0:T(8,128)(2,1)S(1)}, bf16[288,128]{1,0:T(8,128)(2,1)S(1)}, u32[]{:S(2)}, u32[]{:S(2)}) %collective-permute-start.5) | collective-permute-done | bytes 73760 | tf_op jit(solution)/shard_map/ppermute | solution.py:178
  47.5 4.2 %collective-permute-start.6 = (bf16[2,288,128]{2,1,0:T(8,128)(2,1)S(1)}, bf16[2,288,128]{2,1,0:T(8,128)(2,1)S(1)}, u32[]{:S(2)}, u32[]{:S(2)}) collective-permute-start(bf16[2,288,128]{2,1,0:T(8,128)(2,1)S(1)} %pad_maximum_fusion.2), channel_id=1, source_target_pairs={{0,16},{16,0},{1,17},{17,1},{2,18},{18,2},{3,19},{19,3},{4,20},{20... | collective-permute-start | bytes 442376 | tf_op jit(solution)/shard_map/ppermute | solution.py:178
  52.7 4.4 %shard_map.51 = (f32[2,4,2,2,8,512]{5,4,3,2,1,0:T(8,128)S(1)}, bf16[2,4,2,2,8,512]{5,4,3,2,1,0:T(8,128)(2,1)S(1)}, f32[2,2,8,512]{3,2,1,0:T(8,128)S(1)}, bf16[2,...) custom-call(s32[6]{0:T(128)S(1)} %stack.93.where_ref, ...), custom_call_target="tpu_custom_call" | custom-call | tf_op jit(solution)/shard_map/pallas_call | solution.py:165
  61.2 1.8 %collective-permute-start.12 = (bf16[2,8,512]{2,1,0:T(8,128)(2,1)S(1)}, bf16[2,8,512]{2,1,0:T(8,128)(2,1)S(1)}, u32[]{:S(2)}, u32[]{:S(2)}) collective-permute-start(bf16[2,8,512]{2,1,0:T(8,128)(2,1)S(1)} %get-tuple-element.45), channel_id=1, source_target_pairs={{0,16},{16,32},{32,48},{48,64},{64,80},{80,96},{96,112},{112,128},... | collective-permute-start | bytes 49160 | tf_op jit(solution)/shard_map/ppermute | solution.py:228
  63.0 1.7 %collective-permute-start.13 = (bf16[2,8,512]{2,1,0:T(8,128)(2,1)S(1)}, bf16[2,8,512]{2,1,0:T(8,128)(2,1)S(1)}, u32[]{:S(2)}, u32[]{:S(2)}) collective-permute-start(bf16[2,8,512]{2,1,0:T(8,128)(2,1)S(1)} %get-tuple-element.46), channel_id=1, source_target_pairs={{0,128},{64,192},{128,0},{192,64},{1,129},{65,193},{129,1},{193,65... | collective-permute-start | bytes 49160 | tf_op jit(solution)/shard_map/ppermute | solution.py:178
  66.5 1.7 %collective-permute-start.10 = (bf16[2,2,8,512]{3,2,0,1:T(8,128)(2,1)S(1)}, bf16[2,2,8,512]{3,2,0,1:T(8,128)(2,1)S(1)}, u32[]{:S(2)}, u32[]{:S(2)}) collective-permute-start(bf16[2,2,8,512]{3,2,0,1:T(8,128)(2,1)S(1)} %get-tuple-element.52), channel_id=1, source_target_pairs={{0,128},{64,192},{128,0},{192,64},{1,129},{65,193},{129,1},{193,65... | collective-permute-start | bytes 98312 | tf_op jit(solution)/shard_map/ppermute | solution.py:178
  69.1 1.7 %collective-permute-done.10 = bf16[2,2,8,512]{3,2,0,1:T(8,128)(2,1)S(1)} collective-permute-done((bf16[2,2,8,512]{3,2,0,1:T(8,128)(2,1)S(1)}, bf16[2,2,8,512]{3,2,0,1:T(8,128)(2,1)S(1)}, u32[]{:S(2)}, u32[]{:S(2)}) %collective-permute-start.10) | collective-permute-done | bytes 32800 | tf_op jit(solution)/shard_map/ppermute | solution.py:178
  70.8 1.9 %collective-permute-start.14 = (bf16[5,8,512]{2,1,0:T(8,128)(2,1)S(1)}, bf16[5,8,512]{2,1,0:T(8,128)(2,1)S(1)}, u32[]{:S(2)}, u32[]{:S(2)}) collective-permute-start(bf16[5,8,512]{2,1,0:T(8,128)(2,1)S(1)} %fusion.15), channel_id=1, source_target_pairs={{0,1},{1,0},{2,3},{3,2},{4,5},{5,4},{6,7},{7,6},{8,9},{9,8},{10,11... | collective-permute-start | bytes 122888 | tf_op jit(solution)/shard_map/ppermute | solution.py:178
  76.2 15.4 %all_to_all.10 = bf16[8,5,8,512]{3,2,1,0:T(8,128)(2,1)S(1)} all-to-all(bf16[8,5,8,512]{3,2,1,0:T(8,128)(2,1)S(1)} %broadcast_in_dim.5), channel_id=1, replica_groups=mesh['y'=4,'xl'=2,'c'=2,'xh'=2,'za'=4,'zb'=2] {'xh','za'}, dimensions={0} | all-to-all | bytes 655360 | tf_op jit(solution)/shard_map/all_to_all | solution.py:248
  92.3 2.6 %collective-permute-done.15 = bf16[4,8,512]{2,1,0:T(8,128)(2,1)S(1)} collective-permute-done((bf16[4,8,512]{2,1,0:T(8,128)(2,1)S(1)}, bf16[4,8,512]{2,1,0:T(8,128)(2,1)S(1)}, u32[]{:S(2)}, u32[]{:S(2)}) %collective-permute-start.15) | collective-permute-done | bytes 32800 | tf_op jit(solution)/shard_map/ppermute | solution.py:178
  94.8 1.7 %collective-permute-start.17 = (bf16[2,4,8,512]{3,2,1,0:T(8,128)(2,1)S(1)}, bf16[2,4,8,512]{3,2,1,0:T(8,128)(2,1)S(1)}, u32[]{:S(2)}, u32[]{:S(2)}) collective-permute-start(bf16[2,4,8,512]{3,2,1,0:T(8,128)(2,1)S(1)} %get-tuple-element.54), channel_id=1, source_target_pairs={{0,128},{64,192},{128,0},{192,64},{1,129},{65,193},{129,1},{193,65... | collective-permute-start | bytes 196616 | tf_op jit(solution)/shard_map/ppermute | solution.py:178
  96.7 1.5 %collective-permute-start.18 = (bf16[2,4,8,512]{3,2,1,0:T(8,128)(2,1)S(1)}, bf16[2,4,8,512]{3,2,1,0:T(8,128)(2,1)S(1)}, u32[]{:S(2)}, u32[]{:S(2)}) collective-permute-start(bf16[2,4,8,512]{3,2,1,0:T(8,128)(2,1)S(1)} %get-tuple-element.54), channel_id=1, source_target_pairs={{0,192},{64,128},{128,64},{192,0},{1,193},{65,129},{129,65},{193,1... | collective-permute-start | bytes 196616 | tf_op jit(solution)/shard_map/ppermute | solution.py:178
  101.0 3.2 %collective-permute-start.19 = (bf16[4,2,4,8,512]{4,3,2,1,0:T(8,128)(2,1)S(1)}, bf16[4,2,4,8,512]{4,3,2,1,0:T(8,128)(2,1)S(1)}, u32[]{:S(2)}, u32[]{:S(2)}) collective-permute-start(bf16[4,2,4,8,512]{4,3,2,1,0:T(8,128)(2,1)S(1)} %pad_maximum_fusion.1.refs_0_), channel_id=1, source_target_pairs={{0,32},{32,0},{1,33},{33,1},{2,34},{34,2},{3,35},{35,3},{4,36},{36... | collective-permute-start | bytes 786440 | tf_op jit(solution)/shard_map/ppermute | solution.py:178
  104.2 5.3 %collective-permute-start.20 = (bf16[4,2,4,8,512]{4,3,2,1,0:T(8,128)(2,1)S(1)}, bf16[4,2,4,8,512]{4,3,2,1,0:T(8,128)(2,1)S(1)}, u32[]{:S(2)}, u32[]{:S(2)}) collective-permute-start(bf16[4,2,4,8,512]{4,3,2,1,0:T(8,128)(2,1)S(1)} %pad_maximum_fusion.1.refs_0_), channel_id=1, source_target_pairs={{0,16},{16,0},{1,17},{17,1},{2,18},{18,2},{3,19},{19,3},{4,20},{20... | collective-permute-start | bytes 786440 | tf_op jit(solution)/shard_map/ppermute | solution.py:178
  109.5 5.2 %collective-permute-start.21 = (bf16[4,2,4,8,512]{4,3,2,1,0:T(8,128)(2,1)S(1)}, bf16[4,2,4,8,512]{4,3,2,1,0:T(8,128)(2,1)S(1)}, u32[]{:S(2)}, u32[]{:S(2)}) collective-permute-start(bf16[4,2,4,8,512]{4,3,2,1,0:T(8,128)(2,1)S(1)} %collective-permute-done.19.refs_1_), channel_id=1, source_target_pairs={{0,16},{16,0},{1,17},{17,1},{2,18},{18,2},{3,19},{19,3},{4,20},{20... | collective-permute-start | bytes 786440 | tf_op jit(solution)/shard_map/ppermute | solution.py:178
  116.0 2.1 %shard_map.52 = f32[4,256,512]{2,1,0:T(8,128)} custom-call(s32[6]{0:T(128)S(1)} %stack.93.where_ref, bf16[4,2,4,8,512]{4,3,2,1,0:T(8,128)(2,1)S(1)} %pad_maximum_fusion.1.refs_0_, bf16[4,2,4,8,512]{4,3,2,1,0:T(8,128)(2,1)S(1)} %collective-permute-done.19.refs_1_, bf16[4,2,4,8,512]{4,3,2,1,0:T(8,128)(2,1)S(1)} %collective-permute-done.20.refs_2_, ...), custom_call_target="tpu_custom_call" | custom-call | tf_op jit(solution)/shard_map/pallas_call | solution.py:165
  (64 shorter events, 19.6 us)
Async XLA Ops:
  0.6 23.7 %copy-start = (bf16[2048,256]{1,0:T(8,128)(2,1)S(1)}, bf16[2048,256]{1,0:T(8,128)(2,1)}, u32[]{:S(2)}) copy-start(bf16[2048,256]{1,0:T(8,128)(2,1)} %teacher_ref.1) | copy-start | bytes 3145732
  3.7 20.6 %all-to-all-start = ((f32[16,20,128]{2,1,0:T(8,128)}), f32[16,20,128]{2,1,0:T(8,128)S(1)}, u32[]{:S(2)}, u32[]{:S(2)}) async-start(f32[16,20,128]{2,1,0:T(8,128)} %broadcast_in_dim.4), calls=%async_computation | async-start | bytes 393216 | tf_op jit(solution)/shard_map/all_to_all | solution.py:199
  29.7 3.5 %collective-permute-start = (bf16[2,288,128]{2,1,0:T(8,128)(2,1)S(1)}, bf16[2,288,128]{2,1,0:T(8,128)(2,1)S(1)}, u32[]{:S(2)}, u32[]{:S(2)}) collective-permute-start(bf16[2,288,128]{2,1,0:T(8,128)(2,1)S(1)} %get-tuple-element.38), channel_id=1, source_target_pairs={{0,16},{16,0},{1,17},{17,1},{2,18},{18,2},{3,19},{19,3},{4,20},{20... | collective-permute-start | bytes 442376 | tf_op jit(solution)/shard_map/ppermute | solution.py:178
  33.3 3.3 %collective-permute-start.1 = (bf16[288,128]{1,0:T(8,128)(2,1)S(1)}, bf16[288,128]{1,0:T(8,128)(2,1)S(1)}, u32[]{:S(2)}, u32[]{:S(2)}) collective-permute-start(bf16[288,128]{1,0:T(8,128)(2,1)S(1)} %fusion.6), channel_id=1, source_target_pairs={{0,32},{32,0},{1,33},{33,1},{2,34},{34,2},{3,35},{35,3},{4,36},{36... | collective-permute-start | bytes 221192 | tf_op jit(solution)/shard_map/ppermute | solution.py:178
  36.6 4.9 %collective-permute-start.4 = (bf16[288,128]{1,0:T(8,128)(2,1)S(1)}, bf16[288,128]{1,0:T(8,128)(2,1)S(1)}, u32[]{:S(2)}, u32[]{:S(2)}) collective-permute-start(bf16[288,128]{1,0:T(8,128)(2,1)S(1)} %fusion.2), channel_id=1, source_target_pairs={{0,192},{64,128},{128,64},{192,0},{1,193},{65,129},{129,65},{193,1... | collective-permute-start | bytes 221192 | tf_op jit(solution)/shard_map/ppermute | solution.py:178
  39.4 4.7 %collective-permute-start.3 = (bf16[288,128]{1,0:T(8,128)(2,1)S(1)}, bf16[288,128]{1,0:T(8,128)(2,1)S(1)}, u32[]{:S(2)}, u32[]{:S(2)}) collective-permute-start(bf16[288,128]{1,0:T(8,128)(2,1)S(1)} %fusion.2), channel_id=1, source_target_pairs={{0,128},{64,192},{128,0},{192,64},{1,129},{65,193},{129,1},{193,65... | collective-permute-start | bytes 221192 | tf_op jit(solution)/shard_map/ppermute | solution.py:178
  39.8 4.4 %collective-permute-start.2 = (bf16[288,128]{1,0:T(8,128)(2,1)S(1)}, bf16[288,128]{1,0:T(8,128)(2,1)S(1)}, u32[]{:S(2)}, u32[]{:S(2)}) collective-permute-start(bf16[288,128]{1,0:T(8,128)(2,1)S(1)} %fusion.2), channel_id=1, source_target_pairs={{0,64},{64,0},{128,192},{192,128},{1,65},{65,1},{129,193},{193,129... | collective-permute-start | bytes 221192 | tf_op jit(solution)/shard_map/ppermute | solution.py:178
  44.2 3.3 %collective-permute-start.5 = (bf16[288,128]{1,0:T(8,128)(2,1)S(1)}, bf16[288,128]{1,0:T(8,128)(2,1)S(1)}, u32[]{:S(2)}, u32[]{:S(2)}) collective-permute-start(bf16[288,128]{1,0:T(8,128)(2,1)S(1)} %add_convert_fusion), channel_id=1, source_target_pairs={{0,32},{32,0},{1,33},{33,1},{2,34},{34,2},{3,35},{35,3},{4,36},{36... | collective-permute-start | bytes 221192 | tf_op jit(solution)/shard_map/ppermute | solution.py:178
  47.5 5.2 %collective-permute-start.6 = (bf16[2,288,128]{2,1,0:T(8,128)(2,1)S(1)}, bf16[2,288,128]{2,1,0:T(8,128)(2,1)S(1)}, u32[]{:S(2)}, u32[]{:S(2)}) collective-permute-start(bf16[2,288,128]{2,1,0:T(8,128)(2,1)S(1)} %pad_maximum_fusion.2), channel_id=1, source_target_pairs={{0,16},{16,0},{1,17},{17,1},{2,18},{18,2},{3,19},{19,3},{4,20},{20... | collective-permute-start | bytes 442376 | tf_op jit(solution)/shard_map/ppermute | solution.py:178
  57.1 1.6 %collective-permute-start.7 = (bf16[2,4,2,2,8,512]{5,4,2,3,1,0:T(8,128)(2,1)S(1)}, bf16[2,4,2,2,8,512]{5,4,2,3,1,0:T(8,128)(2,1)S(1)}, u32[]{:S(2)}, u32[]{:S(2)}) collective-permute-start(bf16[2,4,2,2,8,512]{5,4,2,3,1,0:T(8,128)(2,1)S(1)} %copy.9), channel_id=1, source_target_pairs={{0,16},{16,0},{1,17},{17,1},{2,18},{18,2},{3,19},{19,3},{4,20},{20... | collective-permute-start | bytes 786440 | tf_op jit(solution)/shard_map/ppermute | solution.py:178
  58.8 6.0 %collective-permute-start.8 = (bf16[4,2,2,8,512]{4,3,1,2,0:T(8,128)(2,1)S(1)}, bf16[4,2,2,8,512]{4,3,1,2,0:T(8,128)(2,1)S(1)}, u32[]{:S(2)}, u32[]{:S(2)}) collective-permute-start(bf16[4,2,2,8,512]{4,3,1,2,0:T(8,128)(2,1)S(1)} %fusion.3), channel_id=1, source_target_pairs={{0,32},{32,0},{1,33},{33,1},{2,34},{34,2},{3,35},{35,3},{4,36},{36... | collective-permute-start | bytes 393224 | tf_op jit(solution)/shard_map/ppermute | solution.py:178
  61.2 7.0 %collective-permute-start.12 = (bf16[2,8,512]{2,1,0:T(8,128)(2,1)S(1)}, bf16[2,8,512]{2,1,0:T(8,128)(2,1)S(1)}, u32[]{:S(2)}, u32[]{:S(2)}) collective-permute-start(bf16[2,8,512]{2,1,0:T(8,128)(2,1)S(1)} %get-tuple-element.45), channel_id=1, source_target_pairs={{0,16},{16,32},{32,48},{48,64},{64,80},{80,96},{96,112},{112,128},... | collective-permute-start | bytes 49160 | tf_op jit(solution)/shard_map/ppermute | solution.py:228
  63.0 5.2 %collective-permute-start.13 = (bf16[2,8,512]{2,1,0:T(8,128)(2,1)S(1)}, bf16[2,8,512]{2,1,0:T(8,128)(2,1)S(1)}, u32[]{:S(2)}, u32[]{:S(2)}) collective-permute-start(bf16[2,8,512]{2,1,0:T(8,128)(2,1)S(1)} %get-tuple-element.46), channel_id=1, source_target_pairs={{0,128},{64,192},{128,0},{192,64},{1,129},{65,193},{129,1},{193,65... | collective-permute-start | bytes 49160 | tf_op jit(solution)/shard_map/ppermute | solution.py:178
  64.9 3.4 %collective-permute-start.9 = (bf16[2,2,8,512]{3,2,0,1:T(8,128)(2,1)S(1)}, bf16[2,2,8,512]{3,2,0,1:T(8,128)(2,1)S(1)}, u32[]{:S(2)}, u32[]{:S(2)}) collective-permute-start(bf16[2,2,8,512]{3,2,0,1:T(8,128)(2,1)S(1)} %get-tuple-element.50), channel_id=1, source_target_pairs={{0,64},{64,0},{128,192},{192,128},{1,65},{65,1},{129,193},{193,129... | collective-permute-start | bytes 98312 | tf_op jit(solution)/shard_map/ppermute | solution.py:178
  65.0 4.1 %collective-permute-start.11 = (bf16[2,2,8,512]{3,2,0,1:T(8,128)(2,1)S(1)}, bf16[2,2,8,512]{3,2,0,1:T(8,128)(2,1)S(1)}, u32[]{:S(2)}, u32[]{:S(2)}) collective-permute-start(bf16[2,2,8,512]{3,2,0,1:T(8,128)(2,1)S(1)} %get-tuple-element.51), channel_id=1, source_target_pairs={{0,192},{64,128},{128,64},{192,0},{1,193},{65,129},{129,65},{193,1... | collective-permute-start | bytes 98312 | tf_op jit(solution)/shard_map/ppermute | solution.py:178
  66.5 4.3 %collective-permute-start.10 = (bf16[2,2,8,512]{3,2,0,1:T(8,128)(2,1)S(1)}, bf16[2,2,8,512]{3,2,0,1:T(8,128)(2,1)S(1)}, u32[]{:S(2)}, u32[]{:S(2)}) collective-permute-start(bf16[2,2,8,512]{3,2,0,1:T(8,128)(2,1)S(1)} %get-tuple-element.52), channel_id=1, source_target_pairs={{0,128},{64,192},{128,0},{192,64},{1,129},{65,193},{129,1},{193,65... | collective-permute-start | bytes 98312 | tf_op jit(solution)/shard_map/ppermute | solution.py:178
  70.8 3.3 %collective-permute-start.14 = (bf16[5,8,512]{2,1,0:T(8,128)(2,1)S(1)}, bf16[5,8,512]{2,1,0:T(8,128)(2,1)S(1)}, u32[]{:S(2)}, u32[]{:S(2)}) collective-permute-start(bf16[5,8,512]{2,1,0:T(8,128)(2,1)S(1)} %fusion.15), channel_id=1, source_target_pairs={{0,1},{1,0},{2,3},{3,2},{4,5},{5,4},{6,7},{7,6},{8,9},{9,8},{10,11... | collective-permute-start | bytes 122888 | tf_op jit(solution)/shard_map/ppermute | solution.py:178
  91.7 3.1 %collective-permute-start.15 = (bf16[4,8,512]{2,1,0:T(8,128)(2,1)S(1)}, bf16[4,8,512]{2,1,0:T(8,128)(2,1)S(1)}, u32[]{:S(2)}, u32[]{:S(2)}) collective-permute-start(bf16[4,8,512]{2,1,0:T(8,128)(2,1)S(1)} %slice.165), channel_id=1, source_target_pairs={{0,1},{1,0},{2,3},{3,2},{4,5},{5,4},{6,7},{7,6},{8,9},{9,8},{10,11... | collective-permute-start | bytes 98312 | tf_op jit(solution)/shard_map/ppermute | solution.py:178
  94.8 4.7 %collective-permute-start.17 = (bf16[2,4,8,512]{3,2,1,0:T(8,128)(2,1)S(1)}, bf16[2,4,8,512]{3,2,1,0:T(8,128)(2,1)S(1)}, u32[]{:S(2)}, u32[]{:S(2)}) collective-permute-start(bf16[2,4,8,512]{3,2,1,0:T(8,128)(2,1)S(1)} %get-tuple-element.54), channel_id=1, source_target_pairs={{0,128},{64,192},{128,0},{192,64},{1,129},{65,193},{129,1},{193,65... | collective-permute-start | bytes 196616 | tf_op jit(solution)/shard_map/ppermute | solution.py:178
  96.5 3.1 %collective-permute-start.16 = (bf16[2,4,8,512]{3,2,1,0:T(8,128)(2,1)S(1)}, bf16[2,4,8,512]{3,2,1,0:T(8,128)(2,1)S(1)}, u32[]{:S(2)}, u32[]{:S(2)}) collective-permute-start(bf16[2,4,8,512]{3,2,1,0:T(8,128)(2,1)S(1)} %get-tuple-element.54), channel_id=1, source_target_pairs={{0,64},{64,0},{128,192},{192,128},{1,65},{65,1},{129,193},{193,129... | collective-permute-start | bytes 196616 | tf_op jit(solution)/shard_map/ppermute | solution.py:178
  96.7 4.3 %collective-permute-start.18 = (bf16[2,4,8,512]{3,2,1,0:T(8,128)(2,1)S(1)}, bf16[2,4,8,512]{3,2,1,0:T(8,128)(2,1)S(1)}, u32[]{:S(2)}, u32[]{:S(2)}) collective-permute-start(bf16[2,4,8,512]{3,2,1,0:T(8,128)(2,1)S(1)} %get-tuple-element.54), channel_id=1, source_target_pairs={{0,192},{64,128},{128,64},{192,0},{1,193},{65,129},{129,65},{193,1... | collective-permute-start | bytes 196616 | tf_op jit(solution)/shard_map/ppermute | solution.py:178
  101.0 8.5 %collective-permute-start.19 = (bf16[4,2,4,8,512]{4,3,2,1,0:T(8,128)(2,1)S(1)}, bf16[4,2,4,8,512]{4,3,2,1,0:T(8,128)(2,1)S(1)}, u32[]{:S(2)}, u32[]{:S(2)}) collective-permute-start(bf16[4,2,4,8,512]{4,3,2,1,0:T(8,128)(2,1)S(1)} %pad_maximum_fusion.1.refs_0_), channel_id=1, source_target_pairs={{0,32},{32,0},{1,33},{33,1},{2,34},{34,2},{3,35},{35,3},{4,36},{36... | collective-permute-start | bytes 786440 | tf_op jit(solution)/shard_map/ppermute | solution.py:178
  104.2 11.7 %collective-permute-start.20 = (bf16[4,2,4,8,512]{4,3,2,1,0:T(8,128)(2,1)S(1)}, bf16[4,2,4,8,512]{4,3,2,1,0:T(8,128)(2,1)S(1)}, u32[]{:S(2)}, u32[]{:S(2)}) collective-permute-start(bf16[4,2,4,8,512]{4,3,2,1,0:T(8,128)(2,1)S(1)} %pad_maximum_fusion.1.refs_0_), channel_id=1, source_target_pairs={{0,16},{16,0},{1,17},{17,1},{2,18},{18,2},{3,19},{19,3},{4,20},{20... | collective-permute-start | bytes 786440 | tf_op jit(solution)/shard_map/ppermute | solution.py:178
  109.5 6.5 %collective-permute-start.21 = (bf16[4,2,4,8,512]{4,3,2,1,0:T(8,128)(2,1)S(1)}, bf16[4,2,4,8,512]{4,3,2,1,0:T(8,128)(2,1)S(1)}, u32[]{:S(2)}, u32[]{:S(2)}) collective-permute-start(bf16[4,2,4,8,512]{4,3,2,1,0:T(8,128)(2,1)S(1)} %collective-permute-done.19.refs_1_), channel_id=1, source_target_pairs={{0,16},{16,0},{1,17},{17,1},{2,18},{18,2},{3,19},{19,3},{4,20},{20... | collective-permute-start | bytes 786440 | tf_op jit(solution)/shard_map/ppermute | solution.py:178
  (1 other events, 1.2 us)

commit v2 on v1

v2 whole, which is shorter than its diff:
```python
import jax
import jax.numpy as jnp
from jax import lax
from jax.experimental import pallas as pl
from jax.experimental.pallas import tpu as pltpu
from jax.sharding import Mesh
from jax.sharding import PartitionSpec as P

DT = 4096
DS = 512
EPS = 1e-06
F32 = jnp.float32
BF16 = jnp.bfloat16
FEAT = ("xh", "za", "zb")
ITEM = ("y", "xl", "c")
ROWS = 576
CHUNK = 512

NT = (((1,), (1,)), ((), ()))
ANY, HBM, SMEM, VMEM = pl.ANY, pltpu.HBM, pltpu.SMEM, pltpu.VMEM


def lanes_of(packed_ref, row, start, count):
    return jnp.concatenate([packed_ref[start + j, row : row + 1, :] for j in range(count)], axis=1)


def codes_of(packed_ref, level, start, count):
    return lanes_of(packed_ref, 16 + level, start, count).astype(jnp.int32)


def pack_kernel(teacher_hbm, codes_hbm, teacher_ref, packed_ref, codes_ref, gathered, sems):
    first = pltpu.make_async_copy(codes_hbm, codes_ref, sems.at[4])
    first.start()
    copies = []
    for n in range(4):
        rows = pl.ds(n * 512, 512)
        copies.append(pltpu.make_async_copy(teacher_hbm.at[rows], teacher_ref.at[rows], sems.at[n]))
        copies[-1].start()
    first.wait()
    gathered[16:20, :] = codes_ref[...].astype(F32)
    gathered[20:24, :] = jnp.zeros((4, 128), F32)
    ones = jnp.ones((8, 256), BF16)
    for n in range(4):
        copies[n].wait()
        rows = teacher_ref[n * 512 : (n + 1) * 512, :].astype(F32)
        squares = rows * rows
        upper = squares.astype(BF16)
        lower = (squares - upper.astype(F32)).astype(BF16)
        sums = lax.dot_general(ones, upper, NT, preferred_element_type=F32)
        sums = sums + lax.dot_general(ones, lower, NT, preferred_element_type=F32)
        for j in range(4):
            gathered[4 * n + j : 4 * n + j + 1, :] = sums[0:1, j * 128 : (j + 1) * 128]
    packed_ref[...] = gathered[...].astype(BF16)


def table_kernel(where_ref, book_ref, table_ref):
    item = where_ref[0]
    low = item & 7
    picked = jnp.concatenate(
        [
            book_ref[0, item],
            book_ref[0, (item + 1) & 15],
            book_ref[1, 2 * low],
            book_ref[1, 2 * low + 1],
            book_ref[2].reshape(256, DS),
            book_ref[3].reshape(256, DS),
        ],
        axis=0,
    )
    table_ref[...] = picked.astype(F32).T.astype(BF16)


def cross_kernel(where_ref, packed_ref, teacher_ref, table_ref, keep_ref, send_ref, student_ref, tnorm_ref, inv_ref, packed):
    packed[...] = packed_ref[...].astype(F32)
    item, feat, me = where_ref[0], where_ref[1], where_ref[2]
    low = item & 7
    table = table_ref[...]
    per = CHUNK // 128
    small = lax.broadcasted_iota(jnp.int32, (32, CHUNK), 0)
    large = lax.broadcasted_iota(jnp.int32, (256, CHUNK), 0)
    for n in range(2048 // CHUNK):
        first = (codes_of(packed, 0, n * per, per) - 16 * item) & 255
        second = codes_of(packed, 1, n * per, per) - 32 * low
        onehot = jnp.concatenate(
            [
                (small == first).astype(F32),
                (small == second).astype(F32),
                (large == codes_of(packed, 2, n * per, per)).astype(F32),
                (large == codes_of(packed, 3, n * per, per)).astype(F32),
            ],
            axis=0,
        ).astype(BF16)
        recon = jnp.dot(table, onehot, preferred_element_type=F32)
        inv = lax.rsqrt(jnp.sum(recon * recon, axis=0, keepdims=True) / DS + EPS)
        student_ref[:, n * CHUNK : (n + 1) * CHUNK] = (recon * inv).astype(BF16)
        inv_ref[:, n * CHUNK : (n + 1) * CHUNK] = inv
    squares = packed[0, 0:16, :]
    for j in range(1, 16):
        squares = squares + packed[j, 0:16, :]
    factor = lax.rsqrt(squares / DT + EPS)
    for j in range(16):
        column = jnp.broadcast_to(factor[j : j + 1, :], (128, 128)).T
        rows = teacher_ref[j * 128 : (j + 1) * 128, :].astype(F32)
        tnorm_ref[j * 128 : (j + 1) * 128, :] = (rows * jnp.concatenate([column, column], axis=1)).astype(BF16)
    student = student_ref[...]
    cross = jnp.dot(student, tnorm_ref[...], preferred_element_type=F32)
    mine = student_ref[pl.ds(pl.multiple_of(feat * 32, 32), 32), :]
    gram = lax.dot_general(mine, student, NT, preferred_element_type=F32)
    for b in range(4):
        to = b ^ me

        def store(ref, at):
            ref[at, 0:128, :] = cross[b * 128 : (b + 1) * 128, 0:128]
            ref[at, 128:256, :] = cross[b * 128 : (b + 1) * 128, 128:256]
            ref[at, 256:288, :] = gram[:, b * 128 : (b + 1) * 128]

        @pl.when(to < 2)
        def _():
            store(keep_ref, to)

        @pl.when(to >= 2)
        def _():
            store(send_ref, to - 2)


def grad_kernel(where_ref, packed_ref, whole_ref, student_ref, tnorm_ref, inv_ref, keep_ref, send_ref, near_ref, other_ref, loss_ref, cross, gram, packed):
    packed[...] = packed_ref[...].astype(F32)
    item, feat, me = where_ref[0], where_ref[1], where_ref[2]
    place, zb, half = where_ref[3], where_ref[4], where_ref[5]
    for b in range(4):
        block = whole_ref[b ^ me]
        cross[b * 128 : (b + 1) * 128, 0:128] = block[0:128]
        cross[b * 128 : (b + 1) * 128, 128:256] = block[128:256]
        gram[:, b * 128 : (b + 1) * 128] = block[256:288]
    cross_f = cross[...].astype(F32)
    gram_f = gram[...].astype(F32)
    loss = jnp.sum(gram_f * gram_f, keepdims=True) - 2.0 * jnp.sum(cross_f * cross_f, keepdims=True)
    high = loss.astype(BF16).astype(F32)
    middle = (loss - high).astype(BF16).astype(F32)
    rest = (loss - high - middle).astype(BF16).astype(F32)
    row = lax.broadcasted_iota(jnp.int32, (8, DS), 0)
    lane = lax.broadcasted_iota(jnp.int32, (8, DS), 1)
    parts = jnp.where(row == 0, high, jnp.where(row == 1, middle, jnp.where(row == 2, rest, 0.0)))
    loss_ref[...] = jnp.where(lane == feat, parts, 0.0)
    gram_t = gram_f.T.astype(BF16)
    per = CHUNK // 128
    total = jnp.zeros((ROWS, DS), F32)
    large = lax.broadcasted_iota(jnp.int32, (512, CHUNK), 0)
    small = lax.broadcasted_iota(jnp.int32, (64, CHUNK), 0) + 512
    for n in range(2048 // CHUNK):
        span = slice(n * CHUNK, (n + 1) * CHUNK)
        mine = student_ref[pl.ds(pl.multiple_of(feat * 32, 32), 32), span]
        push = jnp.dot(gram_t, mine, preferred_element_type=F32)
        pull = lax.dot_general(cross[...], tnorm_ref[span, :], NT, preferred_element_type=F32)
        value = push - pull
        student = student_ref[:, span].astype(F32)
        mean = jnp.sum(value * student, axis=0, keepdims=True) / DS
        grad = ((value - student * mean) * (inv_ref[:, span] / 32768.0)).astype(BF16)

        def spot(code, level):
            low = code & 15
            return (((code >> 4) ^ place) << 5) + (((low >> 3) ^ zb) << 4) + 8 * level + (low & 7)

        first = (codes_of(packed, 0, n * per, per) - 16 * item) & 255
        own = 512 + (((first >> 3) ^ zb) << 4) + (first & 7)
        first = jnp.where(first < 16, own, 560)
        second = codes_of(packed, 1, n * per, per) - 32 * (item & 7)
        low = second & 15
        side = (low >> 3) ^ zb
        second = jnp.where(
            ((second >> 4) ^ half) == 0, 520 + (side << 4) + (low & 7), 544 + (side << 3) + (low & 7)
        )
        third = spot(codes_of(packed, 2, n * per, per), 0)
        fourth = spot(codes_of(packed, 3, n * per, per), 1)
        onehot = jnp.concatenate(
            [
                ((large == third) | (large == fourth)).astype(F32),
                ((small == first) | (small == second)).astype(F32),
            ],
            axis=0,
        ).astype(BF16)
        total = total + lax.dot_general(onehot, grad, NT, preferred_element_type=F32)
    keep_ref[...] = total[0:256].reshape(keep_ref.shape)
    send_ref[0:32] = total[256:512].reshape(32, 8, DS)
    send_ref[32] = total[560:568]
    near_ref[...] = total[512:544].reshape(near_ref.shape)
    other_ref[...] = total[544:560].reshape(other_ref.shape).astype(BF16)


def spread_half(c, where_ref, piece_ref, out_hbm, rows, sems):
    place, zb = where_ref[3], where_ref[4]
    kept = c ^ (place >> 3)
    for x in range(2):
        for y in range(4):
            at = (x * 4 + y) ^ (place & 7)
            ay, axl = at & 3, at >> 2
            row0 = (ay * 2 + axl) * 16
            row1 = ((ay & 1) * 2 + axl) * 32 + (ay >> 1) * 16
            row2 = at * 16
            for z in range(2):
                shift = (z ^ zb) * 8
                for k, (level, row) in enumerate(((2, row2), (3, row2), (0, row0), (1, row1))):
                    rows[level, pl.ds(pl.multiple_of(row + shift, 8), 8), :] = piece_ref[x * 4 + y, z, k].astype(F32)
    copies = []

    def copy(level, start, count, to):
        target = out_hbm.at[level, pl.ds(pl.multiple_of(to, 16), count)]
        copies.append(pltpu.make_async_copy(rows.at[level, pl.ds(start, count)], target, sems.at[len(copies)]))
        copies[-1].start()

    copy(2, 0, 128, kept * 128)
    copy(3, 0, 128, kept * 128)
    for j in range(8):
        copy(0, j * 16, 16, (j * 2 + (kept ^ (j & 1) ^ ((j >> 1) & 1))) * 16)
    for j in range(4):
        copy(1, j * 32, 32, (j * 2 + (kept ^ (j & 1) ^ (j >> 1))) * 32)
    for one in copies:
        one.wait()


def near_kernel(where_ref, piece_ref, parts_ref, out_hbm, loss_ref, rows, sems):
    loss_ref[...] = jnp.sum(parts_ref[...], keepdims=True) / (32768.0 * 32768.0 * DS)
    spread_half(0, where_ref, piece_ref, out_hbm, rows, sems)


def far_kernel(where_ref, piece_ref, begun_hbm, out_hbm, rows, sems):
    spread_half(1, where_ref, piece_ref, out_hbm, rows, sems)


def call(kernel, ins, outs, scratch=(), aliases=None):
    return pl.pallas_call(
        kernel,
        out_shape=[jax.ShapeDtypeStruct(shape, kind) for shape, kind, _ in outs],
        in_specs=[pl.BlockSpec(memory_space=space) for space in ins],
        out_specs=[pl.BlockSpec(memory_space=space) for _, _, space in outs],
        scratch_shapes=list(scratch),
        input_output_aliases=aliases or {},
        compiler_params=pltpu.CompilerParams(vmem_limit_bytes=48 << 20),
    )


def swap(array, axis, size, bit):
    return lax.ppermute(array, axis, [(j, j ^ bit) for j in range(size)])


def in_hbm(array):
    return pltpu.with_memory_space_constraint(array, pltpu.HBM)


def across_x(array):
    return swap(array, ("xl", "c"), 4, 3)


def across_y(array, bits):
    return swap(array, ("y", "c"), 8, 2 * bits + (bits & 1))


def on_device(teacher, codebooks, codes):
    y, xl, c = lax.axis_index("y"), lax.axis_index("xl"), lax.axis_index("c")
    zb = lax.axis_index("zb")
    item = y * 4 + xl * 2 + c
    feat = lax.axis_index(FEAT)
    kept = c ^ xl ^ (y & 1)
    where = jnp.stack([item, feat, kept * 2 + xl, kept * 8 + xl * 4 + y, zb, y >> 1]).astype(jnp.int32)

    teacher, packed = call(
        pack_kernel,
        [HBM, HBM],
        [((2048, 256), BF16, VMEM), ((24, 128), BF16, VMEM)],
        [pltpu.VMEM((4, 128), jnp.int32), pltpu.VMEM((24, 128), F32), pltpu.SemaphoreType.DMA((5,))],
    )(in_hbm(teacher), in_hbm(codes.T))
    packed = lax.all_to_all(jnp.broadcast_to(packed[None], (16, 24, 128)), FEAT, 0, 0, tiled=True)
    (table,) = call(table_kernel, [SMEM, VMEM], [((DS, ROWS), BF16, VMEM)])(where, codebooks.reshape(4, 16, 16, DS))

    keep, send, student, tnorm, inv = call(
        cross_kernel,
        [SMEM, VMEM, VMEM, VMEM],
        [
            ((2, 288, 128), F32, VMEM),
            ((2, 288, 128), F32, VMEM),
            ((DS, 2048), BF16, VMEM),
            ((2048, 256), BF16, VMEM),
            ((1, 2048), F32, VMEM),
        ],
        [pltpu.VMEM((16, 24, 128), F32)],
    )(where, packed, teacher, table)

    part = keep + swap(send, "c", 2, 1)
    part = part[0] + across_x(part[1].astype(BF16)).astype(F32)
    own = part.astype(BF16)
    a, b, d = (across_y(own, k) for k in (1, 2, 3))
    whole = ((own.astype(F32) + a.astype(F32)) + (b.astype(F32) + d.astype(F32))).astype(BF16)
    whole = jnp.stack([whole, across_x(whole)])
    whole = jnp.concatenate([whole, swap(whole, "c", 2, 1)])

    keep, send, near, other, loss = call(
        grad_kernel,
        [SMEM] + [VMEM] * 5,
        [
            ((32, 8, DS), F32, VMEM),
            ((33, 8, DS), F32, VMEM),
            ((2, 2, 8, DS), F32, VMEM),
            ((2, 8, DS), BF16, VMEM),
            ((8, DS), F32, VMEM),
        ],
        [pltpu.VMEM((DS, 256), BF16), pltpu.VMEM((32, DS), BF16), pltpu.VMEM((16, 24, 128), F32)],
    )(where, packed, whole, student, tnorm, inv)

    got = swap(send, "c", 2, 1)
    sums = keep + got[:32]
    none = jnp.zeros((), BF16)
    extra = jnp.where(c == 1, got[32], 0.0)
    ahead = jnp.where((c == 1) & (xl == 0), send[32:], jnp.where((c == 0) & (xl == 1), got[32:], 0.0))
    got = across_x(jnp.concatenate([sums[16:].astype(BF16), ahead.astype(BF16)]))
    sums = sums[:16] + got[:16].astype(F32)
    extra = extra + jnp.where((c == 0) & (xl == 1), got[16].astype(F32), 0.0)
    ahead = jnp.where((c == 1) & (xl == 0), got[16:], none)
    odd = (y & 1) == 1
    one = across_y(jnp.concatenate([sums[4:8].astype(BF16), jnp.where(odd, none, ahead)]), 1)
    two = across_y(jnp.concatenate([sums[8:12].astype(BF16), other]), 2)
    three = across_y(jnp.concatenate([sums[12:16].astype(BF16), jnp.where(odd, ahead, none)]), 3)
    sums = sums[0:4] + one[:4].astype(F32) + two[:4].astype(F32) + three[:4].astype(F32)
    extra = extra + one[4].astype(F32) + three[4].astype(F32)

    def rows_of(z):
        zero = near[z, 0] + jnp.where(zb == z, extra, 0.0)
        first = near[z, 1] + two[4 + z].astype(F32)
        return jnp.concatenate([sums[2 * z : 2 * z + 2], zero[None], first[None], loss[None]])

    rows = rows_of(0) + swap(rows_of(1).astype(BF16), "zb", 2, 1).astype(F32)
    sent = jnp.broadcast_to(rows.astype(BF16)[None], (8, 5, 8, DS))
    got = lax.all_to_all(sent, ("xh", "za"), 0, 0, tiled=True)
    rows = jnp.sum(got.astype(F32), axis=0)
    loss = rows[4]
    rows = rows[:4].astype(BF16)

    rows = jnp.stack([rows, swap(rows, "zb", 2, 1)])
    rows = jnp.stack([rows] + [across_y(rows, k) for k in (1, 2, 3)])
    rows = jnp.concatenate([rows, across_x(rows[:2]), swap(rows[2:], ("xl", "c", "xh"), 8, 7)])
    far = swap(rows, "c", 2, 1)
    rows_and_sems = [pltpu.VMEM((4, 128, DS), F32), pltpu.SemaphoreType.DMA((14,))]
    grads, loss = call(
        near_kernel, [SMEM, VMEM, VMEM], [((4, 256, DS), F32, ANY), ((1, 1), F32, VMEM)], rows_and_sems
    )(where, rows, loss)
    (grads,) = call(far_kernel, [SMEM, VMEM, ANY], [((4, 256, DS), F32, ANY)], rows_and_sems, {2: 0})(where, far, grads)
    return (loss.reshape(()), grads)


def solution(mesh):
    split = Mesh(mesh.devices.reshape(4, 2, 2, 2, 4, 2), ITEM + FEAT)
    return jax.shard_map(
        on_device,
        mesh=split,
        in_specs=(P(ITEM, FEAT), P(), P(ITEM + FEAT, None)),
        out_specs=(P(), P()),
        check_vma=False,
    )
```

time: 120 us -> 114 us (0.950)
  starting transfers between devices: 50 us -> 38.1 us
  waiting for transfers between devices: 31.2 us -> 42.2 us
  Pallas kernels: 10.6 us -> 15.4 us
  between operations: 5.28 us -> 1.07 us
  other arithmetic: 4.13 us -> 0.47 us
  local copies, waits for them, and re-layouts: 2.61 us -> 0.87 us
    ppermute x21 -> x20, waiting for transfers between devices: 22.3 us -> 34.1 us  [swap(): return lax.ppermute(array, axis, [(j, j ^ bit) for j in range(size)])]
    ppermute x21 -> x20, starting transfers between devices: 36.7 us -> 26.6 us  [swap(): return lax.ppermute(array, axis, [(j, j ^ bit) for j in range(size)])]
    pallas_call x3 -> x6, Pallas kernels: 10.6 us -> 15.4 us  [the longest x1 4.37 us: on_device(): call(grad_kernel, [SMEM] + [VMEM] * 5, [((32, 8, DS), F32, VMEM), ((33, 8...]
    reduce_sum x4 -> x1, other arithmetic: 2.82 us -> 0.05 us  [on_device(): rows = jnp.sum(got.astype(F32), axis=0)]
    ppermute x1 -> x0, starting transfers between devices: 1.76 us -> none  [on_device(): after = lax.ppermute(after, ITEM, [(j, (j + 1) % 16) for j in range(16)])]
    unnamed x4 -> x6, local copies, waits for them, and re-layouts: 1.23 us -> 0.03 us
  transfers between devices with their start and end apart: 23 -> 21, of which waited for: 15 -> 15; matrix products, arithmetic and copies ran while one was open for 1% -> 0% of each run, Pallas kernels for 0% -> 3%
where the time goes in v2:
time: 114 us; the launch traced here: 113 us
  waiting for transfers between devices  42.2 us (37%)
  starting transfers between devices  38.1 us (33%)
  Pallas kernels  15.4 us (14%)
  blocking collectives  15.1 us (13%)
    ppermute x20, waiting for transfers between devices, swap(): return lax.ppermute(array, axis, [(j, j ^ bit) for j in range(size)])  34.1 us
    ppermute x20, starting transfers between devices, swap(): return lax.ppermute(array, axis, [(j, j ^ bit) for j in range(size)])  26.6 us
    all_to_all x1, blocking collectives, on_device(): got = lax.all_to_all(sent, ('xh', 'za'), 0, 0, tiled=True)  15.1 us
    all_to_all x1, starting transfers between devices, on_device(): lax.all_to_all(jnp.broadcast_to(packed[None], (16, 24, 128)), FEAT, 0, 0,...  11.6 us
    all_to_all x1, waiting for transfers between devices, on_device(): lax.all_to_all(jnp.broadcast_to(packed[None], (16, 24, 128)), FEAT, 0, 0,...  8.1 us
    pallas_call x1, Pallas kernels, on_device(): call(grad_kernel, [SMEM] + [VMEM] * 5, [((32, 8, DS), F32, VMEM), ((33, 8...  4.37 us
    pallas_call x1, Pallas kernels, on_device(): call(cross_kernel, [SMEM, VMEM, VMEM, VMEM], [((2, 288, 128), F32, VMEM),...  4.04 us
  transfers between devices with their start and end apart: 21, of which 15 were waited for; matrix products, arithmetic and copies ran while one was open for 0% of the time, Pallas kernels for 3%

profile of v2, /device:TPU:1, one launch (start us, length us, event | category | flops | bytes accessed | tf_op | source)
XLA Modules:
  0.0 113.3 jit_solution(2879496851284581977)
XLA Ops:
  0.6 2.2 %shard_map.50 = (bf16[2048,256]{1,0:T(8,128)(2,1)S(1)}, bf16[24,128]{1,0:T(8,128)(2,1)S(1)}) custom-call(bf16[2048,256]{1,0:T(8,128)(2,1)} %teacher_hbm.1, s32[4,128]{1,0:T(4,128)} %bitcast.58), custom_call_target="tpu_custom_call" | custom-call | tf_op jit(solution)/shard_map/pallas_call | solution.py:266
  3.5 11.6 %all-to-all-start = ((bf16[16,24,128]{2,1,0:T(8,128)(2,1)}), bf16[16,24,128]{2,1,0:T(8,128)(2,1)S(1)}, u32[]{:S(2)}, u32[]{:S(2)}) async-start(bf16[16,24,128]{2,1,0:T(8,128)(2,1)} %broadcast_in_dim.36), calls=%async_computation | async-start | bytes 196608 | tf_op jit(solution)/shard_map/all_to_all | solution.py:272
  16.0 8.1 %all-to-all-done.packed_ref = bf16[16,24,128]{2,1,0:T(8,128)(2,1)S(1)} async-done(((bf16[16,24,128]{2,1,0:T(8,128)(2,1)}), bf16[16,24,128]{2,1,0:T(8,128)(2,1)S(1)}, u32[]{:S(2)}, u32[]{:S(2)}) %all-to-all-start) | async-done | bytes 98336 | tf_op jit(solution)/shard_map/all_to_all | solution.py:272
  24.1 4.0 %shard_map.52 = (f32[2,288,128]{2,1,0:T(8,128)S(1)}, f32[2,288,128]{2,1,0:T(8,128)S(1)}, bf16[512,2048]{1,0:T(8,128)(2,1)S(1)}, bf16[2048,256]{1,0:T(8,128)(2,1)S(1)}, f32[1,2048]{1,0:T(1,128)S(1)}) custom-call(s32[6]{0:T(128)S(1)} %stack.62.where_ref, bf16[16,24,128]{2,1,0:T(8,128)(2,1)S(1)} %all-to-all-done.packed_ref, ...), custom_call_target="tpu_custom_call" | custom-call | tf_op jit(solution)/shard_map/pallas_call | solution.py:275
  28.1 2.1 %collective-permute-start = (f32[2,288,128]{2,1,0:T(8,128)S(1)}, f32[2,288,128]{2,1,0:T(8,128)S(1)}, u32[]{:S(2)}, u32[]{:S(2)}) collective-permute-start(f32[2,288,128]{2,1,0:T(8,128)S(1)} %get-tuple-element.19), channel_id=1, source_target_pairs={{0,16},{16,0},{1,17},{17,1},{2,18},{18,2},{3,19},{19,3},{4,20},{20... | collective-permute-start | bytes 884744 | tf_op jit(solution)/shard_map/ppermute | solution.py:243
  32.2 3.7 %collective-permute-done.1 = bf16[288,128]{1,0:T(8,128)(2,1)S(1)} collective-permute-done((bf16[288,128]{1,0:T(8,128)(2,1)S(1)}, bf16[288,128]{1,0:T(8,128)(2,1)S(1)}, u32[]{:S(2)}, u32[]{:S(2)}) %collective-permute-start.1) | collective-permute-done | bytes 73760 | tf_op jit(solution)/shard_map/ppermute | solution.py:243
  35.8 1.6 %collective-permute-start.2 = (bf16[288,128]{1,0:T(8,128)(2,1)S(1)}, bf16[288,128]{1,0:T(8,128)(2,1)S(1)}, u32[]{:S(2)}, u32[]{:S(2)}) collective-permute-start(bf16[288,128]{1,0:T(8,128)(2,1)S(1)} %fusion.1), channel_id=1, source_target_pairs={{0,80},{16,64},{64,16},{80,0},{128,208},{144,192},{192,144},{208,1... | collective-permute-start | bytes 221192 | tf_op jit(solution)/shard_map/ppermute | solution.py:243
  37.5 2.6 %collective-permute-start.3 = (bf16[288,128]{1,0:T(8,128)(2,1)S(1)}, bf16[288,128]{1,0:T(8,128)(2,1)S(1)}, u32[]{:S(2)}, u32[]{:S(2)}) collective-permute-start(bf16[288,128]{1,0:T(8,128)(2,1)S(1)} %fusion.1), channel_id=1, source_target_pairs={{0,128},{16,144},{64,192},{80,208},{128,0},{144,16},{192,64},{208,... | collective-permute-start | bytes 221192 | tf_op jit(solution)/shard_map/ppermute | solution.py:243
  40.4 3.8 %collective-permute-done.3 = bf16[288,128]{1,0:T(8,128)(2,1)S(1)} collective-permute-done((bf16[288,128]{1,0:T(8,128)(2,1)S(1)}, bf16[288,128]{1,0:T(8,128)(2,1)S(1)}, u32[]{:S(2)}, u32[]{:S(2)}) %collective-permute-start.3) | collective-permute-done | bytes 73760 | tf_op jit(solution)/shard_map/ppermute | solution.py:243
  44.2 1.8 %collective-permute-done.4 = bf16[288,128]{1,0:T(8,128)(2,1)S(1)} collective-permute-done((bf16[288,128]{1,0:T(8,128)(2,1)S(1)}, bf16[288,128]{1,0:T(8,128)(2,1)S(1)}, u32[]{:S(2)}, u32[]{:S(2)}) %collective-permute-start.4) | collective-permute-done | bytes 73760 | tf_op jit(solution)/shard_map/ppermute | solution.py:243
  46.7 3.7 %collective-permute-done.5 = bf16[288,128]{1,0:T(8,128)(2,1)S(1)} collective-permute-done((bf16[288,128]{1,0:T(8,128)(2,1)S(1)}, bf16[288,128]{1,0:T(8,128)(2,1)S(1)}, u32[]{:S(2)}, u32[]{:S(2)}) %collective-permute-start.5) | collective-permute-done | bytes 73760 | tf_op jit(solution)/shard_map/ppermute | solution.py:243
  52.0 4.4 %shard_map.53 = (f32[32,8,512]{2,1,0:T(8,128)S(1)}, f32[33,8,512]{2,1,0:T(8,128)S(1)}, f32[2,2,8,512]{3,2,1,0:T(8,128)S(1)}, bf16[2,8,512]{2,1,0:T(8,128)(2,1)S(1)}, f32[8,512]{1,0:T(8,128)S(1)}) custom-call(s32[6]{0:T(128)S(1)} %stack.62.where_ref, bf16[16,24,128]{2,1,0:T(8,128)(2,1)S(1)} %all-to-all-done.packed_ref, ...), custom_call_target="tpu_custom_call" | custom-call | tf_op jit(solution)/shard_map/pallas_call | solution.py:296
  57.0 1.6 %collective-permute-done.7 = f32[33,8,512]{2,1,0:T(8,128)S(1)} collective-permute-done((f32[33,8,512]{2,1,0:T(8,128)S(1)}, f32[33,8,512]{2,1,0:T(8,128)S(1)}, u32[]{:S(2)}, u32[]{:S(2)}) %collective-permute-start.7) | collective-permute-done | bytes 540704 | tf_op jit(solution)/shard_map/ppermute | solution.py:243
  59.3 5.1 %collective-permute-done.8 = bf16[17,8,512]{2,1,0:T(8,128)(2,1)S(1)} collective-permute-done((bf16[17,8,512]{2,1,0:T(8,128)(2,1)S(1)}, bf16[17,8,512]{2,1,0:T(8,128)(2,1)S(1)}, u32[]{:S(2)}, u32[]{:S(2)}) %collective-permute-start.8) | collective-permute-done | bytes 139296 | tf_op jit(solution)/shard_map/ppermute | solution.py:243
  66.5 1.7 %collective-permute-start.11 = (bf16[5,8,512]{2,1,0:T(8,128)(2,1)S(1)}, bf16[5,8,512]{2,1,0:T(8,128)(2,1)S(1)}, u32[]{:S(2)}, u32[]{:S(2)}) collective-permute-start(bf16[5,8,512]{2,1,0:T(8,128)(2,1)S(1)} %pad_maximum_fusion.8), channel_id=1, source_target_pairs={{0,208},{16,192},{64,144},{80,128},{128,80},{144,64},{192,16},{208... | collective-permute-start | bytes 122888 | tf_op jit(solution)/shard_map/ppermute | solution.py:243
  69.2 2.0 %collective-permute-done.11 = bf16[5,8,512]{2,1,0:T(8,128)(2,1)S(1)} collective-permute-done((bf16[5,8,512]{2,1,0:T(8,128)(2,1)S(1)}, bf16[5,8,512]{2,1,0:T(8,128)(2,1)S(1)}, u32[]{:S(2)}, u32[]{:S(2)}) %collective-permute-start.11) | collective-permute-done | bytes 40992 | tf_op jit(solution)/shard_map/ppermute | solution.py:243
  72.1 2.0 %collective-permute-done.12 = bf16[5,8,512]{2,1,0:T(8,128)(2,1)S(1)} collective-permute-done((bf16[5,8,512]{2,1,0:T(8,128)(2,1)S(1)}, bf16[5,8,512]{2,1,0:T(8,128)(2,1)S(1)}, u32[]{:S(2)}, u32[]{:S(2)}) %collective-permute-start.12) | collective-permute-done | bytes 40992 | tf_op jit(solution)/shard_map/ppermute | solution.py:243
  74.2 15.1 %all_to_all.10 = bf16[8,5,8,512]{3,2,1,0:T(8,128)(2,1)S(1)} all-to-all(bf16[8,5,8,512]{3,2,1,0:T(8,128)(2,1)S(1)} %broadcast_in_dim.40), channel_id=1, replica_groups=mesh['y'=4,'xl'=2,'c'=2,'xh'=2,'za'=4,'zb'=2] {'xh','za'}, dimensions={0} | all-to-all | bytes 655360 | tf_op jit(solution)/shard_map/all_to_all | solution.py:332
  89.4 2.4 %collective-permute-start.13 = (bf16[4,8,512]{2,1,0:T(8,128)(2,1)S(1)}, bf16[4,8,512]{2,1,0:T(8,128)(2,1)S(1)}, u32[]{:S(2)}, u32[]{:S(2)}) collective-permute-start(bf16[4,8,512]{2,1,0:T(8,128)(2,1)S(1)} %slice.205), channel_id=1, source_target_pairs={{0,1},{1,0},{2,3},{3,2},{4,5},{5,4},{6,7},{7,6},{8,9},{9,8},{10,11... | collective-permute-start | bytes 98312 | tf_op jit(solution)/shard_map/ppermute | solution.py:243
  94.0 5.0 %collective-permute-start.16 = (bf16[2,4,8,512]{3,2,1,0:T(8,128)(2,1)S(1)}, bf16[2,4,8,512]{3,2,1,0:T(8,128)(2,1)S(1)}, u32[]{:S(2)}, u32[]{:S(2)}) collective-permute-start(bf16[2,4,8,512]{3,2,1,0:T(8,128)(2,1)S(1)} %get-tuple-element.42), channel_id=1, source_target_pairs={{0,208},{16,192},{64,144},{80,128},{128,80},{144,64},{192,16},{208... | collective-permute-start | bytes 196616 | tf_op jit(solution)/shard_map/ppermute | solution.py:243
  101.0 2.5 %collective-permute-start.18 = (bf16[2,2,4,8,512]{4,3,2,1,0:T(8,128)(2,1)S(1)}, bf16[2,2,4,8,512]{4,3,2,1,0:T(8,128)(2,1)S(1)}, u32[]{:S(2)}, u32[]{:S(2)}) collective-permute-start(bf16[2,2,4,8,512]{4,3,2,1,0:T(8,128)(2,1)S(1)} %pad_maximum_fusion.4), channel_id=1, source_target_pairs={{0,56},{8,48},{16,40},{24,32},{32,24},{40,16},{48,8},{56,0},{1,57}... | collective-permute-start | bytes 393224 | tf_op jit(solution)/shard_map/ppermute | solution.py:243
  103.9 4.8 %collective-permute-done.17 = bf16[2,2,4,8,512]{4,3,2,1,0:T(8,128)(2,1)S(1)} collective-permute-done((bf16[2,2,4,8,512]{4,3,2,1,0:T(8,128)(2,1)S(1)}, bf16[2,2,4,8,512]{4,3,2,1,0:T(8,128)(2,1)S(1)}, u32[]{:S(2)}, u32[]{:S(2)}) %collective-permute-start.17) | collective-permute-done | bytes 131104 | tf_op jit(solution)/shard_map/ppermute | solution.py:243
  109.1 2.2 %shard_map.54 = (f32[4,256,512]{2,1,0:T(8,128)}, f32[1,1]{1,0:T(1,128)}) custom-call(s32[6]{0:T(128)S(1)} %stack.62.where_ref, bf16[8,2,4,8,512]{4,3,2,1,0:T(8,128)(2,1)S(1)} %constant_dynamic-update-slice_fusion.piece_ref, f32[8,512]{1,0:T(8,128)S(1)} %slice_bitcast_fusion.1.parts_ref), custom_call_target="tpu_custom_call" | custom-call | tf_op jit(solution)/shard_map/pallas_call | solution.py:342
  111.4 1.8 %shard_map.55 = f32[4,256,512]{2,1,0:T(8,128)} custom-call(s32[6]{0:T(128)S(1)} %stack.62.where_ref, bf16[8,2,4,8,512]{4,3,2,1,0:T(8,128)(2,1)S(1)} %collective-permute-done.19.piece_ref, f32[4,256,512]{2,1,0:T(8,128)} %get-tuple-element.29.begun_hbm), custom_call_target="tpu_custom_call", output_to_operand_aliasing={{}: (2, {})} | custom-call | tf_op jit(solution)/shard_map/pallas_call | solution.py:345
  (66 shorter events, 16.3 us)
Async XLA Ops:
  0.6 14.6 %copy-start = (bf16[4,256,512]{2,1,0:T(8,128)(2,1)S(1)}, bf16[4,256,512]{2,1,0:T(8,128)(2,1)}, u32[]{:S(2)}) copy-start(bf16[4,256,512]{2,1,0:T(8,128)(2,1)} %param.4) | copy-start | bytes 3145732
  3.5 20.6 %all-to-all-start = ((bf16[16,24,128]{2,1,0:T(8,128)(2,1)}), bf16[16,24,128]{2,1,0:T(8,128)(2,1)S(1)}, u32[]{:S(2)}, u32[]{:S(2)}) async-start(bf16[16,24,128]{2,1,0:T(8,128)(2,1)} %broadcast_in_dim.36), calls=%async_computation | async-start | bytes 196608 | tf_op jit(solution)/shard_map/all_to_all | solution.py:272
  28.1 3.3 %collective-permute-start = (f32[2,288,128]{2,1,0:T(8,128)S(1)}, f32[2,288,128]{2,1,0:T(8,128)S(1)}, u32[]{:S(2)}, u32[]{:S(2)}) collective-permute-start(f32[2,288,128]{2,1,0:T(8,128)S(1)} %get-tuple-element.19), channel_id=1, source_target_pairs={{0,16},{16,0},{1,17},{17,1},{2,18},{18,2},{3,19},{19,3},{4,20},{20... | collective-permute-start | bytes 884744 | tf_op jit(solution)/shard_map/ppermute | solution.py:243
  31.5 4.3 %collective-permute-start.1 = (bf16[288,128]{1,0:T(8,128)(2,1)S(1)}, bf16[288,128]{1,0:T(8,128)(2,1)S(1)}, u32[]{:S(2)}, u32[]{:S(2)}) collective-permute-start(bf16[288,128]{1,0:T(8,128)(2,1)S(1)} %fusion.3), channel_id=1, source_target_pairs={{0,48},{16,32},{32,16},{48,0},{1,49},{17,33},{33,17},{49,1},{2,50}... | collective-permute-start | bytes 221192 | tf_op jit(solution)/shard_map/ppermute | solution.py:243
  35.8 4.5 %collective-permute-start.2 = (bf16[288,128]{1,0:T(8,128)(2,1)S(1)}, bf16[288,128]{1,0:T(8,128)(2,1)S(1)}, u32[]{:S(2)}, u32[]{:S(2)}) collective-permute-start(bf16[288,128]{1,0:T(8,128)(2,1)S(1)} %fusion.1), channel_id=1, source_target_pairs={{0,80},{16,64},{64,16},{80,0},{128,208},{144,192},{192,144},{208,1... | collective-permute-start | bytes 221192 | tf_op jit(solution)/shard_map/ppermute | solution.py:243
  37.5 6.7 %collective-permute-start.3 = (bf16[288,128]{1,0:T(8,128)(2,1)S(1)}, bf16[288,128]{1,0:T(8,128)(2,1)S(1)}, u32[]{:S(2)}, u32[]{:S(2)}) collective-permute-start(bf16[288,128]{1,0:T(8,128)(2,1)S(1)} %fusion.1), channel_id=1, source_target_pairs={{0,128},{16,144},{64,192},{80,208},{128,0},{144,16},{192,64},{208,... | collective-permute-start | bytes 221192 | tf_op jit(solution)/shard_map/ppermute | solution.py:243
  40.1 5.9 %collective-permute-start.4 = (bf16[288,128]{1,0:T(8,128)(2,1)S(1)}, bf16[288,128]{1,0:T(8,128)(2,1)S(1)}, u32[]{:S(2)}, u32[]{:S(2)}) collective-permute-start(bf16[288,128]{1,0:T(8,128)(2,1)S(1)} %fusion.1), channel_id=1, source_target_pairs={{0,208},{16,192},{64,144},{80,128},{128,80},{144,64},{192,16},{208... | collective-permute-start | bytes 221192 | tf_op jit(solution)/shard_map/ppermute | solution.py:243
  46.1 4.4 %collective-permute-start.5 = (bf16[288,128]{1,0:T(8,128)(2,1)S(1)}, bf16[288,128]{1,0:T(8,128)(2,1)S(1)}, u32[]{:S(2)}, u32[]{:S(2)}) collective-permute-start(bf16[288,128]{1,0:T(8,128)(2,1)S(1)} %add_convert_fusion), channel_id=1, source_target_pairs={{0,48},{16,32},{32,16},{48,0},{1,49},{17,33},{33,17},{49,1},{2,50}... | collective-permute-start | bytes 221192 | tf_op jit(solution)/shard_map/ppermute | solution.py:243
  50.4 1.5 %collective-permute-start.6 = (bf16[2,288,128]{2,1,0:T(8,128)(2,1)S(1)}, bf16[2,288,128]{2,1,0:T(8,128)(2,1)S(1)}, u32[]{:S(2)}, u32[]{:S(2)}) collective-permute-start(bf16[2,288,128]{2,1,0:T(8,128)(2,1)S(1)} %pad_maximum_fusion.1), channel_id=1, source_target_pairs={{0,16},{16,0},{1,17},{17,1},{2,18},{18,2},{3,19},{19,3},{4,20},{20... | collective-permute-start | bytes 442376 | tf_op jit(solution)/shard_map/ppermute | solution.py:243
  56.3 2.2 %collective-permute-start.7 = (f32[33,8,512]{2,1,0:T(8,128)S(1)}, f32[33,8,512]{2,1,0:T(8,128)S(1)}, u32[]{:S(2)}, u32[]{:S(2)}) collective-permute-start(f32[33,8,512]{2,1,0:T(8,128)S(1)} %get-tuple-element.24), channel_id=1, source_target_pairs={{0,16},{16,0},{1,17},{17,1},{2,18},{18,2},{3,19},{19,3},{4,20},{20... | collective-permute-start | bytes 1622024 | tf_op jit(solution)/shard_map/ppermute | solution.py:243
  58.7 5.7 %collective-permute-start.8 = (bf16[17,8,512]{2,1,0:T(8,128)(2,1)S(1)}, bf16[17,8,512]{2,1,0:T(8,128)(2,1)S(1)}, u32[]{:S(2)}, u32[]{:S(2)}) collective-permute-start(bf16[17,8,512]{2,1,0:T(8,128)(2,1)S(1)} %pad_maximum_fusion.2), channel_id=1, source_target_pairs={{0,48},{16,32},{32,16},{48,0},{1,49},{17,33},{33,17},{49,1},{2,50}... | collective-permute-start | bytes 417800 | tf_op jit(solution)/shard_map/ppermute | solution.py:243
  64.5 6.7 %collective-permute-start.10 = (bf16[6,8,512]{2,1,0:T(8,128)(2,1)S(1)}, bf16[6,8,512]{2,1,0:T(8,128)(2,1)S(1)}, u32[]{:S(2)}, u32[]{:S(2)}) collective-permute-start(bf16[6,8,512]{2,1,0:T(8,128)(2,1)S(1)} %pad_maximum_fusion.6), channel_id=1, source_target_pairs={{0,128},{16,144},{64,192},{80,208},{128,0},{144,16},{192,64},{208,... | collective-permute-start | bytes 147464 | tf_op jit(solution)/shard_map/ppermute | solution.py:243
  65.0 4.2 %collective-permute-start.9 = (bf16[5,8,512]{2,1,0:T(8,128)(2,1)S(1)}, bf16[5,8,512]{2,1,0:T(8,128)(2,1)S(1)}, u32[]{:S(2)}, u32[]{:S(2)}) collective-permute-start(bf16[5,8,512]{2,1,0:T(8,128)(2,1)S(1)} %pad_maximum_fusion.7), channel_id=1, source_target_pairs={{0,80},{16,64},{64,16},{80,0},{128,208},{144,192},{192,144},{208,1... | collective-permute-start | bytes 122888 | tf_op jit(solution)/shard_map/ppermute | solution.py:243
  66.5 4.6 %collective-permute-start.11 = (bf16[5,8,512]{2,1,0:T(8,128)(2,1)S(1)}, bf16[5,8,512]{2,1,0:T(8,128)(2,1)S(1)}, u32[]{:S(2)}, u32[]{:S(2)}) collective-permute-start(bf16[5,8,512]{2,1,0:T(8,128)(2,1)S(1)} %pad_maximum_fusion.8), channel_id=1, source_target_pairs={{0,208},{16,192},{64,144},{80,128},{128,80},{144,64},{192,16},{208... | collective-permute-start | bytes 122888 | tf_op jit(solution)/shard_map/ppermute | solution.py:243
  71.2 2.9 %collective-permute-start.12 = (bf16[5,8,512]{2,1,0:T(8,128)(2,1)S(1)}, bf16[5,8,512]{2,1,0:T(8,128)(2,1)S(1)}, u32[]{:S(2)}, u32[]{:S(2)}) collective-permute-start(bf16[5,8,512]{2,1,0:T(8,128)(2,1)S(1)} %pad_maximum_fusion.9), channel_id=1, source_target_pairs={{0,1},{1,0},{2,3},{3,2},{4,5},{5,4},{6,7},{7,6},{8,9},{9,8},{10,11... | collective-permute-start | bytes 122888 | tf_op jit(solution)/shard_map/ppermute | solution.py:243
  89.4 3.8 %collective-permute-start.13 = (bf16[4,8,512]{2,1,0:T(8,128)(2,1)S(1)}, bf16[4,8,512]{2,1,0:T(8,128)(2,1)S(1)}, u32[]{:S(2)}, u32[]{:S(2)}) collective-permute-start(bf16[4,8,512]{2,1,0:T(8,128)(2,1)S(1)} %slice.205), channel_id=1, source_target_pairs={{0,1},{1,0},{2,3},{3,2},{4,5},{5,4},{6,7},{7,6},{8,9},{9,8},{10,11... | collective-permute-start | bytes 98312 | tf_op jit(solution)/shard_map/ppermute | solution.py:243
  93.2 6.6 %collective-permute-start.15 = (bf16[2,4,8,512]{3,2,1,0:T(8,128)(2,1)S(1)}, bf16[2,4,8,512]{3,2,1,0:T(8,128)(2,1)S(1)}, u32[]{:S(2)}, u32[]{:S(2)}) collective-permute-start(bf16[2,4,8,512]{3,2,1,0:T(8,128)(2,1)S(1)} %get-tuple-element.42), channel_id=1, source_target_pairs={{0,128},{16,144},{64,192},{80,208},{128,0},{144,16},{192,64},{208,... | collective-permute-start | bytes 196616 | tf_op jit(solution)/shard_map/ppermute | solution.py:243
  94.0 7.0 %collective-permute-start.16 = (bf16[2,4,8,512]{3,2,1,0:T(8,128)(2,1)S(1)}, bf16[2,4,8,512]{3,2,1,0:T(8,128)(2,1)S(1)}, u32[]{:S(2)}, u32[]{:S(2)}) collective-permute-start(bf16[2,4,8,512]{3,2,1,0:T(8,128)(2,1)S(1)} %get-tuple-element.42), channel_id=1, source_target_pairs={{0,208},{16,192},{64,144},{80,128},{128,80},{144,64},{192,16},{208... | collective-permute-start | bytes 196616 | tf_op jit(solution)/shard_map/ppermute | solution.py:243
  99.0 4.4 %collective-permute-start.14 = (bf16[2,4,8,512]{3,2,1,0:T(8,128)(2,1)S(1)}, bf16[2,4,8,512]{3,2,1,0:T(8,128)(2,1)S(1)}, u32[]{:S(2)}, u32[]{:S(2)}) collective-permute-start(bf16[2,4,8,512]{3,2,1,0:T(8,128)(2,1)S(1)} %get-tuple-element.42), channel_id=1, source_target_pairs={{0,80},{16,64},{64,16},{80,0},{128,208},{144,192},{192,144},{208,1... | collective-permute-start | bytes 196616 | tf_op jit(solution)/shard_map/ppermute | solution.py:243
  101.0 7.7 %collective-permute-start.18 = (bf16[2,2,4,8,512]{4,3,2,1,0:T(8,128)(2,1)S(1)}, bf16[2,2,4,8,512]{4,3,2,1,0:T(8,128)(2,1)S(1)}, u32[]{:S(2)}, u32[]{:S(2)}) collective-permute-start(bf16[2,2,4,8,512]{4,3,2,1,0:T(8,128)(2,1)S(1)} %pad_maximum_fusion.4), channel_id=1, source_target_pairs={{0,56},{8,48},{16,40},{24,32},{32,24},{40,16},{48,8},{56,0},{1,57}... | collective-permute-start | bytes 393224 | tf_op jit(solution)/shard_map/ppermute | solution.py:243
  103.5 5.2 %collective-permute-start.17 = (bf16[2,2,4,8,512]{4,3,2,1,0:T(8,128)(2,1)S(1)}, bf16[2,2,4,8,512]{4,3,2,1,0:T(8,128)(2,1)S(1)}, u32[]{:S(2)}, u32[]{:S(2)}) collective-permute-start(bf16[2,2,4,8,512]{4,3,2,1,0:T(8,128)(2,1)S(1)} %pad_maximum_fusion.3), channel_id=1, source_target_pairs={{0,48},{16,32},{32,16},{48,0},{1,49},{17,33},{33,17},{49,1},{2,50}... | collective-permute-start | bytes 393224 | tf_op jit(solution)/shard_map/ppermute | solution.py:243
  108.7 2.6 %collective-permute-start.19 = (bf16[8,2,4,8,512]{4,3,2,1,0:T(8,128)(2,1)S(1)}, bf16[8,2,4,8,512]{4,3,2,1,0:T(8,128)(2,1)S(1)}, u32[]{:S(2)}, u32[]{:S(2)}) collective-permute-start(bf16[8,2,4,8,512]{4,3,2,1,0:T(8,128)(2,1)S(1)} %constant_dynamic-update-slice_fusion.piece_ref), channel_id=1, source_target_pairs={{0,16},{16,0},{1,17},{17,1},{2,18},{18,2},{3,19},{19,3},{4,20},{20... | collective-permute-start | bytes 1572872 | tf_op jit(solution)/shard_map/ppermute | solution.py:243

commit v3 on v2

--- a/solution.py
+++ b/solution.py
@@ -123,7 +123,7 @@
             store(send_ref, to - 2)
 
 
-def grad_kernel(where_ref, packed_ref, whole_ref, student_ref, tnorm_ref, inv_ref, keep_ref, send_ref, near_ref, other_ref, loss_ref, cross, gram, packed):
+def grad_kernel(where_ref, packed_ref, whole_ref, student_ref, tnorm_ref, inv_ref, keep_ref, send_ref, near_ref, other_ref, loss_ref, cross, gram, packed, grads, onehots):
     packed[...] = packed_ref[...].astype(F32)
     item, feat, me = where_ref[0], where_ref[1], where_ref[2]
     place, zb, half = where_ref[3], where_ref[4], where_ref[5]
@@ -144,7 +144,6 @@
     loss_ref[...] = jnp.where(lane == feat, parts, 0.0)
     gram_t = gram_f.T.astype(BF16)
     per = CHUNK // 128
-    total = jnp.zeros((ROWS, DS), F32)
     large = lax.broadcasted_iota(jnp.int32, (512, CHUNK), 0)
     small = lax.broadcasted_iota(jnp.int32, (64, CHUNK), 0) + 512
     for n in range(2048 // CHUNK):
@@ -155,7 +154,7 @@
         value = push - pull
         student = student_ref[:, span].astype(F32)
         mean = jnp.sum(value * student, axis=0, keepdims=True) / DS
-        grad = ((value - student * mean) * (inv_ref[:, span] / 32768.0)).astype(BF16)
+        grads[:, span] = ((value - student * mean) * (inv_ref[:, span] / 32768.0)).astype(BF16)
 
         def spot(code, level):
             low = code & 15
@@ -172,14 +171,9 @@
         )
         third = spot(codes_of(packed, 2, n * per, per), 0)
         fourth = spot(codes_of(packed, 3, n * per, per), 1)
-        onehot = jnp.concatenate(
-            [
-                ((large == third) | (large == fourth)).astype(F32),
-                ((small == first) | (small == second)).astype(F32),
-            ],
-            axis=0,
-        ).astype(BF16)
-        total = total + lax.dot_general(onehot, grad, NT, preferred_element_type=F32)
+        onehots[0:512, span] = ((large == third) | (large == fourth)).astype(F32).astype(BF16)
+        onehots[512:576, span] = ((small == first) | (small == second)).astype(F32).astype(BF16)
+    total = lax.dot_general(onehots[...], grads[...], NT, preferred_element_type=F32)
     keep_ref[...] = total[0:256].reshape(keep_ref.shape)
     send_ref[0:32] = total[256:512].reshape(32, 8, DS)
     send_ref[32] = total[560:568]
@@ -187,20 +181,10 @@
     other_ref[...] = total[544:560].reshape(other_ref.shape).astype(BF16)
 
 
-def spread_half(c, where_ref, piece_ref, out_hbm, rows, sems):
+def spread(c, x, where_ref, piece_ref, out_hbm, rows, sems):
     place, zb = where_ref[3], where_ref[4]
-    kept = c ^ (place >> 3)
-    for x in range(2):
-        for y in range(4):
-            at = (x * 4 + y) ^ (place & 7)
-            ay, axl = at & 3, at >> 2
-            row0 = (ay * 2 + axl) * 16
-            row1 = ((ay & 1) * 2 + axl) * 32 + (ay >> 1) * 16
-            row2 = at * 16
-            for z in range(2):
-                shift = (z ^ zb) * 8
-                for k, (level, row) in enumerate(((2, row2), (3, row2), (0, row0), (1, row1))):
-                    rows[level, pl.ds(pl.multiple_of(row + shift, 8), 8), :] = piece_ref[x * 4 + y, z, k].astype(F32)
+    base = (c * 8 + x * 4) ^ (place & 12)
+    kept, axl = base >> 3, (base >> 2) & 1
     copies = []
 
     def copy(level, start, count, to):
@@ -208,23 +192,38 @@
         copies.append(pltpu.make_async_copy(rows.at[level, pl.ds(start, count)], target, sems.at[len(copies)]))
         copies[-1].start()
 
-    copy(2, 0, 128, kept * 128)
-    copy(3, 0, 128, kept * 128)
-    for j in range(8):
-        copy(0, j * 16, 16, (j * 2 + (kept ^ (j & 1) ^ ((j >> 1) & 1))) * 16)
-    for j in range(4):
-        copy(1, j * 32, 32, (j * 2 + (kept ^ (j & 1) ^ (j >> 1))) * 32)
+    for k, level in enumerate((2, 3, 0, 1)):
+        for y in range(4):
+            ay = y ^ (place & 3)
+            row = (ay & 1) * 32 + (ay >> 1) * 16 if level == 1 else ay * 16
+            for z in range(2):
+                at = pl.multiple_of(row + (z ^ zb) * 8, 8)
+                rows[level, pl.ds(at, 8), :] = piece_ref[y, z, k].astype(F32)
+        if level == 0:
+            for j in range(4):
+                copy(0, j * 16, 16, (j * 4 + axl * 2 + (kept ^ axl ^ (j & 1))) * 16)
+        elif level == 1:
+            for j in range(2):
+                copy(1, j * 32, 32, (j * 4 + axl * 2 + (kept ^ axl ^ j)) * 32)
+        else:
+            copy(level, 0, 64, base * 16)
     for one in copies:
         one.wait()
 
 
-def near_kernel(where_ref, piece_ref, parts_ref, out_hbm, loss_ref, rows, sems):
+def first_kernel(where_ref, piece_ref, parts_ref, out_hbm, loss_ref, rows, sems):
     loss_ref[...] = jnp.sum(parts_ref[...], keepdims=True) / (32768.0 * 32768.0 * DS)
-    spread_half(0, where_ref, piece_ref, out_hbm, rows, sems)
-
-
-def far_kernel(where_ref, piece_ref, begun_hbm, out_hbm, rows, sems):
-    spread_half(1, where_ref, piece_ref, out_hbm, rows, sems)
+    spread(0, 0, where_ref, piece_ref, out_hbm, rows, sems)
+
+
+def next_kernel(c, x):
+    def kernel(where_ref, piece_ref, begun_hbm, out_hbm, *refs):
+        *token, rows, sems = refs
+        if token:
+            token[0][...] = jnp.zeros((8, DS), BF16)
+        spread(c, x, where_ref, piece_ref, out_hbm, rows, sems)
+
+    return kernel
 
 
 def call(kernel, ins, outs, scratch=(), aliases=None):
@@ -303,7 +302,13 @@
             ((2, 8, DS), BF16, VMEM),
             ((8, DS), F32, VMEM),
         ],
-        [pltpu.VMEM((DS, 256), BF16), pltpu.VMEM((32, DS), BF16), pltpu.VMEM((16, 24, 128), F32)],
+        [
+            pltpu.VMEM((DS, 256), BF16),
+            pltpu.VMEM((32, DS), BF16),
+            pltpu.VMEM((16, 24, 128), F32),
+            pltpu.VMEM((DS, 2048), BF16),
+            pltpu.VMEM((ROWS, 2048), BF16),
+        ],
     )(where, packed, whole, student, tnorm, inv)
 
     got = swap(send, "c", 2, 1)
@@ -328,21 +333,25 @@
         return jnp.concatenate([sums[2 * z : 2 * z + 2], zero[None], first[None], loss[None]])
 
     rows = rows_of(0) + swap(rows_of(1).astype(BF16), "zb", 2, 1).astype(F32)
-    sent = jnp.broadcast_to(rows.astype(BF16)[None], (8, 5, 8, DS))
-    got = lax.all_to_all(sent, ("xh", "za"), 0, 0, tiled=True)
-    rows = jnp.sum(got.astype(F32), axis=0)
+    own = (rows + swap(rows, "xh", 2, 1)).astype(BF16)
+    a, b, d = (swap(own, "za", 4, k).astype(F32) for k in (1, 2, 3))
+    rows = (own.astype(F32) + a) + (b + d)
     loss = rows[4]
     rows = rows[:4].astype(BF16)
 
     rows = jnp.stack([rows, swap(rows, "zb", 2, 1)])
     rows = jnp.stack([rows] + [across_y(rows, k) for k in (1, 2, 3)])
-    rows = jnp.concatenate([rows, across_x(rows[:2]), swap(rows[2:], ("xl", "c", "xh"), 8, 7)])
+    parts = across_x(rows[:2]), swap(rows[2:], ("xl", "c", "xh"), 8, 7)
     far = swap(rows, "c", 2, 1)
-    rows_and_sems = [pltpu.VMEM((4, 128, DS), F32), pltpu.SemaphoreType.DMA((14,))]
-    grads, loss = call(
-        near_kernel, [SMEM, VMEM, VMEM], [((4, 256, DS), F32, ANY), ((1, 1), F32, VMEM)], rows_and_sems
-    )(where, rows, loss)
-    (grads,) = call(far_kernel, [SMEM, VMEM, ANY], [((4, 256, DS), F32, ANY)], rows_and_sems, {2: 0})(where, far, grads)
+    rows_and_sems = [pltpu.VMEM((4, 64, DS), F32), pltpu.SemaphoreType.DMA((8,))]
+    out = ((4, 256, DS), F32, ANY)
+    outs = [out, ((8, DS), BF16, VMEM)]
+    grads, loss = call(first_kernel, [SMEM, VMEM, VMEM], [out, ((1, 1), F32, VMEM)], rows_and_sems)(where, rows, loss)
+    grads, token = call(next_kernel(1, 0), [SMEM, VMEM, ANY], outs, rows_and_sems, {2: 0})(where, far, grads)
+    beside = jnp.concatenate([part + token for part in parts])
+    far_beside = swap(beside, "c", 2, 1)
+    for c, piece in ((0, beside), (1, far_beside)):
+        (grads,) = call(next_kernel(c, 1), [SMEM, VMEM, ANY], [out], rows_and_sems, {2: 0})(where, piece, grads)
     return (loss.reshape(()), grads)
 
 

time: 114 us -> 112 us (0.982)
  blocking collectives: 15.1 us -> 0 us
  waiting for transfers between devices: 42.2 us -> 49.7 us
  starting transfers between devices: 38.1 us -> 42.3 us
  Pallas kernels: 15.4 us -> 17.1 us
    all_to_all x1 -> x0, blocking collectives: 15.1 us -> none  [on_device(): got = lax.all_to_all(sent, ('xh', 'za'), 0, 0, tiled=True)]
    ppermute x20 -> x25, waiting for transfers between devices: 34.1 us -> 41.6 us  [swap(): return lax.ppermute(array, axis, [(j, j ^ bit) for j in range(size)])]
    ppermute x20 -> x25, starting transfers between devices: 26.6 us -> 30.7 us  [swap(): return lax.ppermute(array, axis, [(j, j ^ bit) for j in range(size)])]
    pallas_call x2 -> x4, Pallas kernels: 3.98 us -> 6.19 us  [the longest x2 2.85 us: on_device(): call(next_kernel(c, 1), [SMEM, VMEM, ANY], [out], rows_and_sems, {2: 0})]
  transfers between devices with their start and end apart: 21 -> 26, of which waited for: 15 -> 19; matrix products, arithmetic and copies ran while one was open for 0% -> 0% of each run, Pallas kernels for 3% -> 5%
where the time goes in v3:
time: 112 us
  waiting for transfers between devices  49.7 us (44%)
  starting transfers between devices  42.3 us (38%)
  Pallas kernels  17.1 us (15%)
    ppermute x25, waiting for transfers between devices, swap(): return lax.ppermute(array, axis, [(j, j ^ bit) for j in range(size)])  41.6 us
    ppermute x25, starting transfers between devices, swap(): return lax.ppermute(array, axis, [(j, j ^ bit) for j in range(size)])  30.7 us
    all_to_all x1, starting transfers between devices, on_device(): lax.all_to_all(jnp.broadcast_to(packed[None], (16, 24, 128)), FEAT, 0, 0,...  11.6 us
    all_to_all x1, waiting for transfers between devices, on_device(): lax.all_to_all(jnp.broadcast_to(packed[None], (16, 24, 128)), FEAT, 0, 0,...  8.1 us
    pallas_call x1, Pallas kernels, on_device(): call(cross_kernel, [SMEM, VMEM, VMEM, VMEM], [((2, 288, 128), F32, VMEM),...  4.04 us
    pallas_call x1, Pallas kernels, on_device(): call(grad_kernel, [SMEM] + [VMEM] * 5, [((32, 8, DS), F32, VMEM), ((33, 8...  3.91 us
    pallas_call x2, Pallas kernels, on_device(): call(next_kernel(c, 1), [SMEM, VMEM, ANY], [out], rows_and_sems, {2: 0})  2.85 us
  transfers between devices with their start and end apart: 26, of which 19 were waited for; matrix products, arithmetic and copies ran while one was open for 0% of the time, Pallas kernels for 5%

profile of v3, /device:TPU:1, one launch (start us, length us, event | category | flops | bytes accessed | tf_op | source)
XLA Modules:
  0.0 111.6 jit_solution(7585066747775156275)
XLA Ops:
  0.6 2.2 %shard_map.50 = (bf16[2048,256]{1,0:T(8,128)(2,1)S(1)}, bf16[24,128]{1,0:T(8,128)(2,1)S(1)}) custom-call(bf16[2048,256]{1,0:T(8,128)(2,1)} %teacher_hbm.1, s32[4,128]{1,0:T(4,128)} %bitcast.56), custom_call_target="tpu_custom_call" | custom-call | tf_op jit(solution)/shard_map/pallas_call | solution.py:265
  3.5 11.6 %all-to-all-start = ((bf16[16,24,128]{2,1,0:T(8,128)(2,1)}), bf16[16,24,128]{2,1,0:T(8,128)(2,1)S(1)}, u32[]{:S(2)}, u32[]{:S(2)}) async-start(bf16[16,24,128]{2,1,0:T(8,128)(2,1)} %broadcast_in_dim.32), calls=%async_computation | async-start | bytes 196608 | tf_op jit(solution)/shard_map/all_to_all | solution.py:271
  16.0 8.1 %all-to-all-done.packed_ref = bf16[16,24,128]{2,1,0:T(8,128)(2,1)S(1)} async-done(((bf16[16,24,128]{2,1,0:T(8,128)(2,1)}), bf16[16,24,128]{2,1,0:T(8,128)(2,1)S(1)}, u32[]{:S(2)}, u32[]{:S(2)}) %all-to-all-start) | async-done | bytes 98336 | tf_op jit(solution)/shard_map/all_to_all | solution.py:271
  24.1 4.0 %shard_map.52 = (f32[2,288,128]{2,1,0:T(8,128)S(1)}, f32[2,288,128]{2,1,0:T(8,128)S(1)}, bf16[512,2048]{1,0:T(8,128)(2,1)S(1)}, bf16[2048,256]{1,0:T(8,128)(2,1)S(1)}, f32[1,2048]{1,0:T(1,128)S(1)}) custom-call(s32[6]{0:T(128)S(1)} %stack.64.where_ref, bf16[16,24,128]{2,1,0:T(8,128)(2,1)S(1)} %all-to-all-done.packed_ref, ...), custom_call_target="tpu_custom_call" | custom-call | tf_op jit(solution)/shard_map/pallas_call | solution.py:274
  28.1 2.1 %collective-permute-start = (f32[2,288,128]{2,1,0:T(8,128)S(1)}, f32[2,288,128]{2,1,0:T(8,128)S(1)}, u32[]{:S(2)}, u32[]{:S(2)}) collective-permute-start(f32[2,288,128]{2,1,0:T(8,128)S(1)} %get-tuple-element.21), channel_id=1, source_target_pairs={{0,16},{16,0},{1,17},{17,1},{2,18},{18,2},{3,19},{19,3},{4,20},{20... | collective-permute-start | bytes 884744 | tf_op jit(solution)/shard_map/ppermute | solution.py:242
  32.2 3.7 %collective-permute-done.1 = bf16[288,128]{1,0:T(8,128)(2,1)S(1)} collective-permute-done((bf16[288,128]{1,0:T(8,128)(2,1)S(1)}, bf16[288,128]{1,0:T(8,128)(2,1)S(1)}, u32[]{:S(2)}, u32[]{:S(2)}) %collective-permute-start.1) | collective-permute-done | bytes 73760 | tf_op jit(solution)/shard_map/ppermute | solution.py:242
  37.5 2.6 %collective-permute-start.3 = (bf16[288,128]{1,0:T(8,128)(2,1)S(1)}, bf16[288,128]{1,0:T(8,128)(2,1)S(1)}, u32[]{:S(2)}, u32[]{:S(2)}) collective-permute-start(bf16[288,128]{1,0:T(8,128)(2,1)S(1)} %fusion.1), channel_id=1, source_target_pairs={{0,128},{16,144},{64,192},{80,208},{128,0},{144,16},{192,64},{208,... | collective-permute-start | bytes 221192 | tf_op jit(solution)/shard_map/ppermute | solution.py:242
  40.4 3.8 %collective-permute-done.3 = bf16[288,128]{1,0:T(8,128)(2,1)S(1)} collective-permute-done((bf16[288,128]{1,0:T(8,128)(2,1)S(1)}, bf16[288,128]{1,0:T(8,128)(2,1)S(1)}, u32[]{:S(2)}, u32[]{:S(2)}) %collective-permute-start.3) | collective-permute-done | bytes 73760 | tf_op jit(solution)/shard_map/ppermute | solution.py:242
  44.2 1.8 %collective-permute-done.4 = bf16[288,128]{1,0:T(8,128)(2,1)S(1)} collective-permute-done((bf16[288,128]{1,0:T(8,128)(2,1)S(1)}, bf16[288,128]{1,0:T(8,128)(2,1)S(1)}, u32[]{:S(2)}, u32[]{:S(2)}) %collective-permute-start.4) | collective-permute-done | bytes 73760 | tf_op jit(solution)/shard_map/ppermute | solution.py:242
  46.7 3.7 %collective-permute-done.5 = bf16[288,128]{1,0:T(8,128)(2,1)S(1)} collective-permute-done((bf16[288,128]{1,0:T(8,128)(2,1)S(1)}, bf16[288,128]{1,0:T(8,128)(2,1)S(1)}, u32[]{:S(2)}, u32[]{:S(2)}) %collective-permute-start.5) | collective-permute-done | bytes 73760 | tf_op jit(solution)/shard_map/ppermute | solution.py:242
  52.0 3.9 %shard_map.53 = (f32[32,8,512]{2,1,0:T(8,128)S(1)}, f32[33,8,512]{2,1,0:T(8,128)S(1)}, f32[2,2,8,512]{3,2,1,0:T(8,128)S(1)}, bf16[2,8,512]{2,1,0:T(8,128)(2,1)S(1)}, f32[8,512]{1,0:T(8,128)S(1)}) custom-call(s32[6]{0:T(128)S(1)} %stack.64.where_ref, bf16[16,24,128]{2,1,0:T(8,128)(2,1)S(1)} %all-to-all-done.packed_ref, ...), custom_call_target="tpu_custom_call" | custom-call | tf_op jit(solution)/shard_map/pallas_call | solution.py:295
  58.9 5.1 %collective-permute-done.8 = bf16[17,8,512]{2,1,0:T(8,128)(2,1)S(1)} collective-permute-done((bf16[17,8,512]{2,1,0:T(8,128)(2,1)S(1)}, bf16[17,8,512]{2,1,0:T(8,128)(2,1)S(1)}, u32[]{:S(2)}, u32[]{:S(2)}) %collective-permute-start.8) | collective-permute-done | bytes 139296 | tf_op jit(solution)/shard_map/ppermute | solution.py:242
  66.1 1.7 %collective-permute-start.11 = (bf16[5,8,512]{2,1,0:T(8,128)(2,1)S(1)}, bf16[5,8,512]{2,1,0:T(8,128)(2,1)S(1)}, u32[]{:S(2)}, u32[]{:S(2)}) collective-permute-start(bf16[5,8,512]{2,1,0:T(8,128)(2,1)S(1)} %pad_maximum_fusion.10), channel_id=1, source_target_pairs={{0,208},{16,192},{64,144},{80,128},{128,80},{144,64},{192,16},{208... | collective-permute-start | bytes 122888 | tf_op jit(solution)/shard_map/ppermute | solution.py:242
  68.7 2.0 %collective-permute-done.11 = bf16[5,8,512]{2,1,0:T(8,128)(2,1)S(1)} collective-permute-done((bf16[5,8,512]{2,1,0:T(8,128)(2,1)S(1)}, bf16[5,8,512]{2,1,0:T(8,128)(2,1)S(1)}, u32[]{:S(2)}, u32[]{:S(2)}) %collective-permute-start.11) | collective-permute-done | bytes 40992 | tf_op jit(solution)/shard_map/ppermute | solution.py:242
  71.7 2.1 %collective-permute-done.12 = bf16[5,8,512]{2,1,0:T(8,128)(2,1)S(1)} collective-permute-done((bf16[5,8,512]{2,1,0:T(8,128)(2,1)S(1)}, bf16[5,8,512]{2,1,0:T(8,128)(2,1)S(1)}, u32[]{:S(2)}, u32[]{:S(2)}) %collective-permute-start.12) | collective-permute-done | bytes 40992 | tf_op jit(solution)/shard_map/ppermute | solution.py:242
  74.4 4.3 %collective-permute-done.13 = f32[5,8,512]{2,1,0:T(8,128)S(1)} collective-permute-done((f32[5,8,512]{2,1,0:T(8,128)S(1)}, f32[5,8,512]{2,1,0:T(8,128)S(1)}, u32[]{:S(2)}, u32[]{:S(2)}) %collective-permute-start.13) | collective-permute-done | bytes 81952 | tf_op jit(solution)/shard_map/ppermute | solution.py:242
  79.7 2.1 %collective-permute-start.15 = (bf16[5,8,512]{2,1,0:T(8,128)(2,1)S(1)}, bf16[5,8,512]{2,1,0:T(8,128)(2,1)S(1)}, u32[]{:S(2)}, u32[]{:S(2)}) collective-permute-start(bf16[5,8,512]{2,1,0:T(8,128)(2,1)S(1)} %add_convert_fusion.1), channel_id=1, source_target_pairs={{0,4},{2,6},{4,0},{6,2},{1,5},{3,7},{5,1},{7,3},{8,12},{10,14},{12... | collective-permute-start | bytes 122888 | tf_op jit(solution)/shard_map/ppermute | solution.py:242
  81.8 2.6 %collective-permute-start.16 = (bf16[5,8,512]{2,1,0:T(8,128)(2,1)S(1)}, bf16[5,8,512]{2,1,0:T(8,128)(2,1)S(1)}, u32[]{:S(2)}, u32[]{:S(2)}) collective-permute-start(bf16[5,8,512]{2,1,0:T(8,128)(2,1)S(1)} %add_convert_fusion.1), channel_id=1, source_target_pairs={{0,6},{2,4},{4,2},{6,0},{1,7},{3,5},{5,3},{7,1},{8,14},{10,12},{12... | collective-permute-start | bytes 122888 | tf_op jit(solution)/shard_map/ppermute | solution.py:242
  84.4 2.6 %collective-permute-done.15 = bf16[5,8,512]{2,1,0:T(8,128)(2,1)S(1)} collective-permute-done((bf16[5,8,512]{2,1,0:T(8,128)(2,1)S(1)}, bf16[5,8,512]{2,1,0:T(8,128)(2,1)S(1)}, u32[]{:S(2)}, u32[]{:S(2)}) %collective-permute-start.15) | collective-permute-done | bytes 40992 | tf_op jit(solution)/shard_map/ppermute | solution.py:242
  88.7 1.8 %collective-permute-done.17 = bf16[4,8,512]{2,1,0:T(8,128)(2,1)S(1)} collective-permute-done((bf16[4,8,512]{2,1,0:T(8,128)(2,1)S(1)}, bf16[4,8,512]{2,1,0:T(8,128)(2,1)S(1)}, u32[]{:S(2)}, u32[]{:S(2)}) %collective-permute-start.17) | collective-permute-done | bytes 32800 | tf_op jit(solution)/shard_map/ppermute | solution.py:242
  91.5 5.7 %collective-permute-start.20 = (bf16[2,4,8,512]{3,2,1,0:T(8,128)(2,1)S(1)}, bf16[2,4,8,512]{3,2,1,0:T(8,128)(2,1)S(1)}, u32[]{:S(2)}, u32[]{:S(2)}) collective-permute-start(bf16[2,4,8,512]{3,2,1,0:T(8,128)(2,1)S(1)} %get-tuple-element.46), channel_id=1, source_target_pairs={{0,208},{16,192},{64,144},{80,128},{128,80},{144,64},{192,16},{208... | collective-permute-start | bytes 196616 | tf_op jit(solution)/shard_map/ppermute | solution.py:242
  99.2 2.1 %collective-permute-done.18 = bf16[2,4,8,512]{3,2,1,0:T(8,128)(2,1)S(1)} collective-permute-done((bf16[2,4,8,512]{3,2,1,0:T(8,128)(2,1)S(1)}, bf16[2,4,8,512]{3,2,1,0:T(8,128)(2,1)S(1)}, u32[]{:S(2)}, u32[]{:S(2)}) %collective-permute-start.18) | collective-permute-done | bytes 65568 | tf_op jit(solution)/shard_map/ppermute | solution.py:242
  102.5 1.9 %shard_map.54 = (f32[4,256,512]{2,1,0:T(8,128)}, f32[1,1]{1,0:T(1,128)}) custom-call(s32[6]{0:T(128)S(1)} %stack.64.where_ref, bf16[4,2,4,8,512]{4,3,2,1,0:T(8,128)(2,1)S(1)} %pad_maximum_fusion.1.piece_ref, f32[8,512]{1,0:T(8,128)S(1)} %slice_bitcast_fusion.1.parts_ref), custom_call_target="tpu_custom_call" | custom-call | tf_op jit(solution)/shard_map/pallas_call | solution.py:349
  105.8 2.5 %collective-permute-done.23 = bf16[2,2,4,8,512]{4,3,2,1,0:T(8,128)(2,1)S(1)} collective-permute-done((bf16[2,2,4,8,512]{4,3,2,1,0:T(8,128)(2,1)S(1)}, bf16[2,2,4,8,512]{4,3,2,1,0:T(8,128)(2,1)S(1)}, u32[]{:S(2)}, u32[]{:S(2)}) %collective-permute-start.23) | collective-permute-done | bytes 131104 | tf_op jit(solution)/shard_map/ppermute | solution.py:242
  (74 shorter events, 26.6 us)
Async XLA Ops:
  3.5 20.6 %all-to-all-start = ((bf16[16,24,128]{2,1,0:T(8,128)(2,1)}), bf16[16,24,128]{2,1,0:T(8,128)(2,1)S(1)}, u32[]{:S(2)}, u32[]{:S(2)}) async-start(bf16[16,24,128]{2,1,0:T(8,128)(2,1)} %broadcast_in_dim.32), calls=%async_computation | async-start | bytes 196608 | tf_op jit(solution)/shard_map/all_to_all | solution.py:271
  28.1 3.3 %collective-permute-start = (f32[2,288,128]{2,1,0:T(8,128)S(1)}, f32[2,288,128]{2,1,0:T(8,128)S(1)}, u32[]{:S(2)}, u32[]{:S(2)}) collective-permute-start(f32[2,288,128]{2,1,0:T(8,128)S(1)} %get-tuple-element.21), channel_id=1, source_target_pairs={{0,16},{16,0},{1,17},{17,1},{2,18},{18,2},{3,19},{19,3},{4,20},{20... | collective-permute-start | bytes 884744 | tf_op jit(solution)/shard_map/ppermute | solution.py:242
  31.5 4.3 %collective-permute-start.1 = (bf16[288,128]{1,0:T(8,128)(2,1)S(1)}, bf16[288,128]{1,0:T(8,128)(2,1)S(1)}, u32[]{:S(2)}, u32[]{:S(2)}) collective-permute-start(bf16[288,128]{1,0:T(8,128)(2,1)S(1)} %fusion.2), channel_id=1, source_target_pairs={{0,48},{16,32},{32,16},{48,0},{1,49},{17,33},{33,17},{49,1},{2,50}... | collective-permute-start | bytes 221192 | tf_op jit(solution)/shard_map/ppermute | solution.py:242
  35.8 4.5 %collective-permute-start.2 = (bf16[288,128]{1,0:T(8,128)(2,1)S(1)}, bf16[288,128]{1,0:T(8,128)(2,1)S(1)}, u32[]{:S(2)}, u32[]{:S(2)}) collective-permute-start(bf16[288,128]{1,0:T(8,128)(2,1)S(1)} %fusion.1), channel_id=1, source_target_pairs={{0,80},{16,64},{64,16},{80,0},{128,208},{144,192},{192,144},{208,1... | collective-permute-start | bytes 221192 | tf_op jit(solution)/shard_map/ppermute | solution.py:242
  37.5 6.7 %collective-permute-start.3 = (bf16[288,128]{1,0:T(8,128)(2,1)S(1)}, bf16[288,128]{1,0:T(8,128)(2,1)S(1)}, u32[]{:S(2)}, u32[]{:S(2)}) collective-permute-start(bf16[288,128]{1,0:T(8,128)(2,1)S(1)} %fusion.1), channel_id=1, source_target_pairs={{0,128},{16,144},{64,192},{80,208},{128,0},{144,16},{192,64},{208,... | collective-permute-start | bytes 221192 | tf_op jit(solution)/shard_map/ppermute | solution.py:242
  40.1 5.9 %collective-permute-start.4 = (bf16[288,128]{1,0:T(8,128)(2,1)S(1)}, bf16[288,128]{1,0:T(8,128)(2,1)S(1)}, u32[]{:S(2)}, u32[]{:S(2)}) collective-permute-start(bf16[288,128]{1,0:T(8,128)(2,1)S(1)} %fusion.1), channel_id=1, source_target_pairs={{0,208},{16,192},{64,144},{80,128},{128,80},{144,64},{192,16},{208... | collective-permute-start | bytes 221192 | tf_op jit(solution)/shard_map/ppermute | solution.py:242
  46.1 4.4 %collective-permute-start.5 = (bf16[288,128]{1,0:T(8,128)(2,1)S(1)}, bf16[288,128]{1,0:T(8,128)(2,1)S(1)}, u32[]{:S(2)}, u32[]{:S(2)}) collective-permute-start(bf16[288,128]{1,0:T(8,128)(2,1)S(1)} %add_convert_fusion), channel_id=1, source_target_pairs={{0,48},{16,32},{32,16},{48,0},{1,49},{17,33},{33,17},{49,1},{2,50}... | collective-permute-start | bytes 221192 | tf_op jit(solution)/shard_map/ppermute | solution.py:242
  55.9 2.0 %collective-permute-start.7 = (f32[33,8,512]{2,1,0:T(8,128)S(1)}, f32[33,8,512]{2,1,0:T(8,128)S(1)}, u32[]{:S(2)}, u32[]{:S(2)}) collective-permute-start(f32[33,8,512]{2,1,0:T(8,128)S(1)} %get-tuple-element.26), channel_id=1, source_target_pairs={{0,16},{16,0},{1,17},{17,1},{2,18},{18,2},{3,19},{19,3},{4,20},{20... | collective-permute-start | bytes 1622024 | tf_op jit(solution)/shard_map/ppermute | solution.py:242
  58.0 5.9 %collective-permute-start.8 = (bf16[17,8,512]{2,1,0:T(8,128)(2,1)S(1)}, bf16[17,8,512]{2,1,0:T(8,128)(2,1)S(1)}, u32[]{:S(2)}, u32[]{:S(2)}) collective-permute-start(bf16[17,8,512]{2,1,0:T(8,128)(2,1)S(1)} %pad_maximum_fusion.4), channel_id=1, source_target_pairs={{0,48},{16,32},{32,16},{48,0},{1,49},{17,33},{33,17},{49,1},{2,50}... | collective-permute-start | bytes 417800 | tf_op jit(solution)/shard_map/ppermute | solution.py:242
  64.0 6.7 %collective-permute-start.10 = (bf16[6,8,512]{2,1,0:T(8,128)(2,1)S(1)}, bf16[6,8,512]{2,1,0:T(8,128)(2,1)S(1)}, u32[]{:S(2)}, u32[]{:S(2)}) collective-permute-start(bf16[6,8,512]{2,1,0:T(8,128)(2,1)S(1)} %pad_maximum_fusion.8), channel_id=1, source_target_pairs={{0,128},{16,144},{64,192},{80,208},{128,0},{144,16},{192,64},{208,... | collective-permute-start | bytes 147464 | tf_op jit(solution)/shard_map/ppermute | solution.py:242
  64.5 4.2 %collective-permute-start.9 = (bf16[5,8,512]{2,1,0:T(8,128)(2,1)S(1)}, bf16[5,8,512]{2,1,0:T(8,128)(2,1)S(1)}, u32[]{:S(2)}, u32[]{:S(2)}) collective-permute-start(bf16[5,8,512]{2,1,0:T(8,128)(2,1)S(1)} %pad_maximum_fusion.9), channel_id=1, source_target_pairs={{0,80},{16,64},{64,16},{80,0},{128,208},{144,192},{192,144},{208,1... | collective-permute-start | bytes 122888 | tf_op jit(solution)/shard_map/ppermute | solution.py:242
  66.1 4.6 %collective-permute-start.11 = (bf16[5,8,512]{2,1,0:T(8,128)(2,1)S(1)}, bf16[5,8,512]{2,1,0:T(8,128)(2,1)S(1)}, u32[]{:S(2)}, u32[]{:S(2)}) collective-permute-start(bf16[5,8,512]{2,1,0:T(8,128)(2,1)S(1)} %pad_maximum_fusion.10), channel_id=1, source_target_pairs={{0,208},{16,192},{64,144},{80,128},{128,80},{144,64},{192,16},{208... | collective-permute-start | bytes 122888 | tf_op jit(solution)/shard_map/ppermute | solution.py:242
  70.8 2.9 %collective-permute-start.12 = (bf16[5,8,512]{2,1,0:T(8,128)(2,1)S(1)}, bf16[5,8,512]{2,1,0:T(8,128)(2,1)S(1)}, u32[]{:S(2)}, u32[]{:S(2)}) collective-permute-start(bf16[5,8,512]{2,1,0:T(8,128)(2,1)S(1)} %pad_maximum_fusion.11), channel_id=1, source_target_pairs={{0,1},{1,0},{2,3},{3,2},{4,5},{5,4},{6,7},{7,6},{8,9},{9,8},{10,11... | collective-permute-start | bytes 122888 | tf_op jit(solution)/shard_map/ppermute | solution.py:242
  73.7 4.9 %collective-permute-start.13 = (f32[5,8,512]{2,1,0:T(8,128)S(1)}, f32[5,8,512]{2,1,0:T(8,128)S(1)}, u32[]{:S(2)}, u32[]{:S(2)}) collective-permute-start(f32[5,8,512]{2,1,0:T(8,128)S(1)} %maximum_add_fusion), channel_id=1, source_target_pairs={{0,8},{8,0},{1,9},{9,1},{2,10},{10,2},{3,11},{11,3},{4,12},{12,4},... | collective-permute-start | bytes 245768 | tf_op jit(solution)/shard_map/ppermute | solution.py:242
  78.6 5.7 %collective-permute-start.14 = (bf16[5,8,512]{2,1,0:T(8,128)(2,1)S(1)}, bf16[5,8,512]{2,1,0:T(8,128)(2,1)S(1)}, u32[]{:S(2)}, u32[]{:S(2)}) collective-permute-start(bf16[5,8,512]{2,1,0:T(8,128)(2,1)S(1)} %add_convert_fusion.1), channel_id=1, source_target_pairs={{0,2},{2,0},{4,6},{6,4},{1,3},{3,1},{5,7},{7,5},{8,10},{10,8},{12,... | collective-permute-start | bytes 122888 | tf_op jit(solution)/shard_map/ppermute | solution.py:242
  79.7 7.3 %collective-permute-start.15 = (bf16[5,8,512]{2,1,0:T(8,128)(2,1)S(1)}, bf16[5,8,512]{2,1,0:T(8,128)(2,1)S(1)}, u32[]{:S(2)}, u32[]{:S(2)}) collective-permute-start(bf16[5,8,512]{2,1,0:T(8,128)(2,1)S(1)} %add_convert_fusion.1), channel_id=1, source_target_pairs={{0,4},{2,6},{4,0},{6,2},{1,5},{3,7},{5,1},{7,3},{8,12},{10,14},{12... | collective-permute-start | bytes 122888 | tf_op jit(solution)/shard_map/ppermute | solution.py:242
  81.8 5.5 %collective-permute-start.16 = (bf16[5,8,512]{2,1,0:T(8,128)(2,1)S(1)}, bf16[5,8,512]{2,1,0:T(8,128)(2,1)S(1)}, u32[]{:S(2)}, u32[]{:S(2)}) collective-permute-start(bf16[5,8,512]{2,1,0:T(8,128)(2,1)S(1)} %add_convert_fusion.1), channel_id=1, source_target_pairs={{0,6},{2,4},{4,2},{6,0},{1,7},{3,5},{5,3},{7,1},{8,14},{10,12},{12... | collective-permute-start | bytes 122888 | tf_op jit(solution)/shard_map/ppermute | solution.py:242
  87.3 3.2 %collective-permute-start.17 = (bf16[4,8,512]{2,1,0:T(8,128)(2,1)S(1)}, bf16[4,8,512]{2,1,0:T(8,128)(2,1)S(1)}, u32[]{:S(2)}, u32[]{:S(2)}) collective-permute-start(bf16[4,8,512]{2,1,0:T(8,128)(2,1)S(1)} %slice.205), channel_id=1, source_target_pairs={{0,1},{1,0},{2,3},{3,2},{4,5},{5,4},{6,7},{7,6},{8,9},{9,8},{10,11... | collective-permute-start | bytes 98312 | tf_op jit(solution)/shard_map/ppermute | solution.py:242
  90.5 7.4 %collective-permute-start.19 = (bf16[2,4,8,512]{3,2,1,0:T(8,128)(2,1)S(1)}, bf16[2,4,8,512]{3,2,1,0:T(8,128)(2,1)S(1)}, u32[]{:S(2)}, u32[]{:S(2)}) collective-permute-start(bf16[2,4,8,512]{3,2,1,0:T(8,128)(2,1)S(1)} %get-tuple-element.46), channel_id=1, source_target_pairs={{0,128},{16,144},{64,192},{80,208},{128,0},{144,16},{192,64},{208,... | collective-permute-start | bytes 196616 | tf_op jit(solution)/shard_map/ppermute | solution.py:242
  91.5 7.7 %collective-permute-start.20 = (bf16[2,4,8,512]{3,2,1,0:T(8,128)(2,1)S(1)}, bf16[2,4,8,512]{3,2,1,0:T(8,128)(2,1)S(1)}, u32[]{:S(2)}, u32[]{:S(2)}) collective-permute-start(bf16[2,4,8,512]{3,2,1,0:T(8,128)(2,1)S(1)} %get-tuple-element.46), channel_id=1, source_target_pairs={{0,208},{16,192},{64,144},{80,128},{128,80},{144,64},{192,16},{208... | collective-permute-start | bytes 196616 | tf_op jit(solution)/shard_map/ppermute | solution.py:242
  97.2 4.1 %collective-permute-start.18 = (bf16[2,4,8,512]{3,2,1,0:T(8,128)(2,1)S(1)}, bf16[2,4,8,512]{3,2,1,0:T(8,128)(2,1)S(1)}, u32[]{:S(2)}, u32[]{:S(2)}) collective-permute-start(bf16[2,4,8,512]{3,2,1,0:T(8,128)(2,1)S(1)} %get-tuple-element.46), channel_id=1, source_target_pairs={{0,80},{16,64},{64,16},{80,0},{128,208},{144,192},{192,144},{208,1... | collective-permute-start | bytes 196616 | tf_op jit(solution)/shard_map/ppermute | solution.py:242
  101.3 3.1 %collective-permute-start.22 = (bf16[4,2,4,8,512]{4,3,2,1,0:T(8,128)(2,1)S(1)}, bf16[4,2,4,8,512]{4,3,2,1,0:T(8,128)(2,1)S(1)}, u32[]{:S(2)}, u32[]{:S(2)}) collective-permute-start(bf16[4,2,4,8,512]{4,3,2,1,0:T(8,128)(2,1)S(1)} %pad_maximum_fusion.1.piece_ref), channel_id=1, source_target_pairs={{0,16},{16,0},{1,17},{17,1},{2,18},{18,2},{3,19},{19,3},{4,20},{20... | collective-permute-start | bytes 786440 | tf_op jit(solution)/shard_map/ppermute | solution.py:242
  101.8 6.5 %collective-permute-start.23 = (bf16[2,2,4,8,512]{4,3,2,1,0:T(8,128)(2,1)S(1)}, bf16[2,2,4,8,512]{4,3,2,1,0:T(8,128)(2,1)S(1)}, u32[]{:S(2)}, u32[]{:S(2)}) collective-permute-start(bf16[2,2,4,8,512]{4,3,2,1,0:T(8,128)(2,1)S(1)} %pad_maximum_fusion.6), channel_id=1, source_target_pairs={{0,56},{8,48},{16,40},{24,32},{32,24},{40,16},{48,8},{56,0},{1,57}... | collective-permute-start | bytes 393224 | tf_op jit(solution)/shard_map/ppermute | solution.py:242
  102.2 6.1 %collective-permute-start.21 = (bf16[2,2,4,8,512]{4,3,2,1,0:T(8,128)(2,1)S(1)}, bf16[2,2,4,8,512]{4,3,2,1,0:T(8,128)(2,1)S(1)}, u32[]{:S(2)}, u32[]{:S(2)}) collective-permute-start(bf16[2,2,4,8,512]{4,3,2,1,0:T(8,128)(2,1)S(1)} %pad_maximum_fusion.5), channel_id=1, source_target_pairs={{0,48},{16,32},{32,16},{48,0},{1,49},{17,33},{33,17},{49,1},{2,50}... | collective-permute-start | bytes 393224 | tf_op jit(solution)/shard_map/ppermute | solution.py:242
  (3 other events, 17.7 us)

commit v4 on v3

--- a/solution.py
+++ b/solution.py
@@ -110,9 +110,9 @@
         to = b ^ me
 
         def store(ref, at):
-            ref[at, 0:128, :] = cross[b * 128 : (b + 1) * 128, 0:128]
-            ref[at, 128:256, :] = cross[b * 128 : (b + 1) * 128, 128:256]
-            ref[at, 256:288, :] = gram[:, b * 128 : (b + 1) * 128]
+            ref[at, 0:128, :] = cross[b * 128 : (b + 1) * 128, 0:128].astype(ref.dtype)
+            ref[at, 128:256, :] = cross[b * 128 : (b + 1) * 128, 128:256].astype(ref.dtype)
+            ref[at, 256:288, :] = gram[:, b * 128 : (b + 1) * 128].astype(ref.dtype)
 
         @pl.when(to < 2)
         def _():
@@ -123,10 +123,10 @@
             store(send_ref, to - 2)
 
 
-def grad_kernel(where_ref, packed_ref, whole_ref, student_ref, tnorm_ref, inv_ref, keep_ref, send_ref, near_ref, other_ref, loss_ref, cross, gram, packed, grads, onehots):
+def grad_kernel(where_ref, packed_ref, whole_ref, student_ref, tnorm_ref, inv_ref, keep_ref, send_ref, loss_ref, cross, gram, packed, grads, onehots):
     packed[...] = packed_ref[...].astype(F32)
     item, feat, me = where_ref[0], where_ref[1], where_ref[2]
-    place, zb, half = where_ref[3], where_ref[4], where_ref[5]
+    place, zb, half, kept = where_ref[3], where_ref[4], where_ref[5], where_ref[6]
     for b in range(4):
         block = whole_ref[b ^ me]
         cross[b * 128 : (b + 1) * 128, 0:128] = block[0:128]
@@ -161,24 +161,20 @@
             return (((code >> 4) ^ place) << 5) + (((low >> 3) ^ zb) << 4) + 8 * level + (low & 7)
 
         first = (codes_of(packed, 0, n * per, per) - 16 * item) & 255
-        own = 512 + (((first >> 3) ^ zb) << 4) + (first & 7)
+        own = 512 + ((first >> 3) ^ kept) * 24 + (first & 7)
         first = jnp.where(first < 16, own, 560)
         second = codes_of(packed, 1, n * per, per) - 32 * (item & 7)
         low = second & 15
-        side = (low >> 3) ^ zb
-        second = jnp.where(
-            ((second >> 4) ^ half) == 0, 520 + (side << 4) + (low & 7), 544 + (side << 3) + (low & 7)
-        )
+        second = 520 + ((low >> 3) ^ kept) * 24 + ((second >> 4) ^ half) * 8 + (low & 7)
         third = spot(codes_of(packed, 2, n * per, per), 0)
         fourth = spot(codes_of(packed, 3, n * per, per), 1)
         onehots[0:512, span] = ((large == third) | (large == fourth)).astype(F32).astype(BF16)
         onehots[512:576, span] = ((small == first) | (small == second)).astype(F32).astype(BF16)
     total = lax.dot_general(onehots[...], grads[...], NT, preferred_element_type=F32)
-    keep_ref[...] = total[0:256].reshape(keep_ref.shape)
-    send_ref[0:32] = total[256:512].reshape(32, 8, DS)
-    send_ref[32] = total[560:568]
-    near_ref[...] = total[512:544].reshape(near_ref.shape)
-    other_ref[...] = total[544:560].reshape(other_ref.shape).astype(BF16)
+    for k, ref in enumerate((keep_ref, send_ref)):
+        ref[0:32] = total[k * 256 : (k + 1) * 256].reshape(32, 8, DS).astype(ref.dtype)
+        ref[32:35] = total[512 + k * 24 : 536 + k * 24].reshape(3, 8, DS).astype(ref.dtype)
+        ref[35] = total[560:568].astype(ref.dtype)
 
 
 def spread(c, x, where_ref, piece_ref, out_hbm, rows, sems):
@@ -188,25 +184,25 @@
     copies = []
 
     def copy(level, start, count, to):
-        target = out_hbm.at[level, pl.ds(pl.multiple_of(to, 16), count)]
+        target = out_hbm.at[level, pl.ds(pl.multiple_of(to, 8), count)]
         copies.append(pltpu.make_async_copy(rows.at[level, pl.ds(start, count)], target, sems.at[len(copies)]))
         copies[-1].start()
 
     for k, level in enumerate((2, 3, 0, 1)):
         for y in range(4):
-            ay = y ^ (place & 3)
-            row = (ay & 1) * 32 + (ay >> 1) * 16 if level == 1 else ay * 16
             for z in range(2):
-                at = pl.multiple_of(row + (z ^ zb) * 8, 8)
+                at = pl.multiple_of((y ^ (place & 3)) * 16 + (z ^ zb) * 8, 8)
                 rows[level, pl.ds(at, 8), :] = piece_ref[y, z, k].astype(F32)
-        if level == 0:
-            for j in range(4):
-                copy(0, j * 16, 16, (j * 4 + axl * 2 + (kept ^ axl ^ (j & 1))) * 16)
-        elif level == 1:
-            for j in range(2):
-                copy(1, j * 32, 32, (j * 4 + axl * 2 + (kept ^ axl ^ j)) * 32)
-        else:
+        if level > 1:
             copy(level, 0, 64, base * 16)
+            continue
+        for j in range(8):
+            ay, ac = j >> 1, j & 1
+            if level == 0:
+                row = (ay * 4 + axl * 2 + ac) * 16
+            else:
+                row = ((ay & 1) * 4 + axl * 2 + ac) * 32 + (ay >> 1) * 16
+            copy(level, j * 8, 8, row + kept * 8)
     for one in copies:
         one.wait()
 
@@ -254,13 +250,17 @@
     return swap(array, ("y", "c"), 8, 2 * bits + (bits & 1))
 
 
+def across_z(array):
+    return swap(array, ("c", "zb"), 4, 3)
+
+
 def on_device(teacher, codebooks, codes):
     y, xl, c = lax.axis_index("y"), lax.axis_index("xl"), lax.axis_index("c")
     zb = lax.axis_index("zb")
     item = y * 4 + xl * 2 + c
     feat = lax.axis_index(FEAT)
-    kept = c ^ xl ^ (y & 1)
-    where = jnp.stack([item, feat, kept * 2 + xl, kept * 8 + xl * 4 + y, zb, y >> 1]).astype(jnp.int32)
+    kept = c ^ xl ^ (y & 1) ^ lax.axis_index("xh") ^ (lax.axis_index("za") & 1) ^ zb
+    where = jnp.stack([item, feat, kept * 2 + xl, kept * 8 + xl * 4 + y, zb, y >> 1, kept]).astype(jnp.int32)
 
     teacher, packed = call(
         pack_kernel,
@@ -276,7 +276,7 @@
         [SMEM, VMEM, VMEM, VMEM],
         [
             ((2, 288, 128), F32, VMEM),
-            ((2, 288, 128), F32, VMEM),
+            ((2, 288, 128), BF16, VMEM),
             ((DS, 2048), BF16, VMEM),
             ((2048, 256), BF16, VMEM),
             ((1, 2048), F32, VMEM),
@@ -284,7 +284,7 @@
         [pltpu.VMEM((16, 24, 128), F32)],
     )(where, packed, teacher, table)
 
-    part = keep + swap(send, "c", 2, 1)
+    part = keep + swap(send, "c", 2, 1).astype(F32)
     part = part[0] + across_x(part[1].astype(BF16)).astype(F32)
     own = part.astype(BF16)
     a, b, d = (across_y(own, k) for k in (1, 2, 3))
@@ -292,16 +292,10 @@
     whole = jnp.stack([whole, across_x(whole)])
     whole = jnp.concatenate([whole, swap(whole, "c", 2, 1)])
 
-    keep, send, near, other, loss = call(
+    keep, send, loss = call(
         grad_kernel,
         [SMEM] + [VMEM] * 5,
-        [
-            ((32, 8, DS), F32, VMEM),
-            ((33, 8, DS), F32, VMEM),
-            ((2, 2, 8, DS), F32, VMEM),
-            ((2, 8, DS), BF16, VMEM),
-            ((8, DS), F32, VMEM),
-        ],
+        [((36, 8, DS), F32, VMEM), ((36, 8, DS), BF16, VMEM), ((8, DS), F32, VMEM)],
         [
             pltpu.VMEM((DS, 256), BF16),
             pltpu.VMEM((32, DS), BF16),
@@ -311,39 +305,39 @@
         ],
     )(where, packed, whole, student, tnorm, inv)
 
-    got = swap(send, "c", 2, 1)
-    sums = keep + got[:32]
+    got = swap(send, "c", 2, 1).astype(F32)
+    sums = keep[:32] + got[:32]
+    low = jnp.where(c == 0, keep[32:], got[32:])
+    high = jnp.where(c == 0, got[32:], keep[32:])
+    holds = kept == 0
     none = jnp.zeros((), BF16)
-    extra = jnp.where(c == 1, got[32], 0.0)
-    ahead = jnp.where((c == 1) & (xl == 0), send[32:], jnp.where((c == 0) & (xl == 1), got[32:], 0.0))
-    got = across_x(jnp.concatenate([sums[16:].astype(BF16), ahead.astype(BF16)]))
+    high_zero = high[0] + jnp.where(holds, low[3], 0.0)
+    ahead = jnp.where(holds, high[3:], 0.0).astype(BF16)
+    got = across_x(jnp.concatenate([sums[16:].astype(BF16), ahead]))
     sums = sums[:16] + got[:16].astype(F32)
-    extra = extra + jnp.where((c == 0) & (xl == 1), got[16].astype(F32), 0.0)
-    ahead = jnp.where((c == 1) & (xl == 0), got[16:], none)
+    low_zero = low[0] + jnp.where(xl == 1, got[16].astype(F32), 0.0)
+    ahead = jnp.where(xl == 0, got[16:], none)
     odd = (y & 1) == 1
     one = across_y(jnp.concatenate([sums[4:8].astype(BF16), jnp.where(odd, none, ahead)]), 1)
-    two = across_y(jnp.concatenate([sums[8:12].astype(BF16), other]), 2)
+    two = across_y(jnp.concatenate([sums[8:12], low[2:3], high[2:3]]).astype(BF16), 2)
     three = across_y(jnp.concatenate([sums[12:16].astype(BF16), jnp.where(odd, ahead, none)]), 3)
     sums = sums[0:4] + one[:4].astype(F32) + two[:4].astype(F32) + three[:4].astype(F32)
-    extra = extra + one[4].astype(F32) + three[4].astype(F32)
-
-    def rows_of(z):
-        zero = near[z, 0] + jnp.where(zb == z, extra, 0.0)
-        first = near[z, 1] + two[4 + z].astype(F32)
-        return jnp.concatenate([sums[2 * z : 2 * z + 2], zero[None], first[None], loss[None]])
-
-    rows = rows_of(0) + swap(rows_of(1).astype(BF16), "zb", 2, 1).astype(F32)
-    own = (rows + swap(rows, "xh", 2, 1)).astype(BF16)
-    a, b, d = (swap(own, "za", 4, k).astype(F32) for k in (1, 2, 3))
+    low = jnp.stack([low_zero + one[4].astype(F32) + three[4].astype(F32), low[1] + two[4].astype(F32)])
+    high = jnp.stack([high_zero, high[1] + two[5].astype(F32)])
+
+    sent = jnp.concatenate([sums[2:4], jnp.where(zb == 0, high, low), loss[None]]).astype(BF16)
+    rows = jnp.concatenate([sums[0:2], jnp.where(zb == 0, low, high), loss[None]]) + across_z(sent).astype(F32)
+    own = (rows + swap(rows, ("c", "xh"), 4, 3)).astype(BF16)
+    a, b, d = (swap(own, ("c", "za"), 8, k + 4 * (k & 1)).astype(F32) for k in (1, 2, 3))
     rows = (own.astype(F32) + a) + (b + d)
     loss = rows[4]
     rows = rows[:4].astype(BF16)
 
-    rows = jnp.stack([rows, swap(rows, "zb", 2, 1)])
+    rows = jnp.stack([rows, across_z(rows)])
     rows = jnp.stack([rows] + [across_y(rows, k) for k in (1, 2, 3)])
-    parts = across_x(rows[:2]), swap(rows[2:], ("xl", "c", "xh"), 8, 7)
+    parts = across_x(rows[:2]), swap(rows[2:], ("xl", "xh"), 4, 3)
     far = swap(rows, "c", 2, 1)
-    rows_and_sems = [pltpu.VMEM((4, 64, DS), F32), pltpu.SemaphoreType.DMA((8,))]
+    rows_and_sems = [pltpu.VMEM((4, 64, DS), F32), pltpu.SemaphoreType.DMA((18,))]
     out = ((4, 256, DS), F32, ANY)
     outs = [out, ((8, DS), BF16, VMEM)]
     grads, loss = call(first_kernel, [SMEM, VMEM, VMEM], [out, ((1, 1), F32, VMEM)], rows_and_sems)(where, rows, loss)

time: 112 us -> 112 us (level)
  starting transfers between devices: 42.3 us -> 40.2 us
  waiting for transfers between devices: 49.7 us -> 51.5 us
    ppermute x25, starting transfers between devices: 30.7 us -> 28.6 us  [swap(): return lax.ppermute(array, axis, [(j, j ^ bit) for j in range(size)])]
    ppermute x25, waiting for transfers between devices: 41.6 us -> 43.4 us  [swap(): return lax.ppermute(array, axis, [(j, j ^ bit) for j in range(size)])]
where the time goes in v4:
time: 112 us
  waiting for transfers between devices  51.5 us (46%)
  starting transfers between devices  40.2 us (36%)
  Pallas kernels  17.5 us (16%)
    ppermute x25, waiting for transfers between devices, swap(): return lax.ppermute(array, axis, [(j, j ^ bit) for j in range(size)])  43.4 us
    ppermute x25, starting transfers between devices, swap(): return lax.ppermute(array, axis, [(j, j ^ bit) for j in range(size)])  28.6 us
    all_to_all x1, starting transfers between devices, on_device(): lax.all_to_all(jnp.broadcast_to(packed[None], (16, 24, 128)), FEAT, 0, 0,...  11.6 us
    all_to_all x1, waiting for transfers between devices, on_device(): lax.all_to_all(jnp.broadcast_to(packed[None], (16, 24, 128)), FEAT, 0, 0,...  8.09 us
    pallas_call x1, Pallas kernels, on_device(): call(cross_kernel, [SMEM, VMEM, VMEM, VMEM], [((2, 288, 128), F32, VMEM),...  4.04 us
    pallas_call x1, Pallas kernels, on_device(): call(grad_kernel, [SMEM] + [VMEM] * 5, [((36, 8, DS), F32, VMEM), ((36, 8...  3.91 us
    pallas_call x2, Pallas kernels, on_device(): call(next_kernel(c, 1), [SMEM, VMEM, ANY], [out], rows_and_sems, {2: 0})  3.03 us
  transfers between devices with their start and end apart: 26, of which 19 were waited for; matrix products, arithmetic and copies ran while one was open for 0% of the time, Pallas kernels for 5%

profile of v4, /device:TPU:1, one launch (start us, length us, event | category | flops | bytes accessed | tf_op | source)
XLA Modules:
  0.0 111.7 jit_solution(13937997756761479345)
XLA Ops:
  0.6 2.2 %shard_map.50 = (bf16[2048,256]{1,0:T(8,128)(2,1)S(1)}, bf16[24,128]{1,0:T(8,128)(2,1)S(1)}) custom-call(bf16[2048,256]{1,0:T(8,128)(2,1)} %teacher_hbm.1, s32[4,128]{1,0:T(4,128)} %bitcast.45), custom_call_target="tpu_custom_call" | custom-call | tf_op jit(solution)/shard_map/pallas_call | solution.py:265
  3.5 11.6 %all-to-all-start = ((bf16[16,24,128]{2,1,0:T(8,128)(2,1)}), bf16[16,24,128]{2,1,0:T(8,128)(2,1)S(1)}, u32[]{:S(2)}, u32[]{:S(2)}) async-start(bf16[16,24,128]{2,1,0:T(8,128)(2,1)} %broadcast_in_dim.26), calls=%async_computation | async-start | bytes 196608 | tf_op jit(solution)/shard_map/all_to_all | solution.py:271
  16.0 8.1 %all-to-all-done.packed_ref = bf16[16,24,128]{2,1,0:T(8,128)(2,1)S(1)} async-done(((bf16[16,24,128]{2,1,0:T(8,128)(2,1)}), bf16[16,24,128]{2,1,0:T(8,128)(2,1)S(1)}, u32[]{:S(2)}, u32[]{:S(2)}) %all-to-all-start) | async-done | bytes 98336 | tf_op jit(solution)/shard_map/all_to_all | solution.py:271
  24.1 4.0 %shard_map.52 = (f32[2,288,128]{2,1,0:T(8,128)S(1)}, bf16[2,288,128]{2,1,0:T(8,128)(2,1)S(1)}, bf16[512,2048]{1,0:T(8,128)(2,1)S(1)}, bf16[2048,256]{1,0:T(8,128)(2,1)S(1)}, f32[1,2048]{1,0:T(1,128)S(1)}) custom-call(s32[7]{0:T(128)S(1)} %stack.78.where_ref, bf16[16,24,128]{2,1,0:T(8,128)(2,1)S(1)} %all-to-all-done.packed_ref, ...), custom_call_target="tpu_custom_call" | custom-call | tf_op jit(solution)/shard_map/pallas_call | solution.py:274
  28.1 2.1 %collective-permute-start = (bf16[2,288,128]{2,1,0:T(8,128)(2,1)S(1)}, bf16[2,288,128]{2,1,0:T(8,128)(2,1)S(1)}, u32[]{:S(2)}, u32[]{:S(2)}) collective-permute-start(bf16[2,288,128]{2,1,0:T(8,128)(2,1)S(1)} %get-tuple-element.19), channel_id=1, source_target_pairs={{0,16},{16,0},{1,17},{17,1},{2,18},{18,2},{3,19},{19,3},{4,20},{20... | collective-permute-start | bytes 442376 | tf_op jit(solution)/shard_map/ppermute | solution.py:238
  31.9 3.7 %collective-permute-done.1 = bf16[288,128]{1,0:T(8,128)(2,1)S(1)} collective-permute-done((bf16[288,128]{1,0:T(8,128)(2,1)S(1)}, bf16[288,128]{1,0:T(8,128)(2,1)S(1)}, u32[]{:S(2)}, u32[]{:S(2)}) %collective-permute-start.1) | collective-permute-done | bytes 73760 | tf_op jit(solution)/shard_map/ppermute | solution.py:238
  37.3 2.6 %collective-permute-start.3 = (bf16[288,128]{1,0:T(8,128)(2,1)S(1)}, bf16[288,128]{1,0:T(8,128)(2,1)S(1)}, u32[]{:S(2)}, u32[]{:S(2)}) collective-permute-start(bf16[288,128]{1,0:T(8,128)(2,1)S(1)} %fusion.1), channel_id=1, source_target_pairs={{0,128},{16,144},{64,192},{80,208},{128,0},{144,16},{192,64},{208,... | collective-permute-start | bytes 221192 | tf_op jit(solution)/shard_map/ppermute | solution.py:238
  40.1 3.8 %collective-permute-done.3 = bf16[288,128]{1,0:T(8,128)(2,1)S(1)} collective-permute-done((bf16[288,128]{1,0:T(8,128)(2,1)S(1)}, bf16[288,128]{1,0:T(8,128)(2,1)S(1)}, u32[]{:S(2)}, u32[]{:S(2)}) %collective-permute-start.3) | collective-permute-done | bytes 73760 | tf_op jit(solution)/shard_map/ppermute | solution.py:238
  44.0 1.8 %collective-permute-done.4 = bf16[288,128]{1,0:T(8,128)(2,1)S(1)} collective-permute-done((bf16[288,128]{1,0:T(8,128)(2,1)S(1)}, bf16[288,128]{1,0:T(8,128)(2,1)S(1)}, u32[]{:S(2)}, u32[]{:S(2)}) %collective-permute-start.4) | collective-permute-done | bytes 73760 | tf_op jit(solution)/shard_map/ppermute | solution.py:238
  46.5 3.7 %collective-permute-done.5 = bf16[288,128]{1,0:T(8,128)(2,1)S(1)} collective-permute-done((bf16[288,128]{1,0:T(8,128)(2,1)S(1)}, bf16[288,128]{1,0:T(8,128)(2,1)S(1)}, u32[]{:S(2)}, u32[]{:S(2)}) %collective-permute-start.5) | collective-permute-done | bytes 73760 | tf_op jit(solution)/shard_map/ppermute | solution.py:238
  51.7 3.9 %shard_map.53 = (f32[36,8,512]{2,1,0:T(8,128)S(1)}, bf16[36,8,512]{2,1,0:T(8,128)(2,1)S(1)}, f32[8,512]{1,0:T(8,128)S(1)}) custom-call(s32[7]{0:T(128)S(1)} %stack.78.where_ref, bf16[16,24,128]{2,1,0:T(8,128)(2,1)S(1)} %all-to-all-done.packed_ref, bf16[4,288,128]{2,1,0:T(8,128)(2,1)S(1)} %pad_maximum_fusion.whole_ref, ...), custom_call_target="tpu_custom_call" | custom-call | tf_op jit(solution)/shard_map/pallas_call | solution.py:295
  58.4 5.1 %collective-permute-done.8 = bf16[17,8,512]{2,1,0:T(8,128)(2,1)S(1)} collective-permute-done((bf16[17,8,512]{2,1,0:T(8,128)(2,1)S(1)}, bf16[17,8,512]{2,1,0:T(8,128)(2,1)S(1)}, u32[]{:S(2)}, u32[]{:S(2)}) %collective-permute-start.8) | collective-permute-done | bytes 139296 | tf_op jit(solution)/shard_map/ppermute | solution.py:238
  65.6 1.7 %collective-permute-start.11 = (bf16[5,8,512]{2,1,0:T(8,128)(2,1)S(1)}, bf16[5,8,512]{2,1,0:T(8,128)(2,1)S(1)}, u32[]{:S(2)}, u32[]{:S(2)}) collective-permute-start(bf16[5,8,512]{2,1,0:T(8,128)(2,1)S(1)} %pad_maximum_fusion.10), channel_id=1, source_target_pairs={{0,208},{16,192},{64,144},{80,128},{128,80},{144,64},{192,16},{208... | collective-permute-start | bytes 122888 | tf_op jit(solution)/shard_map/ppermute | solution.py:238
  68.2 2.0 %collective-permute-done.11 = bf16[5,8,512]{2,1,0:T(8,128)(2,1)S(1)} collective-permute-done((bf16[5,8,512]{2,1,0:T(8,128)(2,1)S(1)}, bf16[5,8,512]{2,1,0:T(8,128)(2,1)S(1)}, u32[]{:S(2)}, u32[]{:S(2)}) %collective-permute-start.11) | collective-permute-done | bytes 40992 | tf_op jit(solution)/shard_map/ppermute | solution.py:238
  71.1 2.7 %collective-permute-done.12 = bf16[5,8,512]{2,1,0:T(8,128)(2,1)S(1)} collective-permute-done((bf16[5,8,512]{2,1,0:T(8,128)(2,1)S(1)}, bf16[5,8,512]{2,1,0:T(8,128)(2,1)S(1)}, u32[]{:S(2)}, u32[]{:S(2)}) %collective-permute-start.12) | collective-permute-done | bytes 40992 | tf_op jit(solution)/shard_map/ppermute | solution.py:238
  74.4 5.1 %collective-permute-done.13 = f32[5,8,512]{2,1,0:T(8,128)S(1)} collective-permute-done((f32[5,8,512]{2,1,0:T(8,128)S(1)}, f32[5,8,512]{2,1,0:T(8,128)S(1)}, u32[]{:S(2)}, u32[]{:S(2)}) %collective-permute-start.13) | collective-permute-done | bytes 81952 | tf_op jit(solution)/shard_map/ppermute | solution.py:238
  80.5 2.1 %collective-permute-start.15 = (bf16[5,8,512]{2,1,0:T(8,128)(2,1)S(1)}, bf16[5,8,512]{2,1,0:T(8,128)(2,1)S(1)}, u32[]{:S(2)}, u32[]{:S(2)}) collective-permute-start(bf16[5,8,512]{2,1,0:T(8,128)(2,1)S(1)} %add_convert_fusion.1), channel_id=1, source_target_pairs={{0,4},{2,6},{4,0},{6,2},{16,20},{18,22},{20,16},{22,18},{1,5},{3,7... | collective-permute-start | bytes 122888 | tf_op jit(solution)/shard_map/ppermute | solution.py:238
  82.6 3.2 %collective-permute-start.16 = (bf16[5,8,512]{2,1,0:T(8,128)(2,1)S(1)}, bf16[5,8,512]{2,1,0:T(8,128)(2,1)S(1)}, u32[]{:S(2)}, u32[]{:S(2)}) collective-permute-start(bf16[5,8,512]{2,1,0:T(8,128)(2,1)S(1)} %add_convert_fusion.1), channel_id=1, source_target_pairs={{0,22},{2,20},{4,18},{6,16},{16,6},{18,4},{20,2},{22,0},{1,23},{3,... | collective-permute-start | bytes 122888 | tf_op jit(solution)/shard_map/ppermute | solution.py:238
  85.8 1.9 %collective-permute-done.15 = bf16[5,8,512]{2,1,0:T(8,128)(2,1)S(1)} collective-permute-done((bf16[5,8,512]{2,1,0:T(8,128)(2,1)S(1)}, bf16[5,8,512]{2,1,0:T(8,128)(2,1)S(1)}, u32[]{:S(2)}, u32[]{:S(2)}) %collective-permute-start.15) | collective-permute-done | bytes 40992 | tf_op jit(solution)/shard_map/ppermute | solution.py:238
  89.4 2.5 %collective-permute-start.17 = (bf16[4,8,512]{2,1,0:T(8,128)(2,1)S(1)}, bf16[4,8,512]{2,1,0:T(8,128)(2,1)S(1)}, u32[]{:S(2)}, u32[]{:S(2)}) collective-permute-start(bf16[4,8,512]{2,1,0:T(8,128)(2,1)S(1)} %slice.234), channel_id=1, source_target_pairs={{0,17},{1,16},{16,1},{17,0},{2,19},{3,18},{18,3},{19,2},{4,21},{5,... | collective-permute-start | bytes 98312 | tf_op jit(solution)/shard_map/ppermute | solution.py:238
  96.5 2.1 %collective-permute-done.19 = bf16[2,4,8,512]{3,2,1,0:T(8,128)(2,1)S(1)} collective-permute-done((bf16[2,4,8,512]{3,2,1,0:T(8,128)(2,1)S(1)}, bf16[2,4,8,512]{3,2,1,0:T(8,128)(2,1)S(1)}, u32[]{:S(2)}, u32[]{:S(2)}) %collective-permute-start.19) | collective-permute-done | bytes 65568 | tf_op jit(solution)/shard_map/ppermute | solution.py:238
  98.6 1.9 %collective-permute-done.20 = bf16[2,4,8,512]{3,2,1,0:T(8,128)(2,1)S(1)} collective-permute-done((bf16[2,4,8,512]{3,2,1,0:T(8,128)(2,1)S(1)}, bf16[2,4,8,512]{3,2,1,0:T(8,128)(2,1)S(1)}, u32[]{:S(2)}, u32[]{:S(2)}) %collective-permute-start.20) | collective-permute-done | bytes 65568 | tf_op jit(solution)/shard_map/ppermute | solution.py:238
  101.7 2.0 %shard_map.54 = (f32[4,256,512]{2,1,0:T(8,128)}, f32[1,1]{1,0:T(1,128)}) custom-call(s32[7]{0:T(128)S(1)} %stack.78.where_ref, bf16[4,2,4,8,512]{4,3,2,1,0:T(8,128)(2,1)S(1)} %pad_maximum_fusion.1.piece_ref, f32[8,512]{1,0:T(8,128)S(1)} %slice_bitcast_fusion.1.parts_ref), custom_call_target="tpu_custom_call" | custom-call | tf_op jit(solution)/shard_map/pallas_call | solution.py:343
  105.2 2.1 %collective-permute-done.23 = bf16[2,2,4,8,512]{4,3,2,1,0:T(8,128)(2,1)S(1)} collective-permute-done((bf16[2,2,4,8,512]{4,3,2,1,0:T(8,128)(2,1)S(1)}, bf16[2,2,4,8,512]{4,3,2,1,0:T(8,128)(2,1)S(1)}, u32[]{:S(2)}, u32[]{:S(2)}) %collective-permute-start.23) | collective-permute-done | bytes 131104 | tf_op jit(solution)/shard_map/ppermute | solution.py:238
  (79 shorter events, 28.6 us)
Async XLA Ops:
  3.5 20.6 %all-to-all-start = ((bf16[16,24,128]{2,1,0:T(8,128)(2,1)}), bf16[16,24,128]{2,1,0:T(8,128)(2,1)S(1)}, u32[]{:S(2)}, u32[]{:S(2)}) async-start(bf16[16,24,128]{2,1,0:T(8,128)(2,1)} %broadcast_in_dim.26), calls=%async_computation | async-start | bytes 196608 | tf_op jit(solution)/shard_map/all_to_all | solution.py:271
  28.1 3.1 %collective-permute-start = (bf16[2,288,128]{2,1,0:T(8,128)(2,1)S(1)}, bf16[2,288,128]{2,1,0:T(8,128)(2,1)S(1)}, u32[]{:S(2)}, u32[]{:S(2)}) collective-permute-start(bf16[2,288,128]{2,1,0:T(8,128)(2,1)S(1)} %get-tuple-element.19), channel_id=1, source_target_pairs={{0,16},{16,0},{1,17},{17,1},{2,18},{18,2},{3,19},{19,3},{4,20},{20... | collective-permute-start | bytes 442376 | tf_op jit(solution)/shard_map/ppermute | solution.py:238
  31.3 4.3 %collective-permute-start.1 = (bf16[288,128]{1,0:T(8,128)(2,1)S(1)}, bf16[288,128]{1,0:T(8,128)(2,1)S(1)}, u32[]{:S(2)}, u32[]{:S(2)}) collective-permute-start(bf16[288,128]{1,0:T(8,128)(2,1)S(1)} %fusion.2), channel_id=1, source_target_pairs={{0,48},{16,32},{32,16},{48,0},{1,49},{17,33},{33,17},{49,1},{2,50}... | collective-permute-start | bytes 221192 | tf_op jit(solution)/shard_map/ppermute | solution.py:238
  35.6 4.5 %collective-permute-start.2 = (bf16[288,128]{1,0:T(8,128)(2,1)S(1)}, bf16[288,128]{1,0:T(8,128)(2,1)S(1)}, u32[]{:S(2)}, u32[]{:S(2)}) collective-permute-start(bf16[288,128]{1,0:T(8,128)(2,1)S(1)} %fusion.1), channel_id=1, source_target_pairs={{0,80},{16,64},{64,16},{80,0},{128,208},{144,192},{192,144},{208,1... | collective-permute-start | bytes 221192 | tf_op jit(solution)/shard_map/ppermute | solution.py:238
  37.3 6.7 %collective-permute-start.3 = (bf16[288,128]{1,0:T(8,128)(2,1)S(1)}, bf16[288,128]{1,0:T(8,128)(2,1)S(1)}, u32[]{:S(2)}, u32[]{:S(2)}) collective-permute-start(bf16[288,128]{1,0:T(8,128)(2,1)S(1)} %fusion.1), channel_id=1, source_target_pairs={{0,128},{16,144},{64,192},{80,208},{128,0},{144,16},{192,64},{208,... | collective-permute-start | bytes 221192 | tf_op jit(solution)/shard_map/ppermute | solution.py:238
  39.9 5.9 %collective-permute-start.4 = (bf16[288,128]{1,0:T(8,128)(2,1)S(1)}, bf16[288,128]{1,0:T(8,128)(2,1)S(1)}, u32[]{:S(2)}, u32[]{:S(2)}) collective-permute-start(bf16[288,128]{1,0:T(8,128)(2,1)S(1)} %fusion.1), channel_id=1, source_target_pairs={{0,208},{16,192},{64,144},{80,128},{128,80},{144,64},{192,16},{208... | collective-permute-start | bytes 221192 | tf_op jit(solution)/shard_map/ppermute | solution.py:238
  45.8 4.4 %collective-permute-start.5 = (bf16[288,128]{1,0:T(8,128)(2,1)S(1)}, bf16[288,128]{1,0:T(8,128)(2,1)S(1)}, u32[]{:S(2)}, u32[]{:S(2)}) collective-permute-start(bf16[288,128]{1,0:T(8,128)(2,1)S(1)} %add_convert_fusion), channel_id=1, source_target_pairs={{0,48},{16,32},{32,16},{48,0},{1,49},{17,33},{33,17},{49,1},{2,50}... | collective-permute-start | bytes 221192 | tf_op jit(solution)/shard_map/ppermute | solution.py:238
  57.5 5.9 %collective-permute-start.8 = (bf16[17,8,512]{2,1,0:T(8,128)(2,1)S(1)}, bf16[17,8,512]{2,1,0:T(8,128)(2,1)S(1)}, u32[]{:S(2)}, u32[]{:S(2)}) collective-permute-start(bf16[17,8,512]{2,1,0:T(8,128)(2,1)S(1)} %pad_maximum_fusion.4), channel_id=1, source_target_pairs={{0,48},{16,32},{32,16},{48,0},{1,49},{17,33},{33,17},{49,1},{2,50}... | collective-permute-start | bytes 417800 | tf_op jit(solution)/shard_map/ppermute | solution.py:238
  63.5 6.7 %collective-permute-start.10 = (bf16[6,8,512]{2,1,0:T(8,128)(2,1)S(1)}, bf16[6,8,512]{2,1,0:T(8,128)(2,1)S(1)}, u32[]{:S(2)}, u32[]{:S(2)}) collective-permute-start(bf16[6,8,512]{2,1,0:T(8,128)(2,1)S(1)} %pad_maximum_fusion.8), channel_id=1, source_target_pairs={{0,128},{16,144},{64,192},{80,208},{128,0},{144,16},{192,64},{208,... | collective-permute-start | bytes 147464 | tf_op jit(solution)/shard_map/ppermute | solution.py:238
  64.0 4.2 %collective-permute-start.9 = (bf16[5,8,512]{2,1,0:T(8,128)(2,1)S(1)}, bf16[5,8,512]{2,1,0:T(8,128)(2,1)S(1)}, u32[]{:S(2)}, u32[]{:S(2)}) collective-permute-start(bf16[5,8,512]{2,1,0:T(8,128)(2,1)S(1)} %pad_maximum_fusion.9), channel_id=1, source_target_pairs={{0,80},{16,64},{64,16},{80,0},{128,208},{144,192},{192,144},{208,1... | collective-permute-start | bytes 122888 | tf_op jit(solution)/shard_map/ppermute | solution.py:238
  65.6 4.6 %collective-permute-start.11 = (bf16[5,8,512]{2,1,0:T(8,128)(2,1)S(1)}, bf16[5,8,512]{2,1,0:T(8,128)(2,1)S(1)}, u32[]{:S(2)}, u32[]{:S(2)}) collective-permute-start(bf16[5,8,512]{2,1,0:T(8,128)(2,1)S(1)} %pad_maximum_fusion.10), channel_id=1, source_target_pairs={{0,208},{16,192},{64,144},{80,128},{128,80},{144,64},{192,16},{208... | collective-permute-start | bytes 122888 | tf_op jit(solution)/shard_map/ppermute | solution.py:238
  70.3 3.5 %collective-permute-start.12 = (bf16[5,8,512]{2,1,0:T(8,128)(2,1)S(1)}, bf16[5,8,512]{2,1,0:T(8,128)(2,1)S(1)}, u32[]{:S(2)}, u32[]{:S(2)}) collective-permute-start(bf16[5,8,512]{2,1,0:T(8,128)(2,1)S(1)} %pad_maximum_fusion.11), channel_id=1, source_target_pairs={{0,17},{1,16},{16,1},{17,0},{2,19},{3,18},{18,3},{19,2},{4,21},{5,... | collective-permute-start | bytes 122888 | tf_op jit(solution)/shard_map/ppermute | solution.py:238
  73.8 5.7 %collective-permute-start.13 = (f32[5,8,512]{2,1,0:T(8,128)S(1)}, f32[5,8,512]{2,1,0:T(8,128)S(1)}, u32[]{:S(2)}, u32[]{:S(2)}) collective-permute-start(f32[5,8,512]{2,1,0:T(8,128)S(1)} %maximum_add_fusion), channel_id=1, source_target_pairs={{0,24},{8,16},{16,8},{24,0},{1,25},{9,17},{17,9},{25,1},{2,26},{10... | collective-permute-start | bytes 245768 | tf_op jit(solution)/shard_map/ppermute | solution.py:238
  79.5 6.3 %collective-permute-start.14 = (bf16[5,8,512]{2,1,0:T(8,128)(2,1)S(1)}, bf16[5,8,512]{2,1,0:T(8,128)(2,1)S(1)}, u32[]{:S(2)}, u32[]{:S(2)}) collective-permute-start(bf16[5,8,512]{2,1,0:T(8,128)(2,1)S(1)} %add_convert_fusion.1), channel_id=1, source_target_pairs={{0,18},{2,16},{4,22},{6,20},{16,2},{18,0},{20,6},{22,4},{1,19},{3,... | collective-permute-start | bytes 122888 | tf_op jit(solution)/shard_map/ppermute | solution.py:238
  80.5 7.2 %collective-permute-start.15 = (bf16[5,8,512]{2,1,0:T(8,128)(2,1)S(1)}, bf16[5,8,512]{2,1,0:T(8,128)(2,1)S(1)}, u32[]{:S(2)}, u32[]{:S(2)}) collective-permute-start(bf16[5,8,512]{2,1,0:T(8,128)(2,1)S(1)} %add_convert_fusion.1), channel_id=1, source_target_pairs={{0,4},{2,6},{4,0},{6,2},{16,20},{18,22},{20,16},{22,18},{1,5},{3,7... | collective-permute-start | bytes 122888 | tf_op jit(solution)/shard_map/ppermute | solution.py:238
  82.6 6.7 %collective-permute-start.16 = (bf16[5,8,512]{2,1,0:T(8,128)(2,1)S(1)}, bf16[5,8,512]{2,1,0:T(8,128)(2,1)S(1)}, u32[]{:S(2)}, u32[]{:S(2)}) collective-permute-start(bf16[5,8,512]{2,1,0:T(8,128)(2,1)S(1)} %add_convert_fusion.1), channel_id=1, source_target_pairs={{0,22},{2,20},{4,18},{6,16},{16,6},{18,4},{20,2},{22,0},{1,23},{3,... | collective-permute-start | bytes 122888 | tf_op jit(solution)/shard_map/ppermute | solution.py:238
  89.4 4.1 %collective-permute-start.17 = (bf16[4,8,512]{2,1,0:T(8,128)(2,1)S(1)}, bf16[4,8,512]{2,1,0:T(8,128)(2,1)S(1)}, u32[]{:S(2)}, u32[]{:S(2)}) collective-permute-start(bf16[4,8,512]{2,1,0:T(8,128)(2,1)S(1)} %slice.234), channel_id=1, source_target_pairs={{0,17},{1,16},{16,1},{17,0},{2,19},{3,18},{18,3},{19,2},{4,21},{5,... | collective-permute-start | bytes 98312 | tf_op jit(solution)/shard_map/ppermute | solution.py:238
  93.4 5.1 %collective-permute-start.19 = (bf16[2,4,8,512]{3,2,1,0:T(8,128)(2,1)S(1)}, bf16[2,4,8,512]{3,2,1,0:T(8,128)(2,1)S(1)}, u32[]{:S(2)}, u32[]{:S(2)}) collective-permute-start(bf16[2,4,8,512]{3,2,1,0:T(8,128)(2,1)S(1)} %get-tuple-element.40), channel_id=1, source_target_pairs={{0,128},{16,144},{64,192},{80,208},{128,0},{144,16},{192,64},{208,... | collective-permute-start | bytes 196616 | tf_op jit(solution)/shard_map/ppermute | solution.py:238
  94.6 6.0 %collective-permute-start.20 = (bf16[2,4,8,512]{3,2,1,0:T(8,128)(2,1)S(1)}, bf16[2,4,8,512]{3,2,1,0:T(8,128)(2,1)S(1)}, u32[]{:S(2)}, u32[]{:S(2)}) collective-permute-start(bf16[2,4,8,512]{3,2,1,0:T(8,128)(2,1)S(1)} %get-tuple-element.40), channel_id=1, source_target_pairs={{0,208},{16,192},{64,144},{80,128},{128,80},{144,64},{192,16},{208... | collective-permute-start | bytes 196616 | tf_op jit(solution)/shard_map/ppermute | solution.py:238
  95.9 4.7 %collective-permute-start.18 = (bf16[2,4,8,512]{3,2,1,0:T(8,128)(2,1)S(1)}, bf16[2,4,8,512]{3,2,1,0:T(8,128)(2,1)S(1)}, u32[]{:S(2)}, u32[]{:S(2)}) collective-permute-start(bf16[2,4,8,512]{3,2,1,0:T(8,128)(2,1)S(1)} %get-tuple-element.40), channel_id=1, source_target_pairs={{0,80},{16,64},{64,16},{80,0},{128,208},{144,192},{192,144},{208,1... | collective-permute-start | bytes 196616 | tf_op jit(solution)/shard_map/ppermute | solution.py:238
  100.6 3.1 %collective-permute-start.22 = (bf16[4,2,4,8,512]{4,3,2,1,0:T(8,128)(2,1)S(1)}, bf16[4,2,4,8,512]{4,3,2,1,0:T(8,128)(2,1)S(1)}, u32[]{:S(2)}, u32[]{:S(2)}) collective-permute-start(bf16[4,2,4,8,512]{4,3,2,1,0:T(8,128)(2,1)S(1)} %pad_maximum_fusion.1.piece_ref), channel_id=1, source_target_pairs={{0,16},{16,0},{1,17},{17,1},{2,18},{18,2},{3,19},{19,3},{4,20},{20... | collective-permute-start | bytes 786440 | tf_op jit(solution)/shard_map/ppermute | solution.py:238
  101.1 6.2 %collective-permute-start.23 = (bf16[2,2,4,8,512]{4,3,2,1,0:T(8,128)(2,1)S(1)}, bf16[2,2,4,8,512]{4,3,2,1,0:T(8,128)(2,1)S(1)}, u32[]{:S(2)}, u32[]{:S(2)}) collective-permute-start(bf16[2,2,4,8,512]{4,3,2,1,0:T(8,128)(2,1)S(1)} %pad_maximum_fusion.6), channel_id=1, source_target_pairs={{0,40},{8,32},{32,8},{40,0},{1,41},{9,33},{33,9},{41,1},{2,42},{10... | collective-permute-start | bytes 393224 | tf_op jit(solution)/shard_map/ppermute | solution.py:238
  101.4 5.9 %collective-permute-start.21 = (bf16[2,2,4,8,512]{4,3,2,1,0:T(8,128)(2,1)S(1)}, bf16[2,2,4,8,512]{4,3,2,1,0:T(8,128)(2,1)S(1)}, u32[]{:S(2)}, u32[]{:S(2)}) collective-permute-start(bf16[2,2,4,8,512]{4,3,2,1,0:T(8,128)(2,1)S(1)} %pad_maximum_fusion.5), channel_id=1, source_target_pairs={{0,48},{16,32},{32,16},{48,0},{1,49},{17,33},{33,17},{49,1},{2,50}... | collective-permute-start | bytes 393224 | tf_op jit(solution)/shard_map/ppermute | solution.py:238
  107.4 2.6 %collective-permute-start.24 = (bf16[4,2,4,8,512]{4,3,2,1,0:T(8,128)(2,1)S(1)}, bf16[4,2,4,8,512]{4,3,2,1,0:T(8,128)(2,1)S(1)}, u32[]{:S(2)}, u32[]{:S(2)}) collective-permute-start(bf16[4,2,4,8,512]{4,3,2,1,0:T(8,128)(2,1)S(1)} %pad_maximum_fusion.2.piece_ref), channel_id=1, source_target_pairs={{0,16},{16,0},{1,17},{17,1},{2,18},{18,2},{3,19},{19,3},{4,20},{20... | collective-permute-start | bytes 786440 | tf_op jit(solution)/shard_map/ppermute | solution.py:238
  (3 other events, 17.7 us)

commit v5 on v4

--- a/solution.py
+++ b/solution.py
@@ -326,8 +326,11 @@
     high = jnp.stack([high_zero, high[1] + two[5].astype(F32)])
 
     sent = jnp.concatenate([sums[2:4], jnp.where(zb == 0, high, low), loss[None]]).astype(BF16)
-    rows = jnp.concatenate([sums[0:2], jnp.where(zb == 0, low, high), loss[None]]) + across_z(sent).astype(F32)
-    own = (rows + swap(rows, ("c", "xh"), 4, 3)).astype(BF16)
+    own = jnp.concatenate([sums[0:2], jnp.where(zb == 0, low, high), loss[None]]).astype(BF16)
+    a = swap(own, ("c", "xh"), 4, 3).astype(F32)
+    b = swap(sent, ("xh", "zb"), 4, 3).astype(F32)
+    d = across_z(sent).astype(F32)
+    own = ((own.astype(F32) + d) + (a + b)).astype(BF16)
     a, b, d = (swap(own, ("c", "za"), 8, k + 4 * (k & 1)).astype(F32) for k in (1, 2, 3))
     rows = (own.astype(F32) + a) + (b + d)
     loss = rows[4]

time: 112 us -> 111 us (level)
  waiting for transfers between devices: 51.5 us -> 46.2 us
  starting transfers between devices: 40.2 us -> 44.7 us
    ppermute x25 -> x26, waiting for transfers between devices: 43.4 us -> 38.1 us  [swap(): return lax.ppermute(array, axis, [(j, j ^ bit) for j in range(size)])]
    ppermute x25 -> x26, starting transfers between devices: 28.6 us -> 33.1 us  [swap(): return lax.ppermute(array, axis, [(j, j ^ bit) for j in range(size)])]
  transfers between devices with their start and end apart: 26 -> 27, of which waited for: 19 -> 20; matrix products, arithmetic and copies ran while one was open for 0% -> 0% of each run, Pallas kernels for 5% -> 5%
where the time goes in v5:
time: 111 us
  waiting for transfers between devices  46.2 us (42%)
  starting transfers between devices  44.7 us (40%)
  Pallas kernels  17.5 us (16%)
    ppermute x26, waiting for transfers between devices, swap(): return lax.ppermute(array, axis, [(j, j ^ bit) for j in range(size)])  38.1 us
    ppermute x26, starting transfers between devices, swap(): return lax.ppermute(array, axis, [(j, j ^ bit) for j in range(size)])  33.1 us
    all_to_all x1, starting transfers between devices, on_device(): lax.all_to_all(jnp.broadcast_to(packed[None], (16, 24, 128)), FEAT, 0, 0,...  11.6 us
    all_to_all x1, waiting for transfers between devices, on_device(): lax.all_to_all(jnp.broadcast_to(packed[None], (16, 24, 128)), FEAT, 0, 0,...  8.09 us
    pallas_call x1, Pallas kernels, on_device(): call(cross_kernel, [SMEM, VMEM, VMEM, VMEM], [((2, 288, 128), F32, VMEM),...  4.04 us
    pallas_call x1, Pallas kernels, on_device(): call(grad_kernel, [SMEM] + [VMEM] * 5, [((36, 8, DS), F32, VMEM), ((36, 8...  3.91 us
    pallas_call x2, Pallas kernels, on_device(): call(next_kernel(c, 1), [SMEM, VMEM, ANY], [out], rows_and_sems, {2: 0})  3.03 us
  transfers between devices with their start and end apart: 27, of which 20 were waited for; matrix products, arithmetic and copies ran while one was open for 0% of the time, Pallas kernels for 5%

profile of v5, /device:TPU:1, one launch (start us, length us, event | category | flops | bytes accessed | tf_op | source)
XLA Modules:
  0.0 110.9 jit_solution(2615306391786438364)
XLA Ops:
  0.6 2.2 %shard_map.50 = (bf16[2048,256]{1,0:T(8,128)(2,1)S(1)}, bf16[24,128]{1,0:T(8,128)(2,1)S(1)}) custom-call(bf16[2048,256]{1,0:T(8,128)(2,1)} %teacher_hbm.1, s32[4,128]{1,0:T(4,128)} %bitcast.44), custom_call_target="tpu_custom_call" | custom-call | tf_op jit(solution)/shard_map/pallas_call | solution.py:265
  3.5 11.6 %all-to-all-start = ((bf16[16,24,128]{2,1,0:T(8,128)(2,1)}), bf16[16,24,128]{2,1,0:T(8,128)(2,1)S(1)}, u32[]{:S(2)}, u32[]{:S(2)}) async-start(bf16[16,24,128]{2,1,0:T(8,128)(2,1)} %broadcast_in_dim.26), calls=%async_computation | async-start | bytes 196608 | tf_op jit(solution)/shard_map/all_to_all | solution.py:271
  16.0 8.1 %all-to-all-done.packed_ref = bf16[16,24,128]{2,1,0:T(8,128)(2,1)S(1)} async-done(((bf16[16,24,128]{2,1,0:T(8,128)(2,1)}), bf16[16,24,128]{2,1,0:T(8,128)(2,1)S(1)}, u32[]{:S(2)}, u32[]{:S(2)}) %all-to-all-start) | async-done | bytes 98336 | tf_op jit(solution)/shard_map/all_to_all | solution.py:271
  24.1 4.0 %shard_map.52 = (f32[2,288,128]{2,1,0:T(8,128)S(1)}, bf16[2,288,128]{2,1,0:T(8,128)(2,1)S(1)}, bf16[512,2048]{1,0:T(8,128)(2,1)S(1)}, bf16[2048,256]{1,0:T(8,128)(2,1)S(1)}, f32[1,2048]{1,0:T(1,128)S(1)}) custom-call(s32[7]{0:T(128)S(1)} %stack.78.where_ref, bf16[16,24,128]{2,1,0:T(8,128)(2,1)S(1)} %all-to-all-done.packed_ref, ...), custom_call_target="tpu_custom_call" | custom-call | tf_op jit(solution)/shard_map/pallas_call | solution.py:274
  28.1 2.1 %collective-permute-start = (bf16[2,288,128]{2,1,0:T(8,128)(2,1)S(1)}, bf16[2,288,128]{2,1,0:T(8,128)(2,1)S(1)}, u32[]{:S(2)}, u32[]{:S(2)}) collective-permute-start(bf16[2,288,128]{2,1,0:T(8,128)(2,1)S(1)} %get-tuple-element.19), channel_id=1, source_target_pairs={{0,16},{16,0},{1,17},{17,1},{2,18},{18,2},{3,19},{19,3},{4,20},{20... | collective-permute-start | bytes 442376 | tf_op jit(solution)/shard_map/ppermute | solution.py:238
  31.9 3.7 %collective-permute-done.1 = bf16[288,128]{1,0:T(8,128)(2,1)S(1)} collective-permute-done((bf16[288,128]{1,0:T(8,128)(2,1)S(1)}, bf16[288,128]{1,0:T(8,128)(2,1)S(1)}, u32[]{:S(2)}, u32[]{:S(2)}) %collective-permute-start.1) | collective-permute-done | bytes 73760 | tf_op jit(solution)/shard_map/ppermute | solution.py:238
  35.6 1.6 %collective-permute-start.2 = (bf16[288,128]{1,0:T(8,128)(2,1)S(1)}, bf16[288,128]{1,0:T(8,128)(2,1)S(1)}, u32[]{:S(2)}, u32[]{:S(2)}) collective-permute-start(bf16[288,128]{1,0:T(8,128)(2,1)S(1)} %fusion.1), channel_id=1, source_target_pairs={{0,80},{16,64},{64,16},{80,0},{128,208},{144,192},{192,144},{208,1... | collective-permute-start | bytes 221192 | tf_op jit(solution)/shard_map/ppermute | solution.py:238
  37.3 2.6 %collective-permute-start.3 = (bf16[288,128]{1,0:T(8,128)(2,1)S(1)}, bf16[288,128]{1,0:T(8,128)(2,1)S(1)}, u32[]{:S(2)}, u32[]{:S(2)}) collective-permute-start(bf16[288,128]{1,0:T(8,128)(2,1)S(1)} %fusion.1), channel_id=1, source_target_pairs={{0,128},{16,144},{64,192},{80,208},{128,0},{144,16},{192,64},{208,... | collective-permute-start | bytes 221192 | tf_op jit(solution)/shard_map/ppermute | solution.py:238
  40.1 3.8 %collective-permute-done.3 = bf16[288,128]{1,0:T(8,128)(2,1)S(1)} collective-permute-done((bf16[288,128]{1,0:T(8,128)(2,1)S(1)}, bf16[288,128]{1,0:T(8,128)(2,1)S(1)}, u32[]{:S(2)}, u32[]{:S(2)}) %collective-permute-start.3) | collective-permute-done | bytes 73760 | tf_op jit(solution)/shard_map/ppermute | solution.py:238
  44.0 1.8 %collective-permute-done.4 = bf16[288,128]{1,0:T(8,128)(2,1)S(1)} collective-permute-done((bf16[288,128]{1,0:T(8,128)(2,1)S(1)}, bf16[288,128]{1,0:T(8,128)(2,1)S(1)}, u32[]{:S(2)}, u32[]{:S(2)}) %collective-permute-start.4) | collective-permute-done | bytes 73760 | tf_op jit(solution)/shard_map/ppermute | solution.py:238
  46.5 3.7 %collective-permute-done.5 = bf16[288,128]{1,0:T(8,128)(2,1)S(1)} collective-permute-done((bf16[288,128]{1,0:T(8,128)(2,1)S(1)}, bf16[288,128]{1,0:T(8,128)(2,1)S(1)}, u32[]{:S(2)}, u32[]{:S(2)}) %collective-permute-start.5) | collective-permute-done | bytes 73760 | tf_op jit(solution)/shard_map/ppermute | solution.py:238
  51.7 3.9 %shard_map.53 = (f32[36,8,512]{2,1,0:T(8,128)S(1)}, bf16[36,8,512]{2,1,0:T(8,128)(2,1)S(1)}, f32[8,512]{1,0:T(8,128)S(1)}) custom-call(s32[7]{0:T(128)S(1)} %stack.78.where_ref, bf16[16,24,128]{2,1,0:T(8,128)(2,1)S(1)} %all-to-all-done.packed_ref, bf16[4,288,128]{2,1,0:T(8,128)(2,1)S(1)} %pad_maximum_fusion.whole_ref, ...), custom_call_target="tpu_custom_call" | custom-call | tf_op jit(solution)/shard_map/pallas_call | solution.py:295
  58.4 5.1 %collective-permute-done.8 = bf16[17,8,512]{2,1,0:T(8,128)(2,1)S(1)} collective-permute-done((bf16[17,8,512]{2,1,0:T(8,128)(2,1)S(1)}, bf16[17,8,512]{2,1,0:T(8,128)(2,1)S(1)}, u32[]{:S(2)}, u32[]{:S(2)}) %collective-permute-start.8) | collective-permute-done | bytes 139296 | tf_op jit(solution)/shard_map/ppermute | solution.py:238
  65.6 1.7 %collective-permute-start.11 = (bf16[5,8,512]{2,1,0:T(8,128)(2,1)S(1)}, bf16[5,8,512]{2,1,0:T(8,128)(2,1)S(1)}, u32[]{:S(2)}, u32[]{:S(2)}) collective-permute-start(bf16[5,8,512]{2,1,0:T(8,128)(2,1)S(1)} %pad_maximum_fusion.12), channel_id=1, source_target_pairs={{0,208},{16,192},{64,144},{80,128},{128,80},{144,64},{192,16},{208... | collective-permute-start | bytes 122888 | tf_op jit(solution)/shard_map/ppermute | solution.py:238
  68.2 2.0 %collective-permute-done.11 = bf16[5,8,512]{2,1,0:T(8,128)(2,1)S(1)} collective-permute-done((bf16[5,8,512]{2,1,0:T(8,128)(2,1)S(1)}, bf16[5,8,512]{2,1,0:T(8,128)(2,1)S(1)}, u32[]{:S(2)}, u32[]{:S(2)}) %collective-permute-start.11) | collective-permute-done | bytes 40992 | tf_op jit(solution)/shard_map/ppermute | solution.py:238
  72.1 2.7 %collective-permute-start.14 = (bf16[5,8,512]{2,1,0:T(8,128)(2,1)S(1)}, bf16[5,8,512]{2,1,0:T(8,128)(2,1)S(1)}, u32[]{:S(2)}, u32[]{:S(2)}) collective-permute-start(bf16[5,8,512]{2,1,0:T(8,128)(2,1)S(1)} %get-tuple-element.54), channel_id=1, source_target_pairs={{0,9},{1,8},{8,1},{9,0},{2,11},{3,10},{10,3},{11,2},{4,13},{5,12},... | collective-permute-start | bytes 122888 | tf_op jit(solution)/shard_map/ppermute | solution.py:238
  78.9 2.9 %collective-permute-start.16 = (bf16[5,8,512]{2,1,0:T(8,128)(2,1)S(1)}, bf16[5,8,512]{2,1,0:T(8,128)(2,1)S(1)}, u32[]{:S(2)}, u32[]{:S(2)}) collective-permute-start(bf16[5,8,512]{2,1,0:T(8,128)(2,1)S(1)} %add_convert_fusion.1), channel_id=1, source_target_pairs={{0,4},{2,6},{4,0},{6,2},{16,20},{18,22},{20,16},{22,18},{1,5},{3,7... | collective-permute-start | bytes 122888 | tf_op jit(solution)/shard_map/ppermute | solution.py:238
  81.8 1.8 %collective-permute-start.17 = (bf16[5,8,512]{2,1,0:T(8,128)(2,1)S(1)}, bf16[5,8,512]{2,1,0:T(8,128)(2,1)S(1)}, u32[]{:S(2)}, u32[]{:S(2)}) collective-permute-start(bf16[5,8,512]{2,1,0:T(8,128)(2,1)S(1)} %add_convert_fusion.1), channel_id=1, source_target_pairs={{0,22},{2,20},{4,18},{6,16},{16,6},{18,4},{20,2},{22,0},{1,23},{3,... | collective-permute-start | bytes 122888 | tf_op jit(solution)/shard_map/ppermute | solution.py:238
  83.7 2.5 %collective-permute-done.16 = bf16[5,8,512]{2,1,0:T(8,128)(2,1)S(1)} collective-permute-done((bf16[5,8,512]{2,1,0:T(8,128)(2,1)S(1)}, bf16[5,8,512]{2,1,0:T(8,128)(2,1)S(1)}, u32[]{:S(2)}, u32[]{:S(2)}) %collective-permute-start.16) | collective-permute-done | bytes 40992 | tf_op jit(solution)/shard_map/ppermute | solution.py:238
  87.7 2.5 %collective-permute-start.18 = (bf16[4,8,512]{2,1,0:T(8,128)(2,1)S(1)}, bf16[4,8,512]{2,1,0:T(8,128)(2,1)S(1)}, u32[]{:S(2)}, u32[]{:S(2)}) collective-permute-start(bf16[4,8,512]{2,1,0:T(8,128)(2,1)S(1)} %slice.236), channel_id=1, source_target_pairs={{0,17},{1,16},{16,1},{17,0},{2,19},{3,18},{18,3},{19,2},{4,21},{5,... | collective-permute-start | bytes 98312 | tf_op jit(solution)/shard_map/ppermute | solution.py:238
  94.9 2.1 %collective-permute-done.20 = bf16[2,4,8,512]{3,2,1,0:T(8,128)(2,1)S(1)} collective-permute-done((bf16[2,4,8,512]{3,2,1,0:T(8,128)(2,1)S(1)}, bf16[2,4,8,512]{3,2,1,0:T(8,128)(2,1)S(1)}, u32[]{:S(2)}, u32[]{:S(2)}) %collective-permute-start.20) | collective-permute-done | bytes 65568 | tf_op jit(solution)/shard_map/ppermute | solution.py:238
  97.0 2.0 %collective-permute-done.21 = bf16[2,4,8,512]{3,2,1,0:T(8,128)(2,1)S(1)} collective-permute-done((bf16[2,4,8,512]{3,2,1,0:T(8,128)(2,1)S(1)}, bf16[2,4,8,512]{3,2,1,0:T(8,128)(2,1)S(1)}, u32[]{:S(2)}, u32[]{:S(2)}) %collective-permute-start.21) | collective-permute-done | bytes 65568 | tf_op jit(solution)/shard_map/ppermute | solution.py:238
  99.5 2.2 %collective-permute-start.24 = (bf16[2,2,4,8,512]{4,3,2,1,0:T(8,128)(2,1)S(1)}, bf16[2,2,4,8,512]{4,3,2,1,0:T(8,128)(2,1)S(1)}, u32[]{:S(2)}, u32[]{:S(2)}) collective-permute-start(bf16[2,2,4,8,512]{4,3,2,1,0:T(8,128)(2,1)S(1)} %pad_maximum_fusion.6), channel_id=1, source_target_pairs={{0,40},{8,32},{32,8},{40,0},{1,41},{9,33},{33,9},{41,1},{2,42},{10... | collective-permute-start | bytes 393224 | tf_op jit(solution)/shard_map/ppermute | solution.py:238
  101.9 2.0 %shard_map.54 = (f32[4,256,512]{2,1,0:T(8,128)}, f32[1,1]{1,0:T(1,128)}) custom-call(s32[7]{0:T(128)S(1)} %stack.78.where_ref, bf16[4,2,4,8,512]{4,3,2,1,0:T(8,128)(2,1)S(1)} %pad_maximum_fusion.1.piece_ref, f32[8,512]{1,0:T(8,128)S(1)} %slice_bitcast_fusion.1.parts_ref), custom_call_target="tpu_custom_call" | custom-call | tf_op jit(solution)/shard_map/pallas_call | solution.py:346
  (77 shorter events, 31.3 us)
Async XLA Ops:
  3.5 20.6 %all-to-all-start = ((bf16[16,24,128]{2,1,0:T(8,128)(2,1)}), bf16[16,24,128]{2,1,0:T(8,128)(2,1)S(1)}, u32[]{:S(2)}, u32[]{:S(2)}) async-start(bf16[16,24,128]{2,1,0:T(8,128)(2,1)} %broadcast_in_dim.26), calls=%async_computation | async-start | bytes 196608 | tf_op jit(solution)/shard_map/all_to_all | solution.py:271
  28.1 3.1 %collective-permute-start = (bf16[2,288,128]{2,1,0:T(8,128)(2,1)S(1)}, bf16[2,288,128]{2,1,0:T(8,128)(2,1)S(1)}, u32[]{:S(2)}, u32[]{:S(2)}) collective-permute-start(bf16[2,288,128]{2,1,0:T(8,128)(2,1)S(1)} %get-tuple-element.19), channel_id=1, source_target_pairs={{0,16},{16,0},{1,17},{17,1},{2,18},{18,2},{3,19},{19,3},{4,20},{20... | collective-permute-start | bytes 442376 | tf_op jit(solution)/shard_map/ppermute | solution.py:238
  31.3 4.3 %collective-permute-start.1 = (bf16[288,128]{1,0:T(8,128)(2,1)S(1)}, bf16[288,128]{1,0:T(8,128)(2,1)S(1)}, u32[]{:S(2)}, u32[]{:S(2)}) collective-permute-start(bf16[288,128]{1,0:T(8,128)(2,1)S(1)} %fusion.2), channel_id=1, source_target_pairs={{0,48},{16,32},{32,16},{48,0},{1,49},{17,33},{33,17},{49,1},{2,50}... | collective-permute-start | bytes 221192 | tf_op jit(solution)/shard_map/ppermute | solution.py:238
  35.6 4.5 %collective-permute-start.2 = (bf16[288,128]{1,0:T(8,128)(2,1)S(1)}, bf16[288,128]{1,0:T(8,128)(2,1)S(1)}, u32[]{:S(2)}, u32[]{:S(2)}) collective-permute-start(bf16[288,128]{1,0:T(8,128)(2,1)S(1)} %fusion.1), channel_id=1, source_target_pairs={{0,80},{16,64},{64,16},{80,0},{128,208},{144,192},{192,144},{208,1... | collective-permute-start | bytes 221192 | tf_op jit(solution)/shard_map/ppermute | solution.py:238
  37.3 6.7 %collective-permute-start.3 = (bf16[288,128]{1,0:T(8,128)(2,1)S(1)}, bf16[288,128]{1,0:T(8,128)(2,1)S(1)}, u32[]{:S(2)}, u32[]{:S(2)}) collective-permute-start(bf16[288,128]{1,0:T(8,128)(2,1)S(1)} %fusion.1), channel_id=1, source_target_pairs={{0,128},{16,144},{64,192},{80,208},{128,0},{144,16},{192,64},{208,... | collective-permute-start | bytes 221192 | tf_op jit(solution)/shard_map/ppermute | solution.py:238
  39.9 5.9 %collective-permute-start.4 = (bf16[288,128]{1,0:T(8,128)(2,1)S(1)}, bf16[288,128]{1,0:T(8,128)(2,1)S(1)}, u32[]{:S(2)}, u32[]{:S(2)}) collective-permute-start(bf16[288,128]{1,0:T(8,128)(2,1)S(1)} %fusion.1), channel_id=1, source_target_pairs={{0,208},{16,192},{64,144},{80,128},{128,80},{144,64},{192,16},{208... | collective-permute-start | bytes 221192 | tf_op jit(solution)/shard_map/ppermute | solution.py:238
  45.8 4.4 %collective-permute-start.5 = (bf16[288,128]{1,0:T(8,128)(2,1)S(1)}, bf16[288,128]{1,0:T(8,128)(2,1)S(1)}, u32[]{:S(2)}, u32[]{:S(2)}) collective-permute-start(bf16[288,128]{1,0:T(8,128)(2,1)S(1)} %add_convert_fusion), channel_id=1, source_target_pairs={{0,48},{16,32},{32,16},{48,0},{1,49},{17,33},{33,17},{49,1},{2,50}... | collective-permute-start | bytes 221192 | tf_op jit(solution)/shard_map/ppermute | solution.py:238
  57.5 5.9 %collective-permute-start.8 = (bf16[17,8,512]{2,1,0:T(8,128)(2,1)S(1)}, bf16[17,8,512]{2,1,0:T(8,128)(2,1)S(1)}, u32[]{:S(2)}, u32[]{:S(2)}) collective-permute-start(bf16[17,8,512]{2,1,0:T(8,128)(2,1)S(1)} %pad_maximum_fusion.4), channel_id=1, source_target_pairs={{0,48},{16,32},{32,16},{48,0},{1,49},{17,33},{33,17},{49,1},{2,50}... | collective-permute-start | bytes 417800 | tf_op jit(solution)/shard_map/ppermute | solution.py:238
  63.5 6.7 %collective-permute-start.10 = (bf16[6,8,512]{2,1,0:T(8,128)(2,1)S(1)}, bf16[6,8,512]{2,1,0:T(8,128)(2,1)S(1)}, u32[]{:S(2)}, u32[]{:S(2)}) collective-permute-start(bf16[6,8,512]{2,1,0:T(8,128)(2,1)S(1)} %pad_maximum_fusion.10), channel_id=1, source_target_pairs={{0,128},{16,144},{64,192},{80,208},{128,0},{144,16},{192,64},{208,... | collective-permute-start | bytes 147464 | tf_op jit(solution)/shard_map/ppermute | solution.py:238
  64.0 4.2 %collective-permute-start.9 = (bf16[5,8,512]{2,1,0:T(8,128)(2,1)S(1)}, bf16[5,8,512]{2,1,0:T(8,128)(2,1)S(1)}, u32[]{:S(2)}, u32[]{:S(2)}) collective-permute-start(bf16[5,8,512]{2,1,0:T(8,128)(2,1)S(1)} %pad_maximum_fusion.11), channel_id=1, source_target_pairs={{0,80},{16,64},{64,16},{80,0},{128,208},{144,192},{192,144},{208,1... | collective-permute-start | bytes 122888 | tf_op jit(solution)/shard_map/ppermute | solution.py:238
  65.6 4.6 %collective-permute-start.11 = (bf16[5,8,512]{2,1,0:T(8,128)(2,1)S(1)}, bf16[5,8,512]{2,1,0:T(8,128)(2,1)S(1)}, u32[]{:S(2)}, u32[]{:S(2)}) collective-permute-start(bf16[5,8,512]{2,1,0:T(8,128)(2,1)S(1)} %pad_maximum_fusion.12), channel_id=1, source_target_pairs={{0,208},{16,192},{64,144},{80,128},{128,80},{144,64},{192,16},{208... | collective-permute-start | bytes 122888 | tf_op jit(solution)/shard_map/ppermute | solution.py:238
  70.3 4.5 %collective-permute-start.12 = (bf16[5,8,512]{2,1,0:T(8,128)(2,1)S(1)}, bf16[5,8,512]{2,1,0:T(8,128)(2,1)S(1)}, u32[]{:S(2)}, u32[]{:S(2)}) collective-permute-start(bf16[5,8,512]{2,1,0:T(8,128)(2,1)S(1)} %get-tuple-element.54), channel_id=1, source_target_pairs={{0,17},{1,16},{16,1},{17,0},{2,19},{3,18},{18,3},{19,2},{4,21},{5,... | collective-permute-start | bytes 122888 | tf_op jit(solution)/shard_map/ppermute | solution.py:238
  71.1 5.3 %collective-permute-start.13 = (bf16[5,8,512]{2,1,0:T(8,128)(2,1)S(1)}, bf16[5,8,512]{2,1,0:T(8,128)(2,1)S(1)}, u32[]{:S(2)}, u32[]{:S(2)}) collective-permute-start(bf16[5,8,512]{2,1,0:T(8,128)(2,1)S(1)} %get-tuple-element.53), channel_id=1, source_target_pairs={{0,24},{8,16},{16,8},{24,0},{1,25},{9,17},{17,9},{25,1},{2,26},{10... | collective-permute-start | bytes 122888 | tf_op jit(solution)/shard_map/ppermute | solution.py:238
  72.1 5.3 %collective-permute-start.14 = (bf16[5,8,512]{2,1,0:T(8,128)(2,1)S(1)}, bf16[5,8,512]{2,1,0:T(8,128)(2,1)S(1)}, u32[]{:S(2)}, u32[]{:S(2)}) collective-permute-start(bf16[5,8,512]{2,1,0:T(8,128)(2,1)S(1)} %get-tuple-element.54), channel_id=1, source_target_pairs={{0,9},{1,8},{8,1},{9,0},{2,11},{3,10},{10,3},{11,2},{4,13},{5,12},... | collective-permute-start | bytes 122888 | tf_op jit(solution)/shard_map/ppermute | solution.py:238
  77.4 6.3 %collective-permute-start.15 = (bf16[5,8,512]{2,1,0:T(8,128)(2,1)S(1)}, bf16[5,8,512]{2,1,0:T(8,128)(2,1)S(1)}, u32[]{:S(2)}, u32[]{:S(2)}) collective-permute-start(bf16[5,8,512]{2,1,0:T(8,128)(2,1)S(1)} %add_convert_fusion.1), channel_id=1, source_target_pairs={{0,18},{2,16},{4,22},{6,20},{16,2},{18,0},{20,6},{22,4},{1,19},{3,... | collective-permute-start | bytes 122888 | tf_op jit(solution)/shard_map/ppermute | solution.py:238
  78.9 7.2 %collective-permute-start.16 = (bf16[5,8,512]{2,1,0:T(8,128)(2,1)S(1)}, bf16[5,8,512]{2,1,0:T(8,128)(2,1)S(1)}, u32[]{:S(2)}, u32[]{:S(2)}) collective-permute-start(bf16[5,8,512]{2,1,0:T(8,128)(2,1)S(1)} %add_convert_fusion.1), channel_id=1, source_target_pairs={{0,4},{2,6},{4,0},{6,2},{16,20},{18,22},{20,16},{22,18},{1,5},{3,7... | collective-permute-start | bytes 122888 | tf_op jit(solution)/shard_map/ppermute | solution.py:238
  81.8 5.8 %collective-permute-start.17 = (bf16[5,8,512]{2,1,0:T(8,128)(2,1)S(1)}, bf16[5,8,512]{2,1,0:T(8,128)(2,1)S(1)}, u32[]{:S(2)}, u32[]{:S(2)}) collective-permute-start(bf16[5,8,512]{2,1,0:T(8,128)(2,1)S(1)} %add_convert_fusion.1), channel_id=1, source_target_pairs={{0,22},{2,20},{4,18},{6,16},{16,6},{18,4},{20,2},{22,0},{1,23},{3,... | collective-permute-start | bytes 122888 | tf_op jit(solution)/shard_map/ppermute | solution.py:238
  87.7 4.1 %collective-permute-start.18 = (bf16[4,8,512]{2,1,0:T(8,128)(2,1)S(1)}, bf16[4,8,512]{2,1,0:T(8,128)(2,1)S(1)}, u32[]{:S(2)}, u32[]{:S(2)}) collective-permute-start(bf16[4,8,512]{2,1,0:T(8,128)(2,1)S(1)} %slice.236), channel_id=1, source_target_pairs={{0,17},{1,16},{16,1},{17,0},{2,19},{3,18},{18,3},{19,2},{4,21},{5,... | collective-permute-start | bytes 98312 | tf_op jit(solution)/shard_map/ppermute | solution.py:238
  91.8 5.1 %collective-permute-start.20 = (bf16[2,4,8,512]{3,2,1,0:T(8,128)(2,1)S(1)}, bf16[2,4,8,512]{3,2,1,0:T(8,128)(2,1)S(1)}, u32[]{:S(2)}, u32[]{:S(2)}) collective-permute-start(bf16[2,4,8,512]{3,2,1,0:T(8,128)(2,1)S(1)} %get-tuple-element.40), channel_id=1, source_target_pairs={{0,128},{16,144},{64,192},{80,208},{128,0},{144,16},{192,64},{208,... | collective-permute-start | bytes 196616 | tf_op jit(solution)/shard_map/ppermute | solution.py:238
  92.7 6.2 %collective-permute-start.21 = (bf16[2,4,8,512]{3,2,1,0:T(8,128)(2,1)S(1)}, bf16[2,4,8,512]{3,2,1,0:T(8,128)(2,1)S(1)}, u32[]{:S(2)}, u32[]{:S(2)}) collective-permute-start(bf16[2,4,8,512]{3,2,1,0:T(8,128)(2,1)S(1)} %get-tuple-element.40), channel_id=1, source_target_pairs={{0,208},{16,192},{64,144},{80,128},{128,80},{144,64},{192,16},{208... | collective-permute-start | bytes 196616 | tf_op jit(solution)/shard_map/ppermute | solution.py:238
  94.1 4.8 %collective-permute-start.19 = (bf16[2,4,8,512]{3,2,1,0:T(8,128)(2,1)S(1)}, bf16[2,4,8,512]{3,2,1,0:T(8,128)(2,1)S(1)}, u32[]{:S(2)}, u32[]{:S(2)}) collective-permute-start(bf16[2,4,8,512]{3,2,1,0:T(8,128)(2,1)S(1)} %get-tuple-element.40), channel_id=1, source_target_pairs={{0,80},{16,64},{64,16},{80,0},{128,208},{144,192},{192,144},{208,1... | collective-permute-start | bytes 196616 | tf_op jit(solution)/shard_map/ppermute | solution.py:238
  99.0 4.9 %collective-permute-start.23 = (bf16[4,2,4,8,512]{4,3,2,1,0:T(8,128)(2,1)S(1)}, bf16[4,2,4,8,512]{4,3,2,1,0:T(8,128)(2,1)S(1)}, u32[]{:S(2)}, u32[]{:S(2)}) collective-permute-start(bf16[4,2,4,8,512]{4,3,2,1,0:T(8,128)(2,1)S(1)} %pad_maximum_fusion.1.piece_ref), channel_id=1, source_target_pairs={{0,16},{16,0},{1,17},{17,1},{2,18},{18,2},{3,19},{19,3},{4,20},{20... | collective-permute-start | bytes 786440 | tf_op jit(solution)/shard_map/ppermute | solution.py:238
  99.5 6.2 %collective-permute-start.24 = (bf16[2,2,4,8,512]{4,3,2,1,0:T(8,128)(2,1)S(1)}, bf16[2,2,4,8,512]{4,3,2,1,0:T(8,128)(2,1)S(1)}, u32[]{:S(2)}, u32[]{:S(2)}) collective-permute-start(bf16[2,2,4,8,512]{4,3,2,1,0:T(8,128)(2,1)S(1)} %pad_maximum_fusion.6), channel_id=1, source_target_pairs={{0,40},{8,32},{32,8},{40,0},{1,41},{9,33},{33,9},{41,1},{2,42},{10... | collective-permute-start | bytes 393224 | tf_op jit(solution)/shard_map/ppermute | solution.py:238
  101.6 5.5 %collective-permute-start.22 = (bf16[2,2,4,8,512]{4,3,2,1,0:T(8,128)(2,1)S(1)}, bf16[2,2,4,8,512]{4,3,2,1,0:T(8,128)(2,1)S(1)}, u32[]{:S(2)}, u32[]{:S(2)}) collective-permute-start(bf16[2,2,4,8,512]{4,3,2,1,0:T(8,128)(2,1)S(1)} %pad_maximum_fusion.5), channel_id=1, source_target_pairs={{0,48},{16,32},{32,16},{48,0},{1,49},{17,33},{33,17},{49,1},{2,50}... | collective-permute-start | bytes 393224 | tf_op jit(solution)/shard_map/ppermute | solution.py:238
  (4 other events, 19.7 us)
